TPU v7x, 32 devices: a whole 2x2x4 slice. The times are simulated.
32 devices in a mesh: path: 4 (over y, x), head: 2 (over core), expert: 4 (over z).
Axes of the slice: x: 2, y: 2, z: 4, core: 2. Of those that a mesh axis runs over, the one named last changes fastest.
Arguments:
- tokens: bfloat16 [4096, 2048], P(('path', 'expert'), 'head'), may hold values from -6 to 6
- routes: int32 [4096, 2], P(('path', 'expert')), may hold values from 0 to 15, all different within a row; in each aligned block of 256 rows (0 to 255, 256 to 511, ...) at most 64 rows name the same one
- combine_weights: float32 [4096, 2], P(('path', 'expert')), may hold values from 0.1 to 0.9
- w_gate: bfloat16 [16, 2048, 768], P(('path', 'expert'), None, 'head'), may hold values from -0.125 to 0.125
- w_up: bfloat16 [16, 2048, 768], P(('path', 'expert'), None, 'head'), may hold values from -0.125 to 0.125
- w_down: bfloat16 [16, 768, 2048], P(('path', 'expert'), 'head'), may hold values from -0.21875 to 0.21875
- cotangent: bfloat16 [4096, 2048], P(('path', 'expert'), 'head'), may hold values from -1.5 to 1.5
Outputs:
- layer_out: bfloat16 [4096, 2048], P(('path', 'expert'), 'head')
- d_tokens: bfloat16 [4096, 2048], P(('path', 'expert'), 'head')
- d_gates: float32 [4096, 2], P(('path', 'expert'))
- grad_gate: bfloat16 [16, 2048, 768], P(('path', 'expert'), None, 'head')
- grad_up: bfloat16 [16, 2048, 768], P(('path', 'expert'), None, 'head')
- grad_down: bfloat16 [16, 768, 2048], P(('path', 'expert'), 'head')
Inputs may be any that keep to these rules, and one draw needn't show every extreme that they name: `routes`: each row names 2 different experts. Within the 256 rows of one device (aligned blocks) no expert is named more than 64 times, and in every draw some expert is named exactly 64 times within some block.
All inputs are finite; a program needn't handle non-finite values.
Results may differ from a plain program's by a relative error of at most 0.0072.
Values may be sent and summed in bfloat16 or wider, within the bound.
No kernel may reach another device: no remote copies, remote signals or barrier semaphores. Data moves between devices by JAX's collectives and lax.ppermute only.
A program may use at most 128 MiB of HBM per device.

v0:
```python
import functools

import jax
import jax.numpy as jnp
from jax import lax
from jax.experimental import pallas as pl
from jax.experimental.pallas import tpu as pltpu
from jax.sharding import PartitionSpec as P

BF = jnp.bfloat16
F32 = jnp.float32
VMEM = pl.BlockSpec(memory_space=pltpu.VMEM)
SMEM = pl.BlockSpec(memory_space=pltpu.SMEM)
ANY = pl.BlockSpec(memory_space=pl.ANY)
PARAMS = pltpu.CompilerParams(vmem_limit_bytes=48 << 20)
SWAP = [(0, 1), (1, 0)]
SMALL = pl.CostEstimate(flops=0, bytes_accessed=0, transcendentals=0)


def dot(a, b, ca, cb):
    return lax.dot_general(a, b, (((ca,), (cb,)), ((), ())), preferred_element_type=F32)


def powers(line):
    bits = [1]
    while bits[-1] * 2 < line:
        bits.append(bits[-1] * 2)
    return bits


def to_place(value, d, line):
    return lax.ppermute(value, "expert", [(i, i ^ d) for i in range(line)])


def line_gather(block, line):
    got = {0: block}
    for bit in reversed(powers(line)):
        for d in list(got):
            got[d | bit] = to_place(got[d], bit, line)
    return got


def line_reduce(parts, line):
    parts = dict(enumerate(parts))
    for bit in powers(line):
        for d in sorted((d for d in parts if d & bit), reverse=True):
            moved = to_place(parts.pop(d), bit, line)
            kept = parts[d ^ bit].astype(F32) + moved.astype(F32)
            parts[d ^ bit] = kept.astype(moved.dtype)
    return parts[0]


def pick_kernel(n, cap, columns, scaled, *refs):
    slot_ref, weight_ref = refs[:2]
    blocks, pieces = refs[2 : 2 + n], refs[2 + n :]
    slots = columns * cap
    for j in range(n):
        block = blocks[j][...]
        ids = lax.broadcasted_iota(jnp.int32, (slots, block.shape[0]), 0)
        hits = [ids == slot_ref[j, k : k + 1, :] for k in range(slot_ref.shape[1])]
        pick = functools.reduce(jnp.add, [h.astype(F32) for h in hits]).astype(BF)
        rows = dot(pick, block, 1, 0)
        if scaled:
            given = functools.reduce(
                jnp.add,
                [jnp.where(h, weight_ref[j, k : k + 1, :], 0.0) for k, h in enumerate(hits)],
            )
            rows = rows * jnp.sum(given, axis=1, keepdims=True)
        rows = rows.astype(BF)
        for d in range(columns):
            pieces[d][j * cap : (j + 1) * cap, :] = rows[d * cap : (d + 1) * cap, :]


def pick_rows(slot, weight, blocks, cap, columns, scaled):
    rows, half = blocks[0].shape
    n = len(blocks)
    return pl.pallas_call(
        functools.partial(pick_kernel, n, cap, columns, scaled),
        out_shape=[jax.ShapeDtypeStruct((n * cap, half), BF)] * columns,
        in_specs=[VMEM] * (2 + n),
        out_specs=[VMEM] * columns,
        compiler_params=PARAMS,
        cost_estimate=SMALL,
        name="pick_scaled" if scaled else "pick",
    )(slot, weight, *blocks)


def stack_kernel(count, *refs):
    pieces, out = refs[:count], refs[count]
    at = 0
    for piece in pieces:
        size = piece.shape[0]
        out[at : at + size, :] = piece[...]
        at += size


def stack_rows(pieces):
    total = sum(p.shape[0] for p in pieces)
    half = pieces[0].shape[1]
    return pl.pallas_call(
        functools.partial(stack_kernel, len(pieces)),
        out_shape=jax.ShapeDtypeStruct((total, half), BF),
        in_specs=[VMEM] * len(pieces),
        out_specs=VMEM,
        compiler_params=PARAMS,
        cost_estimate=SMALL,
        name="stack",
    )(*pieces)


def join_kernel(n, cap, columns, weighted, *refs):
    slot_ref, weight_ref = refs[:2]
    pieces, rest = refs[2 : 2 + columns], refs[2 + columns :]
    held = rest[-1]
    if weighted:
        cots, parts, gates = rest[:n], rest[n : 2 * n], rest[2 * n]
    else:
        parts = rest[:n]
    slots = columns * cap
    top = slot_ref.shape[1]
    for j in range(n):
        for d in range(columns):
            held[d * cap : (d + 1) * cap, :] = pieces[d][j * cap : (j + 1) * cap, :]
        rows = held[...]
        ids = lax.broadcasted_iota(jnp.int32, (slots, slot_ref.shape[2]), 0)
        hits = [ids == slot_ref[j, k : k + 1, :] for k in range(top)]
        if weighted:
            given = functools.reduce(
                jnp.add,
                [jnp.where(h, weight_ref[j, k : k + 1, :], 0.0) for k, h in enumerate(hits)],
            )
            high = given.astype(BF)
            low = (given - high.astype(F32)).astype(BF)
            parts[j][...] = (dot(high, rows, 0, 0) + dot(low, rows, 0, 0)).astype(BF)
            meet = dot(rows, cots[j][...], 1, 1)
            for k, h in enumerate(hits):
                gates[j, k : k + 1, :] = jnp.sum(jnp.where(h, meet, 0.0), axis=0, keepdims=True)
        else:
            pick = functools.reduce(jnp.add, [h.astype(F32) for h in hits]).astype(BF)
            parts[j][...] = dot(pick, rows, 0, 0).astype(BF)


def join_rows(slot, weight, pieces, cap, cots=None):
    columns, half = len(pieces), pieces[0].shape[1]
    n, top, rows = slot.shape
    weighted = cots is not None
    outs = [jax.ShapeDtypeStruct((rows, half), BF)] * n
    if weighted:
        outs.append(jax.ShapeDtypeStruct((n, top, rows), F32))
    ins = [slot, weight] + list(pieces) + (list(cots) if weighted else [])
    out = pl.pallas_call(
        functools.partial(join_kernel, n, cap, columns, weighted),
        out_shape=outs,
        in_specs=[VMEM] * len(ins),
        out_specs=[VMEM] * len(outs),
        scratch_shapes=[pltpu.VMEM((columns * cap, half), BF)],
        compiler_params=PARAMS,
        cost_estimate=SMALL,
        name="join_weighted" if weighted else "join",
    )(*ins)
    return (list(out[:n]), out[n]) if weighted else (list(out[:n]), None)


def halves(head_ref, half):
    head = head_ref[0]
    return (
        pl.ds(pl.multiple_of(head * half, half), half),
        pl.ds(pl.multiple_of((1 - head) * half, half), half),
    )


def ahead_kernel(
    half, head_ref, mine_ref, other_ref, gate_ref, up_ref, down_ref,
    pre_gate_ref, pre_up_ref, act_ref, kept_ref, sent_ref,
):
    own, away = halves(head_ref, half)
    mine, other = mine_ref[...], other_ref[...]
    pre_gate = dot(mine, gate_ref[own, :], 1, 0) + dot(other, gate_ref[away, :], 1, 0)
    pre_up = dot(mine, up_ref[own, :], 1, 0) + dot(other, up_ref[away, :], 1, 0)
    pre_gate_ref[...] = pre_gate
    pre_up_ref[...] = pre_up
    act = (pre_gate * (1.0 / (1.0 + jnp.exp(-pre_gate))) * pre_up).astype(BF)
    act_ref[...] = act
    sent_ref[...] = dot(act, down_ref[:, away], 1, 0).astype(BF)
    kept_ref[...] = dot(act, down_ref[:, own], 1, 0).astype(BF)


def back_kernel(
    half, head_ref, mine_ref, other_ref, pre_gate_ref, pre_up_ref, gate_ref, up_ref, down_ref,
    d_gate_ref, d_up_ref, kept_ref, sent_ref,
):
    own, away = halves(head_ref, half)
    d_act = dot(mine_ref[...], down_ref[:, own], 1, 1) + dot(other_ref[...], down_ref[:, away], 1, 1)
    pre_gate, pre_up = pre_gate_ref[...], pre_up_ref[...]
    sig = 1.0 / (1.0 + jnp.exp(-pre_gate))
    d_gate = (d_act * pre_up * sig * (1.0 + pre_gate * (1.0 - sig))).astype(BF)
    d_up = (d_act * (pre_gate * sig)).astype(BF)
    d_gate_ref[...] = d_gate
    d_up_ref[...] = d_up
    for span, ref in ((away, sent_ref), (own, kept_ref)):
        ref[...] = (dot(d_gate, gate_ref[span, :], 1, 1) + dot(d_up, up_ref[span, :], 1, 1)).astype(BF)


def by_rows(kernel, head, rows_in, whole_in, outs, name):
    total, half = rows_in[0].shape
    block = min(256, total)

    def cut(width):
        return pl.BlockSpec((block, width), lambda i: (i, 0))

    return pl.pallas_call(
        functools.partial(kernel, half),
        grid=(total // block,),
        out_shape=[jax.ShapeDtypeStruct((total, width), dtype) for width, dtype in outs],
        in_specs=[SMEM]
        + [cut(v.shape[1]) for v in rows_in]
        + [pl.BlockSpec(v.shape, lambda i: (0, 0)) for v in whole_in],
        out_specs=[cut(width) for width, _ in outs],
        compiler_params=PARAMS,
        cost_estimate=SMALL,
        name=name,
    )(head, *rows_in, *whole_in)


def deal_kernel(sizes, kept_ref, came_ref, *pieces):
    at = 0
    for piece, size in zip(pieces, sizes):
        total = kept_ref[at : at + size, :].astype(F32) + came_ref[at : at + size, :].astype(F32)
        piece[...] = total.astype(BF)
        at += size


def deal_rows(kept, came, sizes):
    return pl.pallas_call(
        functools.partial(deal_kernel, sizes),
        out_shape=[jax.ShapeDtypeStruct((size, kept.shape[1]), BF) for size in sizes],
        in_specs=[VMEM, VMEM],
        out_specs=[VMEM] * len(sizes),
        compiler_params=PARAMS,
        cost_estimate=SMALL,
        name="deal",
    )(kept, came)


def together(*values):
    return lax.optimization_barrier(values)


def shards(tokens, routes, combine_weights, w_gate, w_up, w_down, cotangent):
    columns, line = lax.axis_size("path"), lax.axis_size("expert")
    column, place, head = lax.axis_index("path"), lax.axis_index("expert"), lax.axis_index("head")
    tok_rows, half = tokens.shape
    top = routes.shape[1]
    groups = columns * line
    cap = max(2, 2 * tok_rows * top // groups)
    flat = routes.reshape(-1)
    order = jnp.arange(flat.shape[0], dtype=jnp.int32)
    earlier = (flat[:, None] == flat[None, :]) & (order[:, None] < order[None, :])
    rank = jnp.sum(earlier.astype(jnp.int32), axis=0)
    position = (flat * cap + rank).astype(F32).reshape(tok_rows, top)
    about = jnp.concatenate([position.T, combine_weights.T], axis=0)

    info = jnp.stack([about] + [to_place(about, d, line) for d in range(1, line)], axis=0)
    where_to = info[:, :top].astype(jnp.int32)
    expert = where_to // cap
    slot = ((expert // line) ^ column) * cap + where_to % cap
    slot = jnp.where(expert % line == place, slot, -1)
    weight = info[:, top:]

    def exchange(pieces):
        return [pieces[0]] + [
            lax.ppermute(pieces[d], "path", [(i, i ^ d) for i in range(columns)])
            for d in range(columns - 1, 0, -1)
        ][::-1]

    near, far = slice(0, line - 1), slice(line - 1, line)

    def fetch(got, scaled):
        pieces = []
        for part in (near, far):
            blocks = [got[d] for d in range(line)[part]]
            pieces += exchange(pick_rows(slot[part], weight[part], blocks, cap, columns, scaled))
        return pieces

    tok_in = line_gather(tokens, line)
    cot_gated, _ = together(cotangent, tok_in[line - 1])
    cot_in = line_gather(cot_gated, line)

    gate_cols, up_cols, down_rows = w_gate[0], w_up[0], w_down[0]
    head_arg = head.reshape(1).astype(jnp.int32)
    hidden = gate_cols.shape[1]

    def swap(value):
        return lax.ppermute(value, "head", SWAP)

    def full(mine, other):
        first = head == 0
        return jnp.concatenate(
            [jnp.where(first, mine, other), jnp.where(first, other, mine)], axis=1
        )

    tok_mine = stack_rows(fetch(tok_in, False))
    tok_other = swap(tok_mine)
    pre_gate, pre_up, activation, out_kept, out_sent = by_rows(
        ahead_kernel,
        head_arg,
        [tok_mine, tok_other],
        [gate_cols, up_cols, down_rows],
        [(hidden, F32), (hidden, F32), (hidden, BF), (half, BF), (half, BF)],
        "ahead",
    )
    sizes = [cap * (line - 1)] * columns + [cap] * columns

    def send_home(kept, sent):
        pieces = deal_rows(kept, swap(sent), sizes)
        far_rows = exchange(pieces[columns:])
        return exchange(pieces[:columns]), far_rows

    out_near, out_far = send_home(out_kept, out_sent)
    cot_mine = stack_rows(fetch(cot_in, True))
    cot_other = swap(cot_mine)
    d_pre_gate, d_pre_up, back_kept, back_sent = by_rows(
        back_kernel,
        head_arg,
        [cot_mine, cot_other, pre_gate, pre_up],
        [gate_cols, up_cols, down_rows],
        [(hidden, BF), (hidden, BF), (half, BF), (half, BF)],
        "back",
    )
    back_near, back_far = send_home(back_kept, back_sent)

    d_pre_gate, d_pre_up, activation, _ = together(d_pre_gate, d_pre_up, activation, back_far[0])
    inbound, grad_in = full(tok_mine, tok_other), full(cot_mine, cot_other)
    grad_gate = dot(inbound, d_pre_gate, 0, 0).astype(BF)
    grad_up = dot(inbound, d_pre_up, 0, 0).astype(BF)
    grad_down = dot(activation, grad_in, 0, 0).astype(BF)

    def settle(near_rows, far_rows, cots):
        parts_far, gates_far = join_rows(
            slot[far], weight[far], far_rows, cap, None if cots is None else cots[far]
        )
        parts, gates_near = join_rows(
            slot[near], weight[near], near_rows, cap, None if cots is None else cots[near]
        )
        total = line_reduce(parts + parts_far, line)
        if cots is None:
            return total, None
        gates = [gates_near[d] for d in range(line - 1)] + [gates_far[0]]
        return total, line_reduce(gates, line)

    layer_out, local_gates = settle(out_near, out_far, [cot_in[d] for d in range(line)])
    d_tokens, _ = settle(back_near, back_far, None)
    d_gates = (local_gates + swap(local_gates)).T
    return (layer_out, d_tokens, d_gates, grad_gate[None], grad_up[None], grad_down[None])


def solution(mesh):
    rows = P(("path", "expert"), "head")
    whole = P(("path", "expert"), None)
    cols = P(("path", "expert"), None, "head")
    downs = P(("path", "expert"), "head", None)
    return jax.shard_map(
        shards,
        mesh=mesh,
        in_specs=(rows, whole, whole, cols, cols, downs, rows),
        out_specs=(rows, rows, whole, cols, cols, downs),
        check_vma=False,
    )
```

profile of v0, /device:TPU:0, one launch (start us, length us, event | category | flops | bytes accessed | tf_op | source)
XLA Modules:
  0.0 244.5 jit_solution(11032310163252366506)
XLA Ops:
  0.6 4.1 %collective-permute-start.4 = (bf16[256,1024]{1,0:T(8,128)(2,1)}, bf16[256,1024]{1,0:T(8,128)(2,1)S(1)}, u32[]{:S(2)}, u32[]{:S(2)}) collective-permute-start(bf16[256,1024]{1,0:T(8,128)(2,1)} %refs_2_.1), channel_id=1, source_target_pairs={{0,2},{1,3},{2,0},{3,1},{4,6},{5,7},{6,4},{7,5},{8,10},{9,11},{10,... | collective-permute-start | bytes 1572872 | tf_op jit(solution)/shard_map/ppermute | solution.py:32
  4.7 1.6 collective-permute-start.3
  9.1 1.9 collective-permute-start.1
  11.0 2.5 %collective-permute-start = (f32[4,256]{1,0:T(4,128)S(1)}, f32[4,256]{1,0:T(4,128)S(1)}, u32[]{:S(2)}, u32[]{:S(2)}) collective-permute-start(f32[4,256]{1,0:T(4,128)S(1)} %get-tuple-element.119), channel_id=1, source_target_pairs={{0,1},{1,0},{2,3},{3,2},{4,5},{5,4},{6,7},{7,6},{8,9},{9,8},{10,11... | collective-permute-start | bytes 12296 | tf_op jit(solution)/shard_map/ppermute | solution.py:32
  13.5 14.9 %collective-permute-done.4.refs_4_ = bf16[256,1024]{1,0:T(8,128)(2,1)S(1)} collective-permute-done((bf16[256,1024]{1,0:T(8,128)(2,1)}, bf16[256,1024]{1,0:T(8,128)(2,1)S(1)}, u32[]{:S(2)}, u32[]{:S(2)}) %collective-permute-start.4) | collective-permute-done | bytes 524320 | tf_op jit(solution)/shard_map/ppermute | solution.py:32
  31.1 1.6 collective-permute-start.5
  32.7 1.5 collective-permute-start.6
  34.7 6.6 %collective-permute-done.8.refs_2_ = bf16[256,1024]{1,0:T(8,128)(2,1)S(1)} collective-permute-done((bf16[256,1024]{1,0:T(8,128)(2,1)S(1)}, bf16[256,1024]{1,0:T(8,128)(2,1)S(1)}, u32[]{:S(2)}, u32[]{:S(2)}) %collective-permute-start.8) | collective-permute-done | bytes 524320 | tf_op jit(solution)/shard_map/ppermute | solution.py:32
  41.6 1.4 collective-permute-start.9
  43.0 1.5 collective-permute-start.10
  45.7 6.4 %collective-permute-done.6.refs_2_ = bf16[192,1024]{1,0:T(8,128)(2,1)S(1)} collective-permute-done((bf16[192,1024]{1,0:T(8,128)(2,1)S(1)}, bf16[192,1024]{1,0:T(8,128)(2,1)S(1)}, u32[]{:S(2)}, u32[]{:S(2)}) %collective-permute-start.6) | collective-permute-done | bytes 393248 | tf_op jit(solution)/shard_map/ppermute | solution.py:272
  52.7 1.5 collective-permute-done.9.refs_5_
  54.3 2.6 %collective-permute-done.10.refs_6_ = bf16[64,1024]{1,0:T(8,128)(2,1)S(1)} collective-permute-done((bf16[64,1024]{1,0:T(8,128)(2,1)S(1)}, bf16[64,1024]{1,0:T(8,128)(2,1)S(1)}, u32[]{:S(2)}, u32[]{:S(2)}) %collective-permute-start.10) | collective-permute-done | bytes 131104 | tf_op jit(solution)/shard_map/ppermute | solution.py:272
  57.9 3.3 %collective-permute-start.18 = (bf16[256,1024]{1,0:T(8,128)(2,1)S(1)}, bf16[256,1024]{1,0:T(8,128)(2,1)S(1)}, u32[]{:S(2)}, u32[]{:S(2)}) collective-permute-start(bf16[256,1024]{1,0:T(8,128)(2,1)S(1)} %copy-done.7), channel_id=1, source_target_pairs={{0,2},{1,3},{2,0},{3,1},{4,6},{5,7},{6,4},{7,5},{8,10},{9,11},{10,... | collective-permute-start | bytes 1572872 | tf_op jit(solution)/shard_map/ppermute | solution.py:32
  61.6 22.9 %collective-permute-done.18.refs_8_.refs_4_ = bf16[256,1024]{1,0:T(8,128)(2,1)S(1)} collective-permute-done((bf16[256,1024]{1,0:T(8,128)(2,1)S(1)}, bf16[256,1024]{1,0:T(8,128)(2,1)S(1)}, u32[]{:S(2)}, u32[]{:S(2)}) %collective-permute-start.18) | collective-permute-done | bytes 524320 | tf_op jit(solution)/shard_map/ppermute | solution.py:32
  84.5 1.4 collective-permute-done.17.refs_7_.refs_3_
  85.9 1.6 pick_scaled.2
  90.3 1.5 collective-permute-start.28
  91.8 6.5 %collective-permute-done.23.refs_6_.refs_2_ = bf16[256,1024]{1,0:T(8,128)(2,1)S(1)} collective-permute-done((bf16[256,1024]{1,0:T(8,128)(2,1)S(1)}, bf16[256,1024]{1,0:T(8,128)(2,1)S(1)}, u32[]{:S(2)}, u32[]{:S(2)}) %collective-permute-start.23) | collective-permute-done | bytes 524320 | tf_op jit(solution)/shard_map/ppermute | solution.py:32
  103.6 1.3 copy-done.31
  105.0 1.5 collective-permute-start.31
  106.5 1.4 copy-done.4
  107.9 10.7 %ahead.1 = (f32[1024,384]{1,0:T(8,128)S(1)}, f32[1024,384]{1,0:T(8,128)S(1)}, bf16[1024,384]{1,0:T(8,128)(2,1)S(1)}, bf16[1024,1024]{1,0:T(8,128)(2,1)}, bf16[1024,1024]{1,0:T(8,128)(2,1)}) custom-call(s32[1]{0:T(128)} %bitcast.6.head_ref, bf16[1024,1024]{1,0:T(8,128)(2,1)} %copy-done, bf16[1024,1024]{1,0:T(8,128)(2,1)} %copy-done.31, ...), custom_call_target="tpu_custom_call" | custom-call | tf_op jit(solution)/shard_map/ahead/pallas_call | solution.py:211
  119.5 1.5 stack.26.mine_ref
  121.6 2.2 collective-permute-done.13.came_ref
  125.2 2.7 %deal.2 = (bf16[192,1024]{1,0:T(8,128)(2,1)S(1)}, bf16[192,1024]{1,0:T(8,128)(2,1)}, bf16[192,1024]{1,0:T(8,128)(2,1)}, bf16[192,1024]{1,0:T(8,128)(2,1)}, bf16[...) custom-call(bf16[1024,1024]{1,0:T(8,128)(2,1)S(1)} %copy-done.6, ...), custom_call_target="tpu_custom_call" | custom-call | tf_op jit(solution)/shard_map/deal/pallas_call | solution.py:234
  132.3 1.3 copy-done.33
  133.6 11.6 %back.1 = (bf16[1024,384]{1,0:T(8,128)(2,1)S(1)}, bf16[1024,384]{1,0:T(8,128)(2,1)S(1)}, bf16[1024,1024]{1,0:T(8,128)(2,1)}, bf16[1024,1024]{1,0:T(8,128)(2,1)}) custom-call(s32[1]{0:T(128)} %bitcast.6.head_ref, bf16[1024,1024]{1,0:T(8,128)(2,1)} %copy-done.2, bf16[1024,1024]{1,0:T(8,128)(2,1)} %copy-done.33, ...), custom_call_target="tpu_custom_call" | custom-call | tf_op jit(solution)/shard_map/back/pallas_call | solution.py:211
  147.3 6.4 %collective-permute-done.21.refs_4_ = bf16[64,1024]{1,0:T(8,128)(2,1)S(1)} collective-permute-done((bf16[64,1024]{1,0:T(8,128)(2,1)S(1)}, bf16[64,1024]{1,0:T(8,128)(2,1)S(1)}, u32[]{:S(2)}, u32[]{:S(2)}) %collective-permute-start.21) | collective-permute-done | bytes 131104 | tf_op jit(solution)/shard_map/ppermute | solution.py:272
  154.9 5.1 %collective-permute-done.22.refs_5_ = bf16[64,1024]{1,0:T(8,128)(2,1)S(1)} collective-permute-done((bf16[64,1024]{1,0:T(8,128)(2,1)S(1)}, bf16[64,1024]{1,0:T(8,128)(2,1)S(1)}, u32[]{:S(2)}, u32[]{:S(2)}) %collective-permute-start.22) | collective-permute-done | bytes 131104 | tf_op jit(solution)/shard_map/ppermute | solution.py:272
  163.4 2.9 %join_weighted.2 = (bf16[256,1024]{1,0:T(8,128)(2,1)S(1)}, bf16[256,1024]{1,0:T(8,128)(2,1)S(1)}, bf16[256,1024]{1,0:T(8,128)(2,1)S(1)}, f32[3,2,256]{2,1,0:T(2,128)S(1)}) custom-call(s32[3,2,256]{2,1,0:T(2,128)S(1)} %slice.49.refs_0_, f32[3,2,256]{2,1,0:T(2,128)S(1)} %pad_maximum_fusion.10.refs_1_, bf16[192,1024]{1,0:T(8,128)(2,1)S(1)} %get-tuple-element.70.refs_2_, ...), custom_call_target="tpu_custom_call" | custom-call | tf_op jit(solution)/shard_map/join_weighted/pallas_call | solution.py:151
  167.1 1.9 collective-permute-start.45
  169.3 2.4 broadcast_select_fusion.3
  171.8 1.6 collective-permute-start.24
  175.2 2.2 deal.3
  179.3 1.7 collective-permute-start.40
  181.0 5.6 %collective-permute-done.24 = bf16[256,1024]{1,0:T(8,128)(2,1)S(1)} collective-permute-done((bf16[256,1024]{1,0:T(8,128)(2,1)S(1)}, bf16[256,1024]{1,0:T(8,128)(2,1)S(1)}, u32[]{:S(2)}, u32[]{:S(2)}) %collective-permute-start.24) | collective-permute-done | bytes 524320 | tf_op jit(solution)/shard_map/ppermute | solution.py:32
  188.7 1.7 collective-permute-start.36
  190.7 1.7 collective-permute-start.41
  192.4 3.6 %fusion.7 = bf16[1,2048,384]{2,1,0:T(8,128)(2,1)} fusion(bf16[1024,384]{1,0:T(8,128)(2,1)S(1)} %copy-done.28, bf16[1024,1024]{1,0:T(8,128)(2,1)S(1)} %copy-done.37, bf16[1024,1024]{1,0:T(8,128)(2,1)S(1)} %copy-done.36), kind=kOutput, calls=%fused_computation.8 | convolution fusion | flops 1619787776 | bytes 6553600 | tf_op jit(solution)/shard_map/dot_general | solution.py:21
  196.0 3.6 %fusion.8 = bf16[1,2048,384]{2,1,0:T(8,128)(2,1)} fusion(bf16[1024,384]{1,0:T(8,128)(2,1)S(1)} %copy-done.26, bf16[1024,1024]{1,0:T(8,128)(2,1)S(1)} %copy-done.37, bf16[1024,1024]{1,0:T(8,128)(2,1)S(1)} %copy-done.36), kind=kOutput, calls=%fused_computation.9 | convolution fusion | flops 1619787776 | bytes 6553600 | tf_op jit(solution)/shard_map/dot_general | solution.py:21
  200.7 2.8 %collective-permute-done.35.refs_4_ = bf16[192,1024]{1,0:T(8,128)(2,1)S(1)} collective-permute-done((bf16[192,1024]{1,0:T(8,128)(2,1)S(1)}, bf16[192,1024]{1,0:T(8,128)(2,1)S(1)}, u32[]{:S(2)}, u32[]{:S(2)}) %collective-permute-start.35) | collective-permute-done | bytes 393248 | tf_op jit(solution)/shard_map/ppermute | solution.py:272
  204.2 1.3 collective-permute-start.37
  205.5 15.4 %collective-permute-done.41 = bf16[256,1024]{1,0:T(8,128)(2,1)S(1)} collective-permute-done((bf16[256,1024]{1,0:T(8,128)(2,1)S(1)}, bf16[256,1024]{1,0:T(8,128)(2,1)S(1)}, u32[]{:S(2)}, u32[]{:S(2)}) %collective-permute-start.41) | collective-permute-done | bytes 524320 | tf_op jit(solution)/shard_map/ppermute | solution.py:32
  221.2 3.0 %fusion.9 = bf16[1,384,2048]{2,1,0:T(8,128)(2,1)} fusion(bf16[1024,384]{1,0:T(8,128)(2,1)S(1)} %copy-done.24, bf16[1024,1024]{1,0:T(8,128)(2,1)S(1)} %get-tuple-element.115, bf16[1024,1024]{1,0:T(8,128)(2,1)S(1)} %get-tuple-element.114), kind=kOutput, calls=%fused_computation.10 | convolution fusion | flops 1619787776 | bytes 6553600 | tf_op jit(solution)/shard_map/dot_general | solution.py:21
  224.2 2.1 add_convert_fusion.3
  226.3 12.5 %collective-permute-done.37 = bf16[256,1024]{1,0:T(8,128)(2,1)S(1)} collective-permute-done((bf16[256,1024]{1,0:T(8,128)(2,1)S(1)}, bf16[256,1024]{1,0:T(8,128)(2,1)S(1)}, u32[]{:S(2)}, u32[]{:S(2)}) %collective-permute-start.37) | collective-permute-done | bytes 524320 | tf_op jit(solution)/shard_map/ppermute | solution.py:32
  238.8 4.7 %collective-permute-done.42 = bf16[256,1024]{1,0:T(8,128)(2,1)S(1)} collective-permute-done((bf16[256,1024]{1,0:T(8,128)(2,1)S(1)}, bf16[256,1024]{1,0:T(8,128)(2,1)S(1)}, u32[]{:S(2)}, u32[]{:S(2)}) %collective-permute-start.42) | collective-permute-done | bytes 524320 | tf_op jit(solution)/shard_map/ppermute | solution.py:32
  (161 shorter events, 41.8 us)
Async XLA Ops:
  0.6 27.7 %collective-permute-start.4 = (bf16[256,1024]{1,0:T(8,128)(2,1)}, bf16[256,1024]{1,0:T(8,128)(2,1)S(1)}, u32[]{:S(2)}, u32[]{:S(2)}) collective-permute-start(bf16[256,1024]{1,0:T(8,128)(2,1)} %refs_2_.1), channel_id=1, source_target_pairs={{0,2},{1,3},{2,0},{3,1},{4,6},{5,7},{6,4},{7,5},{8,10},{9,11},{10,... | collective-permute-start | bytes 1572872 | tf_op jit(solution)/shard_map/ppermute | solution.py:32
  4.7 24.8 %collective-permute-start.3 = (bf16[256,1024]{1,0:T(8,128)(2,1)}, bf16[256,1024]{1,0:T(8,128)(2,1)S(1)}, u32[]{:S(2)}, u32[]{:S(2)}) collective-permute-start(bf16[256,1024]{1,0:T(8,128)(2,1)} %refs_2_.1), channel_id=1, source_target_pairs={{0,1},{1,0},{2,3},{3,2},{4,5},{5,4},{6,7},{7,6},{8,9},{9,8},{10,11... | collective-permute-start | bytes 1572872 | tf_op jit(solution)/shard_map/ppermute | solution.py:32
  9.1 20.3 %collective-permute-start.2 = (f32[4,256]{1,0:T(4,128)S(1)}, f32[4,256]{1,0:T(4,128)S(1)}, u32[]{:S(2)}, u32[]{:S(2)}) collective-permute-start(f32[4,256]{1,0:T(4,128)S(1)} %get-tuple-element.119), channel_id=1, source_target_pairs={{0,3},{1,2},{2,1},{3,0},{4,7},{5,6},{6,5},{7,4},{8,11},{9,10},{10,... | collective-permute-start | bytes 12296 | tf_op jit(solution)/shard_map/ppermute | solution.py:32
  9.1 20.3 %collective-permute-start.1 = (f32[4,256]{1,0:T(4,128)S(1)}, f32[4,256]{1,0:T(4,128)S(1)}, u32[]{:S(2)}, u32[]{:S(2)}) collective-permute-start(f32[4,256]{1,0:T(4,128)S(1)} %get-tuple-element.119), channel_id=1, source_target_pairs={{0,2},{1,3},{2,0},{3,1},{4,6},{5,7},{6,4},{7,5},{8,10},{9,11},{10,... | collective-permute-start | bytes 12296 | tf_op jit(solution)/shard_map/ppermute | solution.py:32
  11.0 18.4 %collective-permute-start = (f32[4,256]{1,0:T(4,128)S(1)}, f32[4,256]{1,0:T(4,128)S(1)}, u32[]{:S(2)}, u32[]{:S(2)}) collective-permute-start(f32[4,256]{1,0:T(4,128)S(1)} %get-tuple-element.119), channel_id=1, source_target_pairs={{0,1},{1,0},{2,3},{3,2},{4,5},{5,4},{6,7},{7,6},{8,9},{9,8},{10,11... | collective-permute-start | bytes 12296 | tf_op jit(solution)/shard_map/ppermute | solution.py:32
  28.3 12.9 %collective-permute-start.8 = (bf16[256,1024]{1,0:T(8,128)(2,1)S(1)}, bf16[256,1024]{1,0:T(8,128)(2,1)S(1)}, u32[]{:S(2)}, u32[]{:S(2)}) collective-permute-start(bf16[256,1024]{1,0:T(8,128)(2,1)S(1)} %collective-permute-done.4.refs_4_), channel_id=1, source_target_pairs={{0,1},{1,0},{2,3},{3,2},{4,5},{5,4},{6,7},{7,6},{8,9},{9,8},{10,11... | collective-permute-start | bytes 1572872 | tf_op jit(solution)/shard_map/ppermute | solution.py:32
  31.1 13.4 %collective-permute-start.5 = (bf16[192,1024]{1,0:T(8,128)(2,1)S(1)}, bf16[192,1024]{1,0:T(8,128)(2,1)S(1)}, u32[]{:S(2)}, u32[]{:S(2)}) collective-permute-start(bf16[192,1024]{1,0:T(8,128)(2,1)S(1)} %get-tuple-element.61), channel_id=1, source_target_pairs={{0,8},{8,0},{16,24},{24,16},{1,9},{9,1},{17,25},{25,17},{2,10},{10... | collective-permute-start | bytes 1179656 | tf_op jit(solution)/shard_map/ppermute | solution.py:272
  32.7 19.4 %collective-permute-start.6 = (bf16[192,1024]{1,0:T(8,128)(2,1)S(1)}, bf16[192,1024]{1,0:T(8,128)(2,1)S(1)}, u32[]{:S(2)}, u32[]{:S(2)}) collective-permute-start(bf16[192,1024]{1,0:T(8,128)(2,1)S(1)} %get-tuple-element.62), channel_id=1, source_target_pairs={{0,16},{8,24},{16,0},{24,8},{1,17},{9,25},{17,1},{25,9},{2,18},{10... | collective-permute-start | bytes 1179656 | tf_op jit(solution)/shard_map/ppermute | solution.py:272
  34.2 18.5 %collective-permute-start.7 = (bf16[192,1024]{1,0:T(8,128)(2,1)S(1)}, bf16[192,1024]{1,0:T(8,128)(2,1)S(1)}, u32[]{:S(2)}, u32[]{:S(2)}) collective-permute-start(bf16[192,1024]{1,0:T(8,128)(2,1)S(1)} %get-tuple-element.63), channel_id=1, source_target_pairs={{0,24},{8,16},{16,8},{24,0},{1,25},{9,17},{17,9},{25,1},{2,26},{10... | collective-permute-start | bytes 1179656 | tf_op jit(solution)/shard_map/ppermute | solution.py:272
  34.7 63.6 %copy-start.17 = (s32[1,2,256]{2,1,0:T(2,128)}, s32[1,2,256]{2,1,0:T(2,128)S(1)}, u32[]{:S(2)}) copy-start(s32[1,2,256]{2,1,0:T(2,128)S(1)} %slice.50.refs_0_) | copy-start | bytes 6148
  41.6 12.7 %collective-permute-start.9 = (bf16[64,1024]{1,0:T(8,128)(2,1)S(1)}, bf16[64,1024]{1,0:T(8,128)(2,1)S(1)}, u32[]{:S(2)}, u32[]{:S(2)}) collective-permute-start(bf16[64,1024]{1,0:T(8,128)(2,1)S(1)} %get-tuple-element.65), channel_id=1, source_target_pairs={{0,8},{8,0},{16,24},{24,16},{1,9},{9,1},{17,25},{25,17},{2,10},{10... | collective-permute-start | bytes 393224 | tf_op jit(solution)/shard_map/ppermute | solution.py:272
  43.0 13.9 %collective-permute-start.10 = (bf16[64,1024]{1,0:T(8,128)(2,1)S(1)}, bf16[64,1024]{1,0:T(8,128)(2,1)S(1)}, u32[]{:S(2)}, u32[]{:S(2)}) collective-permute-start(bf16[64,1024]{1,0:T(8,128)(2,1)S(1)} %get-tuple-element.66), channel_id=1, source_target_pairs={{0,16},{8,24},{16,0},{24,8},{1,17},{9,25},{17,1},{25,9},{2,18},{10... | collective-permute-start | bytes 393224 | tf_op jit(solution)/shard_map/ppermute | solution.py:272
  44.5 12.4 %collective-permute-start.11 = (bf16[64,1024]{1,0:T(8,128)(2,1)S(1)}, bf16[64,1024]{1,0:T(8,128)(2,1)S(1)}, u32[]{:S(2)}, u32[]{:S(2)}) collective-permute-start(bf16[64,1024]{1,0:T(8,128)(2,1)S(1)} %get-tuple-element.67), channel_id=1, source_target_pairs={{0,24},{8,16},{16,8},{24,0},{1,25},{9,17},{17,9},{25,1},{2,26},{10... | collective-permute-start | bytes 393224 | tf_op jit(solution)/shard_map/ppermute | solution.py:272
  57.0 46.6 %collective-permute-start.12 = (bf16[1024,1024]{1,0:T(8,128)(2,1)S(1)}, bf16[1024,1024]{1,0:T(8,128)(2,1)S(1)}, u32[]{:S(2)}, u32[]{:S(2)}) collective-permute-start(bf16[1024,1024]{1,0:T(8,128)(2,1)S(1)} %stack.25.mine_ref), channel_id=1, source_target_pairs={{0,4},{4,0},{1,5},{5,1},{2,6},{6,2},{3,7},{7,3},{8,12},{12,8},{9,1... | collective-permute-start | bytes 6291464 | tf_op jit(solution)/shard_map/ppermute | solution.py:294
  57.9 26.6 %collective-permute-start.18 = (bf16[256,1024]{1,0:T(8,128)(2,1)S(1)}, bf16[256,1024]{1,0:T(8,128)(2,1)S(1)}, u32[]{:S(2)}, u32[]{:S(2)}) collective-permute-start(bf16[256,1024]{1,0:T(8,128)(2,1)S(1)} %copy-done.7), channel_id=1, source_target_pairs={{0,2},{1,3},{2,0},{3,1},{4,6},{5,7},{6,4},{7,5},{8,10},{9,11},{10,... | collective-permute-start | bytes 1572872 | tf_op jit(solution)/shard_map/ppermute | solution.py:32
  61.2 24.7 %collective-permute-start.17 = (bf16[256,1024]{1,0:T(8,128)(2,1)S(1)}, bf16[256,1024]{1,0:T(8,128)(2,1)S(1)}, u32[]{:S(2)}, u32[]{:S(2)}) collective-permute-start(bf16[256,1024]{1,0:T(8,128)(2,1)S(1)} %copy-done.7), channel_id=1, source_target_pairs={{0,1},{1,0},{2,3},{3,2},{4,5},{5,4},{6,7},{7,6},{8,9},{9,8},{10,11... | collective-permute-start | bytes 1572872 | tf_op jit(solution)/shard_map/ppermute | solution.py:32
  84.5 13.8 %collective-permute-start.23 = (bf16[256,1024]{1,0:T(8,128)(2,1)S(1)}, bf16[256,1024]{1,0:T(8,128)(2,1)S(1)}, u32[]{:S(2)}, u32[]{:S(2)}) collective-permute-start(bf16[256,1024]{1,0:T(8,128)(2,1)S(1)} %collective-permute-done.18.refs_8_.refs_4_), channel_id=1, source_target_pairs={{0,1},{1,0},{2,3},{3,2},{4,5},{5,4},{6,7},{7,6},{8,9},{9,8},{10,11... | collective-permute-start | bytes 1572872 | tf_op jit(solution)/shard_map/ppermute | solution.py:32
  88.3 13.5 %collective-permute-start.26 = (bf16[192,1024]{1,0:T(8,128)(2,1)S(1)}, bf16[192,1024]{1,0:T(8,128)(2,1)S(1)}, u32[]{:S(2)}, u32[]{:S(2)}) collective-permute-start(bf16[192,1024]{1,0:T(8,128)(2,1)S(1)} %get-tuple-element.84), channel_id=1, source_target_pairs={{0,8},{8,0},{16,24},{24,16},{1,9},{9,1},{17,25},{25,17},{2,10},{10... | collective-permute-start | bytes 1179656 | tf_op jit(solution)/shard_map/ppermute | solution.py:272
  89.3 30.2 %collective-permute-start.27 = (bf16[192,1024]{1,0:T(8,128)(2,1)}, bf16[192,1024]{1,0:T(8,128)(2,1)}, u32[]{:S(2)}, u32[]{:S(2)}) collective-permute-start(bf16[192,1024]{1,0:T(8,128)(2,1)} %get-tuple-element.85), channel_id=1, source_target_pairs={{0,16},{8,24},{16,0},{24,8},{1,17},{9,25},{17,1},{25,9},{2,18},{10... | collective-permute-start | bytes 1179656 | tf_op jit(solution)/shard_map/ppermute | solution.py:272
  90.3 29.2 %collective-permute-start.28 = (bf16[192,1024]{1,0:T(8,128)(2,1)}, bf16[192,1024]{1,0:T(8,128)(2,1)}, u32[]{:S(2)}, u32[]{:S(2)}) collective-permute-start(bf16[192,1024]{1,0:T(8,128)(2,1)} %get-tuple-element.86), channel_id=1, source_target_pairs={{0,24},{8,16},{16,8},{24,0},{1,25},{9,17},{17,9},{25,1},{2,26},{10... | collective-permute-start | bytes 1179656 | tf_op jit(solution)/shard_map/ppermute | solution.py:272
  100.9 18.6 %collective-permute-start.29 = (bf16[64,1024]{1,0:T(8,128)(2,1)}, bf16[64,1024]{1,0:T(8,128)(2,1)}, u32[]{:S(2)}, u32[]{:S(2)}) collective-permute-start(bf16[64,1024]{1,0:T(8,128)(2,1)} %get-tuple-element.88), channel_id=1, source_target_pairs={{0,8},{8,0},{16,24},{24,16},{1,9},{9,1},{17,25},{25,17},{2,10},{10... | collective-permute-start | bytes 393224 | tf_op jit(solution)/shard_map/ppermute | solution.py:272
  102.5 17.0 %collective-permute-start.30 = (bf16[64,1024]{1,0:T(8,128)(2,1)}, bf16[64,1024]{1,0:T(8,128)(2,1)}, u32[]{:S(2)}, u32[]{:S(2)}) collective-permute-start(bf16[64,1024]{1,0:T(8,128)(2,1)} %get-tuple-element.89), channel_id=1, source_target_pairs={{0,16},{8,24},{16,0},{24,8},{1,17},{9,25},{17,1},{25,9},{2,18},{10... | collective-permute-start | bytes 393224 | tf_op jit(solution)/shard_map/ppermute | solution.py:272
  105.0 14.5 %collective-permute-start.31 = (bf16[64,1024]{1,0:T(8,128)(2,1)}, bf16[64,1024]{1,0:T(8,128)(2,1)}, u32[]{:S(2)}, u32[]{:S(2)}) collective-permute-start(bf16[64,1024]{1,0:T(8,128)(2,1)} %get-tuple-element.90), channel_id=1, source_target_pairs={{0,24},{8,16},{16,8},{24,0},{1,25},{9,17},{17,9},{25,1},{2,26},{10... | collective-permute-start | bytes 393224 | tf_op jit(solution)/shard_map/ppermute | solution.py:272
  119.5 4.4 %collective-permute-start.13 = (bf16[1024,1024]{1,0:T(8,128)(2,1)}, bf16[1024,1024]{1,0:T(8,128)(2,1)S(1)}, u32[]{:S(2)}, u32[]{:S(2)}) collective-permute-start(bf16[1024,1024]{1,0:T(8,128)(2,1)} %get-tuple-element.69), channel_id=1, source_target_pairs={{0,4},{4,0},{1,5},{5,1},{2,6},{6,2},{3,7},{7,3},{8,12},{12,8},{9,1... | collective-permute-start | bytes 6291464 | tf_op jit(solution)/shard_map/ppermute | solution.py:294
  121.1 11.2 %collective-permute-start.32 = (bf16[1024,1024]{1,0:T(8,128)(2,1)S(1)}, bf16[1024,1024]{1,0:T(8,128)(2,1)S(1)}, u32[]{:S(2)}, u32[]{:S(2)}) collective-permute-start(bf16[1024,1024]{1,0:T(8,128)(2,1)S(1)} %stack.26.mine_ref), channel_id=1, source_target_pairs={{0,4},{4,0},{1,5},{5,1},{2,6},{6,2},{3,7},{7,3},{8,12},{12,8},{9,1... | collective-permute-start | bytes 6291464 | tf_op jit(solution)/shard_map/ppermute | solution.py:294
  127.9 18.2 %collective-permute-start.20 = (bf16[64,1024]{1,0:T(8,128)(2,1)S(1)}, bf16[64,1024]{1,0:T(8,128)(2,1)S(1)}, u32[]{:S(2)}, u32[]{:S(2)}) collective-permute-start(bf16[64,1024]{1,0:T(8,128)(2,1)S(1)} %get-tuple-element.79), channel_id=1, source_target_pairs={{0,8},{8,0},{16,24},{24,16},{1,9},{9,1},{17,25},{25,17},{2,10},{10... | collective-permute-start | bytes 393224 | tf_op jit(solution)/shard_map/ppermute | solution.py:272
  128.8 33.6 %collective-permute-start.14 = (bf16[192,1024]{1,0:T(8,128)(2,1)}, bf16[192,1024]{1,0:T(8,128)(2,1)}, u32[]{:S(2)}, u32[]{:S(2)}) collective-permute-start(bf16[192,1024]{1,0:T(8,128)(2,1)} %get-tuple-element.71), channel_id=1, source_target_pairs={{0,8},{8,0},{16,24},{24,16},{1,9},{9,1},{17,25},{25,17},{2,10},{10... | collective-permute-start | bytes 1179656 | tf_op jit(solution)/shard_map/ppermute | solution.py:272
  129.9 32.5 %collective-permute-start.15 = (bf16[192,1024]{1,0:T(8,128)(2,1)}, bf16[192,1024]{1,0:T(8,128)(2,1)}, u32[]{:S(2)}, u32[]{:S(2)}) collective-permute-start(bf16[192,1024]{1,0:T(8,128)(2,1)} %get-tuple-element.72), channel_id=1, source_target_pairs={{0,16},{8,24},{16,0},{24,8},{1,17},{9,25},{17,1},{25,9},{2,18},{10... | collective-permute-start | bytes 1179656 | tf_op jit(solution)/shard_map/ppermute | solution.py:272
  131.0 31.3 %collective-permute-start.16 = (bf16[192,1024]{1,0:T(8,128)(2,1)}, bf16[192,1024]{1,0:T(8,128)(2,1)}, u32[]{:S(2)}, u32[]{:S(2)}) collective-permute-start(bf16[192,1024]{1,0:T(8,128)(2,1)} %get-tuple-element.73), channel_id=1, source_target_pairs={{0,24},{8,16},{16,8},{24,0},{1,25},{9,17},{17,9},{25,1},{2,26},{10... | collective-permute-start | bytes 1179656 | tf_op jit(solution)/shard_map/ppermute | solution.py:272
  146.1 29.1 %collective-permute-start.33 = (bf16[1024,1024]{1,0:T(8,128)(2,1)}, bf16[1024,1024]{1,0:T(8,128)(2,1)}, u32[]{:S(2)}, u32[]{:S(2)}) collective-permute-start(bf16[1024,1024]{1,0:T(8,128)(2,1)} %get-tuple-element.94), channel_id=1, source_target_pairs={{0,4},{4,0},{1,5},{5,1},{2,6},{6,2},{3,7},{7,3},{8,12},{12,8},{9,1... | collective-permute-start | bytes 6291464 | tf_op jit(solution)/shard_map/ppermute | solution.py:294
  146.1 7.6 %collective-permute-start.21 = (bf16[64,1024]{1,0:T(8,128)(2,1)S(1)}, bf16[64,1024]{1,0:T(8,128)(2,1)S(1)}, u32[]{:S(2)}, u32[]{:S(2)}) collective-permute-start(bf16[64,1024]{1,0:T(8,128)(2,1)S(1)} %get-tuple-element.80), channel_id=1, source_target_pairs={{0,16},{8,24},{16,0},{24,8},{1,17},{9,25},{17,1},{25,9},{2,18},{10... | collective-permute-start | bytes 393224 | tf_op jit(solution)/shard_map/ppermute | solution.py:272
  153.7 6.4 %collective-permute-start.22 = (bf16[64,1024]{1,0:T(8,128)(2,1)S(1)}, bf16[64,1024]{1,0:T(8,128)(2,1)S(1)}, u32[]{:S(2)}, u32[]{:S(2)}) collective-permute-start(bf16[64,1024]{1,0:T(8,128)(2,1)S(1)} %get-tuple-element.81), channel_id=1, source_target_pairs={{0,24},{8,16},{16,8},{24,0},{1,25},{9,17},{17,9},{25,1},{2,26},{10... | collective-permute-start | bytes 393224 | tf_op jit(solution)/shard_map/ppermute | solution.py:272
  162.1 4.3 %collective-permute-start.44 = (f32[2,256]{1,0:T(2,128)}, f32[2,256]{1,0:T(2,128)}, u32[]{:S(2)}, u32[]{:S(2)}) collective-permute-start(f32[2,256]{1,0:T(2,128)} %bitcast.13), channel_id=1, source_target_pairs={{0,1},{1,0},{2,3},{3,2},{4,5},{5,4},{6,7},{7,6},{8,9},{9,8},{10,11... | collective-permute-start | bytes 6152 | tf_op jit(solution)/shard_map/ppermute | solution.py:32
  167.1 6.3 %collective-permute-start.45 = (f32[2,256]{1,0:T(2,128)S(1)}, f32[2,256]{1,0:T(2,128)S(1)}, u32[]{:S(2)}, u32[]{:S(2)}) collective-permute-start(f32[2,256]{1,0:T(2,128)S(1)} %bitcast_add_fusion), channel_id=1, source_target_pairs={{0,2},{1,3},{2,0},{3,1},{4,6},{5,7},{6,4},{7,5},{8,10},{9,11},{10,... | collective-permute-start | bytes 6152 | tf_op jit(solution)/shard_map/ppermute | solution.py:32
  169.0 4.4 %collective-permute-start.43 = (f32[2,256]{1,0:T(2,128)S(1)}, f32[2,256]{1,0:T(2,128)S(1)}, u32[]{:S(2)}, u32[]{:S(2)}) collective-permute-start(f32[2,256]{1,0:T(2,128)S(1)} %slice_bitcast_fusion), channel_id=1, source_target_pairs={{0,1},{1,0},{2,3},{3,2},{4,5},{5,4},{6,7},{7,6},{8,9},{9,8},{10,11... | collective-permute-start | bytes 6152 | tf_op jit(solution)/shard_map/ppermute | solution.py:32
  171.8 14.9 %collective-permute-start.24 = (bf16[256,1024]{1,0:T(8,128)(2,1)S(1)}, bf16[256,1024]{1,0:T(8,128)(2,1)S(1)}, u32[]{:S(2)}, u32[]{:S(2)}) collective-permute-start(bf16[256,1024]{1,0:T(8,128)(2,1)S(1)} %copy-done.30), channel_id=1, source_target_pairs={{0,1},{1,0},{2,3},{3,2},{4,5},{5,4},{6,7},{7,6},{8,9},{9,8},{10,11... | collective-permute-start | bytes 1572872 | tf_op jit(solution)/shard_map/ppermute | solution.py:32
  173.4 1.2 collective-permute-start.46
  173.8 50.4 %collective-permute-start.19 = (bf16[256,1024]{1,0:T(8,128)(2,1)S(1)}, bf16[256,1024]{1,0:T(8,128)(2,1)}, u32[]{:S(2)}, u32[]{:S(2)}) collective-permute-start(bf16[256,1024]{1,0:T(8,128)(2,1)S(1)} %get-tuple-element.76), channel_id=1, source_target_pairs={{0,1},{1,0},{2,3},{3,2},{4,5},{5,4},{6,7},{7,6},{8,9},{9,8},{10,11... | collective-permute-start | bytes 1572872 | tf_op jit(solution)/shard_map/ppermute | solution.py:32
  177.5 10.4 %collective-permute-start.38 = (bf16[64,1024]{1,0:T(8,128)(2,1)S(1)}, bf16[64,1024]{1,0:T(8,128)(2,1)S(1)}, u32[]{:S(2)}, u32[]{:S(2)}) collective-permute-start(bf16[64,1024]{1,0:T(8,128)(2,1)S(1)} %get-tuple-element.103), channel_id=1, source_target_pairs={{0,8},{8,0},{16,24},{24,16},{1,9},{9,1},{17,25},{25,17},{2,10},{10... | collective-permute-start | bytes 393224 | tf_op jit(solution)/shard_map/ppermute | solution.py:272
  178.5 10.2 %collective-permute-start.39 = (bf16[64,1024]{1,0:T(8,128)(2,1)S(1)}, bf16[64,1024]{1,0:T(8,128)(2,1)S(1)}, u32[]{:S(2)}, u32[]{:S(2)}) collective-permute-start(bf16[64,1024]{1,0:T(8,128)(2,1)S(1)} %get-tuple-element.104), channel_id=1, source_target_pairs={{0,16},{8,24},{16,0},{24,8},{1,17},{9,25},{17,1},{25,9},{2,18},{10... | collective-permute-start | bytes 393224 | tf_op jit(solution)/shard_map/ppermute | solution.py:272
  179.3 11.1 %collective-permute-start.40 = (bf16[64,1024]{1,0:T(8,128)(2,1)S(1)}, bf16[64,1024]{1,0:T(8,128)(2,1)S(1)}, u32[]{:S(2)}, u32[]{:S(2)}) collective-permute-start(bf16[64,1024]{1,0:T(8,128)(2,1)S(1)} %get-tuple-element.105), channel_id=1, source_target_pairs={{0,24},{8,16},{16,8},{24,0},{1,25},{9,17},{17,9},{25,1},{2,26},{10... | collective-permute-start | bytes 393224 | tf_op jit(solution)/shard_map/ppermute | solution.py:272
  186.8 12.8 %collective-permute-start.34 = (bf16[192,1024]{1,0:T(8,128)(2,1)S(1)}, bf16[192,1024]{1,0:T(8,128)(2,1)S(1)}, u32[]{:S(2)}, u32[]{:S(2)}) collective-permute-start(bf16[192,1024]{1,0:T(8,128)(2,1)S(1)} %get-tuple-element.96), channel_id=1, source_target_pairs={{0,8},{8,0},{16,24},{24,16},{1,9},{9,1},{17,25},{25,17},{2,10},{10... | collective-permute-start | bytes 1179656 | tf_op jit(solution)/shard_map/ppermute | solution.py:272
  187.8 15.7 %collective-permute-start.35 = (bf16[192,1024]{1,0:T(8,128)(2,1)S(1)}, bf16[192,1024]{1,0:T(8,128)(2,1)S(1)}, u32[]{:S(2)}, u32[]{:S(2)}) collective-permute-start(bf16[192,1024]{1,0:T(8,128)(2,1)S(1)} %get-tuple-element.97), channel_id=1, source_target_pairs={{0,16},{8,24},{16,0},{24,8},{1,17},{9,25},{17,1},{25,9},{2,18},{10... | collective-permute-start | bytes 1179656 | tf_op jit(solution)/shard_map/ppermute | solution.py:272
  188.7 14.8 %collective-permute-start.36 = (bf16[192,1024]{1,0:T(8,128)(2,1)S(1)}, bf16[192,1024]{1,0:T(8,128)(2,1)S(1)}, u32[]{:S(2)}, u32[]{:S(2)}) collective-permute-start(bf16[192,1024]{1,0:T(8,128)(2,1)S(1)} %get-tuple-element.98), channel_id=1, source_target_pairs={{0,24},{8,16},{16,8},{24,0},{1,25},{9,17},{17,9},{25,1},{2,26},{10... | collective-permute-start | bytes 1179656 | tf_op jit(solution)/shard_map/ppermute | solution.py:272
  190.7 30.2 %collective-permute-start.41 = (bf16[256,1024]{1,0:T(8,128)(2,1)S(1)}, bf16[256,1024]{1,0:T(8,128)(2,1)S(1)}, u32[]{:S(2)}, u32[]{:S(2)}) collective-permute-start(bf16[256,1024]{1,0:T(8,128)(2,1)S(1)} %join.3), channel_id=1, source_target_pairs={{0,1},{1,0},{2,3},{3,2},{4,5},{5,4},{6,7},{7,6},{8,9},{9,8},{10,11... | collective-permute-start | bytes 1572872 | tf_op jit(solution)/shard_map/ppermute | solution.py:32
  199.6 24.6 %collective-permute-start.25 = (bf16[256,1024]{1,0:T(8,128)(2,1)S(1)}, bf16[256,1024]{1,0:T(8,128)(2,1)S(1)}, u32[]{:S(2)}, u32[]{:S(2)}) collective-permute-start(bf16[256,1024]{1,0:T(8,128)(2,1)S(1)} %add_convert_fusion.4), channel_id=1, source_target_pairs={{0,2},{1,3},{2,0},{3,1},{4,6},{5,7},{6,4},{7,5},{8,10},{9,11},{10,... | collective-permute-start | bytes 1572872 | tf_op jit(solution)/shard_map/ppermute | solution.py:32
  204.2 34.6 %collective-permute-start.37 = (bf16[256,1024]{1,0:T(8,128)(2,1)S(1)}, bf16[256,1024]{1,0:T(8,128)(2,1)S(1)}, u32[]{:S(2)}, u32[]{:S(2)}) collective-permute-start(bf16[256,1024]{1,0:T(8,128)(2,1)S(1)} %get-tuple-element.100), channel_id=1, source_target_pairs={{0,1},{1,0},{2,3},{3,2},{4,5},{5,4},{6,7},{7,6},{8,9},{9,8},{10,11... | collective-permute-start | bytes 1572872 | tf_op jit(solution)/shard_map/ppermute | solution.py:32
  221.1 22.4 %collective-permute-start.42 = (bf16[256,1024]{1,0:T(8,128)(2,1)S(1)}, bf16[256,1024]{1,0:T(8,128)(2,1)S(1)}, u32[]{:S(2)}, u32[]{:S(2)}) collective-permute-start(bf16[256,1024]{1,0:T(8,128)(2,1)S(1)} %add_convert_fusion.1), channel_id=1, source_target_pairs={{0,2},{1,3},{2,0},{3,1},{4,6},{5,7},{6,4},{7,5},{8,10},{9,11},{10,... | collective-permute-start | bytes 1572872 | tf_op jit(solution)/shard_map/ppermute | solution.py:32
  (37 other events, 391.1 us)
where the time goes:
time: 245 us
  waiting for transfers between devices  119 us (49%)
  starting transfers between devices  52.6 us (21%)
  Pallas kernels  37.6 us (15%)
  local copies, waits for them, and re-layouts  15.1 us (6%)
  matrix products  10.1 us (4%)
  other arithmetic  9.15 us (4%)
    ppermute x18, waiting for transfers between devices, to_place(): return lax.ppermute(value, 'expert', [(i, i ^ d) for i in range(line)])  90.7 us
    ppermute x24, starting transfers between devices, exchange(): lax.ppermute(pieces[d], 'path', [(i, i ^ d) for i in range(columns)])  28.5 us
    ppermute x24, waiting for transfers between devices, exchange(): lax.ppermute(pieces[d], 'path', [(i, i ^ d) for i in range(columns)])  25.5 us
    ppermute x18, starting transfers between devices, to_place(): return lax.ppermute(value, 'expert', [(i, i ^ d) for i in range(line)])  23.4 us
    pallas_call x2, Pallas kernels, by_rows(): pl.pallas_call(functools.partial(kernel, half), grid=(total // block,), o...  22.3 us
    unnamed x77, local copies, waits for them, and re-layouts  14.8 us
    dot_general x3, matrix products, dot(): lax.dot_general(a, b, (((ca,), (cb,)), ((), ())), preferred_element_type=...  10.1 us
    pallas_call x4, Pallas kernels, join_rows(): pl.pallas_call(functools.partial(join_kernel, n, cap, columns, weighted),...  5.16 us
  transfers between devices with their start and end apart: 47, of which 19 were waited for; matrix products, arithmetic and copies ran while one was open for 8% of the time, Pallas kernels for 15%

commit v1 on v0

--- a/solution.py
+++ b/solution.py
@@ -14,6 +14,7 @@
 ANY = pl.BlockSpec(memory_space=pl.ANY)
 PARAMS = pltpu.CompilerParams(vmem_limit_bytes=48 << 20)
 SWAP = [(0, 1), (1, 0)]
+LARGE = pl.CostEstimate(flops=400_000_000_000, bytes_accessed=40 << 20, transcendentals=0)
 SMALL = pl.CostEstimate(flops=0, bytes_accessed=0, transcendentals=0)
 
 
@@ -32,22 +33,24 @@
     return lax.ppermute(value, "expert", [(i, i ^ d) for i in range(line)])
 
 
-def line_gather(block, line):
+def line_gather(block, line, early=None, first=None):
     got = {0: block}
     for bit in reversed(powers(line)):
         for d in list(got):
-            got[d | bit] = to_place(got[d], bit, line)
+            if d | bit in got:
+                continue
+            sent = early if early is not None and len(got) == 1 else got[d]
+            got[d | bit] = to_place(sent, bit, line)
+            if first is not None and d == 0 and bit == powers(line)[-1]:
+                got[bit], _, got[1] = together(got[bit], first, to_place(block, 1, line))
     return got
 
 
-def line_reduce(parts, line):
-    parts = dict(enumerate(parts))
-    for bit in powers(line):
-        for d in sorted((d for d in parts if d & bit), reverse=True):
-            moved = to_place(parts.pop(d), bit, line)
-            kept = parts[d ^ bit].astype(F32) + moved.astype(F32)
-            parts[d ^ bit] = kept.astype(moved.dtype)
-    return parts[0]
+def reduce_bit(parts, bit, line):
+    for d in sorted((d for d in parts if d & bit), reverse=True):
+        moved = to_place(parts.pop(d), bit, line)
+        kept = parts[d ^ bit].astype(F32) + moved.astype(F32)
+        parts[d ^ bit] = kept.astype(moved.dtype)
 
 
 def pick_kernel(n, cap, columns, scaled, *refs):
@@ -71,18 +74,18 @@
             pieces[d][j * cap : (j + 1) * cap, :] = rows[d * cap : (d + 1) * cap, :]
 
 
-def pick_rows(slot, weight, blocks, cap, columns, scaled):
+def pick_rows(slot, weight, blocks, cap, columns, scaled, cost):
     rows, half = blocks[0].shape
     n = len(blocks)
-    return pl.pallas_call(
+    return list(pl.pallas_call(
         functools.partial(pick_kernel, n, cap, columns, scaled),
         out_shape=[jax.ShapeDtypeStruct((n * cap, half), BF)] * columns,
         in_specs=[VMEM] * (2 + n),
         out_specs=[VMEM] * columns,
         compiler_params=PARAMS,
-        cost_estimate=SMALL,
+        cost_estimate=cost,
         name="pick_scaled" if scaled else "pick",
-    )(slot, weight, *blocks)
+    )(slot, weight, *blocks))
 
 
 def stack_kernel(count, *refs):
@@ -113,7 +116,7 @@
     pieces, rest = refs[2 : 2 + columns], refs[2 + columns :]
     held = rest[-1]
     if weighted:
-        cots, parts, gates = rest[:n], rest[n : 2 * n], rest[2 * n]
+        cots, parts = rest[:n], rest[n : 2 * n]
     else:
         parts = rest[:n]
     slots = columns * cap
@@ -131,10 +134,16 @@
             )
             high = given.astype(BF)
             low = (given - high.astype(F32)).astype(BF)
-            parts[j][...] = (dot(high, rows, 0, 0) + dot(low, rows, 0, 0)).astype(BF)
+            parts[j][: high.shape[1], :] = (dot(high, rows, 0, 0) + dot(low, rows, 0, 0)).astype(BF)
             meet = dot(rows, cots[j][...], 1, 1)
+            width = meet.shape[1]
             for k, h in enumerate(hits):
-                gates[j, k : k + 1, :] = jnp.sum(jnp.where(h, meet, 0.0), axis=0, keepdims=True)
+                gate = jnp.sum(jnp.where(h, meet, 0.0), axis=0, keepdims=True)
+                gate_high = gate.astype(BF)
+                gate_low = (gate - gate_high.astype(F32)).astype(BF)
+                for half_at, value in ((0, gate_high), (top, gate_low)):
+                    at = (half_at + k) * width
+                    parts[j][width : width + 16, at : at + width] = jnp.broadcast_to(value, (16, width))
         else:
             pick = functools.reduce(jnp.add, [h.astype(F32) for h in hits]).astype(BF)
             parts[j][...] = dot(pick, rows, 0, 0).astype(BF)
@@ -144,9 +153,7 @@
     columns, half = len(pieces), pieces[0].shape[1]
     n, top, rows = slot.shape
     weighted = cots is not None
-    outs = [jax.ShapeDtypeStruct((rows, half), BF)] * n
-    if weighted:
-        outs.append(jax.ShapeDtypeStruct((n, top, rows), F32))
+    outs = [jax.ShapeDtypeStruct((rows + (16 if weighted else 0), half), BF)] * n
     ins = [slot, weight] + list(pieces) + (list(cots) if weighted else [])
     out = pl.pallas_call(
         functools.partial(join_kernel, n, cap, columns, weighted),
@@ -155,10 +162,10 @@
         out_specs=[VMEM] * len(outs),
         scratch_shapes=[pltpu.VMEM((columns * cap, half), BF)],
         compiler_params=PARAMS,
-        cost_estimate=SMALL,
+        cost_estimate=LARGE,
         name="join_weighted" if weighted else "join",
     )(*ins)
-    return (list(out[:n]), out[n]) if weighted else (list(out[:n]), None)
+    return list(out)
 
 
 def halves(head_ref, half):
@@ -217,7 +224,7 @@
         + [pl.BlockSpec(v.shape, lambda i: (0, 0)) for v in whole_in],
         out_specs=[cut(width) for width, _ in outs],
         compiler_params=PARAMS,
-        cost_estimate=SMALL,
+        cost_estimate=LARGE,
         name=name,
     )(head, *rows_in, *whole_in)
 
@@ -253,6 +260,9 @@
     top = routes.shape[1]
     groups = columns * line
     cap = max(2, 2 * tok_rows * top // groups)
+    def after(value, *others):
+        return together(value, *others)[0]
+
     flat = routes.reshape(-1)
     order = jnp.arange(flat.shape[0], dtype=jnp.int32)
     earlier = (flat[:, None] == flat[None, :]) & (order[:, None] < order[None, :])
@@ -260,31 +270,32 @@
     position = (flat * cap + rank).astype(F32).reshape(tok_rows, top)
     about = jnp.concatenate([position.T, combine_weights.T], axis=0)
 
+    def exchange(pieces):
+        return [pieces[0]] + [
+            lax.ppermute(pieces[d], "path", [(i, i ^ d) for i in range(columns)])
+            for d in range(columns - 1, 0, -1)
+        ][::-1]
+
+    near, far = slice(0, line - 1), slice(line - 1, line)
+
+    every = slice(0, line)
+
+    def pick_group(got, part, scaled, cost=SMALL):
+        blocks = [got[d] for d in range(line)[part]]
+        return pick_rows(slot[part], weight[part], blocks, cap, columns, scaled, cost)
+
+    first_bit = powers(line)[-1]
     info = jnp.stack([about] + [to_place(about, d, line) for d in range(1, line)], axis=0)
     where_to = info[:, :top].astype(jnp.int32)
     expert = where_to // cap
     slot = ((expert // line) ^ column) * cap + where_to % cap
     slot = jnp.where(expert % line == place, slot, -1)
     weight = info[:, top:]
-
-    def exchange(pieces):
-        return [pieces[0]] + [
-            lax.ppermute(pieces[d], "path", [(i, i ^ d) for i in range(columns)])
-            for d in range(columns - 1, 0, -1)
-        ][::-1]
-
-    near, far = slice(0, line - 1), slice(line - 1, line)
-
-    def fetch(got, scaled):
-        pieces = []
-        for part in (near, far):
-            blocks = [got[d] for d in range(line)[part]]
-            pieces += exchange(pick_rows(slot[part], weight[part], blocks, cap, columns, scaled))
-        return pieces
-
-    tok_in = line_gather(tokens, line)
-    cot_gated, _ = together(cotangent, tok_in[line - 1])
-    cot_in = line_gather(cot_gated, line)
+    tok_in = line_gather(tokens, line, first=info)
+
+    cot_far = after(cotangent, tok_in[first_bit])
+    cot_near = after(cotangent, tok_in[line - 1])
+    cot_in = line_gather(cot_near, line, cot_far)
 
     gate_cols, up_cols, down_rows = w_gate[0], w_up[0], w_down[0]
     head_arg = head.reshape(1).astype(jnp.int32)
@@ -299,8 +310,14 @@
             [jnp.where(first, mine, other), jnp.where(first, other, mine)], axis=1
         )
 
-    tok_mine = stack_rows(fetch(tok_in, False))
-    tok_other = swap(tok_mine)
+    tok_near = exchange(pick_group(tok_in, near, False))
+    tok_in[line - 1] = after(tok_in[line - 1], *tok_near[1:])
+    tok_far = exchange(pick_group(tok_in, far, False))
+    tok_far[-1] = after(tok_far[-1], cot_in[first_bit], cot_in[1])
+    tok_mine = stack_rows([p for pair in zip(tok_near, tok_far) for p in pair])
+    cot_in[0] = after(cot_in[0], tok_mine)
+    cot_near_rows = pick_group(cot_in, near, True)
+    tok_other = after(swap(tok_mine), cot_near_rows[0])
     pre_gate, pre_up, activation, out_kept, out_sent = by_rows(
         ahead_kernel,
         head_arg,
@@ -309,16 +326,19 @@
         [(hidden, F32), (hidden, F32), (hidden, BF), (half, BF), (half, BF)],
         "ahead",
     )
-    sizes = [cap * (line - 1)] * columns + [cap] * columns
-
-    def send_home(kept, sent):
-        pieces = deal_rows(kept, swap(sent), sizes)
-        far_rows = exchange(pieces[columns:])
-        return exchange(pieces[:columns]), far_rows
-
-    out_near, out_far = send_home(out_kept, out_sent)
-    cot_mine = stack_rows(fetch(cot_in, True))
-    cot_other = swap(cot_mine)
+    cot_near_in = exchange(cot_near_rows)
+    cot_in[line - 1] = after(cot_in[line - 1], out_sent, *cot_near_in[1:])
+    cot_far_rows = pick_group(cot_in, far, True, LARGE)
+    out_came = after(swap(out_sent), cot_far_rows[0])
+    out_pieces = deal_rows(out_kept, out_came, [cap * (line - 1), cap] * columns)
+    cot_far_in = exchange(cot_far_rows)
+    out_far = exchange(out_pieces[1::2])
+    cot_mine = stack_rows([p for pair in zip(cot_near_in, cot_far_in) for p in pair])
+    cots = [cot_in[d] for d in range(line)]
+    out_far[-1] = after(out_far[-1], cot_mine)
+    out_parts_far = join_rows(slot[far], weight[far], out_far, cap, cots[far])
+    out_near = exchange(list(together(*out_pieces[::2], cot_mine)[:-1]))
+    cot_other = after(swap(cot_mine), out_parts_far[0])
     d_pre_gate, d_pre_up, back_kept, back_sent = by_rows(
         back_kernel,
         head_arg,
@@ -327,29 +347,46 @@
         [(hidden, BF), (hidden, BF), (half, BF), (half, BF)],
         "back",
     )
-    back_near, back_far = send_home(back_kept, back_sent)
-
-    d_pre_gate, d_pre_up, activation, _ = together(d_pre_gate, d_pre_up, activation, back_far[0])
-    inbound, grad_in = full(tok_mine, tok_other), full(cot_mine, cot_other)
+    out_near[-1] = after(out_near[-1], back_sent)
+    out_parts = join_rows(slot[near], weight[near], out_near, cap, cots[near]) + out_parts_far
+    back_came = after(swap(back_sent), out_parts[0])
+    first, last = slice(0, line - 2), slice(line - 2, line)
+    back_pieces = deal_rows(back_kept, back_came, [cap * (line - 2), cap * 2] * columns)
+    back_last = exchange(back_pieces[1::2])
+    out_parts[0] = after(out_parts[0], *back_pieces)
+    out_sums = dict(enumerate(out_parts))
+    reduce_bit(out_sums, 1, line)
+    back_last[-1] = after(back_last[-1], *out_sums.values())
+    back_parts_last = join_rows(slot[last], weight[last], back_last, cap)
+    back_first = exchange(
+        [back_pieces[0]] + list(together(*back_pieces[2::2], *back_last[1:])[: columns - 1])
+    )
+    moved = to_place(back_parts_last[1], 1, line)
+
+    d_pre_gate, d_pre_up, tok_mine, tok_other, _ = together(
+        d_pre_gate, d_pre_up, tok_mine, tok_other, back_parts_last[0]
+    )
+    inbound = full(tok_mine, tok_other)
     grad_gate = dot(inbound, d_pre_gate, 0, 0).astype(BF)
     grad_up = dot(inbound, d_pre_up, 0, 0).astype(BF)
-    grad_down = dot(activation, grad_in, 0, 0).astype(BF)
-
-    def settle(near_rows, far_rows, cots):
-        parts_far, gates_far = join_rows(
-            slot[far], weight[far], far_rows, cap, None if cots is None else cots[far]
-        )
-        parts, gates_near = join_rows(
-            slot[near], weight[near], near_rows, cap, None if cots is None else cots[near]
-        )
-        total = line_reduce(parts + parts_far, line)
-        if cots is None:
-            return total, None
-        gates = [gates_near[d] for d in range(line - 1)] + [gates_far[0]]
-        return total, line_reduce(gates, line)
-
-    layer_out, local_gates = settle(out_near, out_far, [cot_in[d] for d in range(line)])
-    d_tokens, _ = settle(back_near, back_far, None)
+
+    moved = after(moved, grad_gate, grad_up)
+    back_pair = (back_parts_last[0].astype(F32) + moved.astype(F32)).astype(BF)
+    activation, cot_mine, cot_other, _ = together(activation, cot_mine, cot_other, back_pair)
+    grad_down = dot(activation, full(cot_mine, cot_other), 0, 0).astype(BF)
+
+    out_sums[0] = after(out_sums[0], back_pair)
+    for bit in powers(line)[1:]:
+        reduce_bit(out_sums, bit, line)
+    out_total = out_sums[0]
+    back_first[-1] = after(back_first[-1], back_pair, out_total)
+    back_sums = dict(enumerate(join_rows(slot[first], weight[first], back_first, cap) + [back_pair]))
+    for bit in powers(line):
+        reduce_bit(back_sums, bit, line)
+    d_tokens = back_sums[0]
+    layer_out = out_total[:tok_rows]
+    gate_terms = out_total[tok_rows, : 2 * top * tok_rows].astype(F32).reshape(2, top, tok_rows)
+    local_gates = gate_terms[0] + gate_terms[1]
     d_gates = (local_gates + swap(local_gates)).T
     return (layer_out, d_tokens, d_gates, grad_gate[None], grad_up[None], grad_down[None])
 

time: 245 us -> 207 us (0.84)
  waiting for transfers between devices: 119 us -> 70 us
  Pallas kernels: 37.6 us -> 44.1 us
  other arithmetic: 9.15 us -> 14.8 us
  local copies, waits for them, and re-layouts: 15.1 us -> 10.8 us
    ppermute x18 -> x15, waiting for transfers between devices: 90.7 us -> 63.4 us  [to_place(): return lax.ppermute(value, 'expert', [(i, i ^ d) for i in range(line)])]
    ppermute x24, waiting for transfers between devices: 25.5 us -> 6.6 us  [exchange(): lax.ppermute(pieces[d], 'path', [(i, i ^ d) for i in range(columns)])]
    unnamed x77 -> x65, local copies, waits for them, and re-layouts: 14.8 us -> 9.05 us
    convert_element_type x4 -> x6, other arithmetic: 3.55 us -> 7.44 us  [the longest x4 6.44 us: reduce_bit(): parts[d ^ bit] = kept.astype(moved.dtype)]
    ppermute x18 -> x15, starting transfers between devices: 23.4 us -> 26.8 us  [to_place(): return lax.ppermute(value, 'expert', [(i, i ^ d) for i in range(line)])]
    ppermute x5, waiting for transfers between devices: 2.58 us -> 0.01 us  [swap(): return lax.ppermute(value, 'head', SWAP)]
    pallas_call x4, Pallas kernels: 5.16 us -> 7.7 us  [join_rows(): pl.pallas_call(functools.partial(join_kernel, n, cap, columns, weighted),...]
  transfers between devices with their start and end apart: 47 -> 44, of which waited for: 19 -> 13; matrix products, arithmetic and copies ran while one was open for 8% -> 12% of each run, Pallas kernels for 15% -> 21%
where the time goes in v1:
time: 207 us; the launch traced here: 206 us
  waiting for transfers between devices  70 us (34%)
  starting transfers between devices  55 us (27%)
  Pallas kernels  44.1 us (21%)
  other arithmetic  14.8 us (7%)
  local copies, waits for them, and re-layouts  10.8 us (5%)
  matrix products  10.1 us (5%)
    ppermute x15, waiting for transfers between devices, to_place(): return lax.ppermute(value, 'expert', [(i, i ^ d) for i in range(line)])  63.4 us
    ppermute x24, starting transfers between devices, exchange(): lax.ppermute(pieces[d], 'path', [(i, i ^ d) for i in range(columns)])  28.1 us
    ppermute x15, starting transfers between devices, to_place(): return lax.ppermute(value, 'expert', [(i, i ^ d) for i in range(line)])  26.8 us
    pallas_call x2, Pallas kernels, by_rows(): pl.pallas_call(functools.partial(kernel, half), grid=(total // block,), o...  22.2 us
    dot_general x3, matrix products, dot(): lax.dot_general(a, b, (((ca,), (cb,)), ((), ())), preferred_element_type=...  10.1 us
    unnamed x65, local copies, waits for them, and re-layouts  9.05 us
    pallas_call x4, Pallas kernels, join_rows(): pl.pallas_call(functools.partial(join_kernel, n, cap, columns, weighted),...  7.7 us
    ppermute x24, waiting for transfers between devices, exchange(): lax.ppermute(pieces[d], 'path', [(i, i ^ d) for i in range(columns)])  6.6 us
  transfers between devices with their start and end apart: 44, of which 13 were waited for; matrix products, arithmetic and copies ran while one was open for 12% of the time, Pallas kernels for 21%

profile of v1, /device:TPU:0, one launch (start us, length us, event | category | flops | bytes accessed | tf_op | source)
XLA Modules:
  0.0 205.9 jit_solution(13962463374722406973)
XLA Ops:
  0.6 4.1 %collective-permute-start.3 = (bf16[256,1024]{1,0:T(8,128)(2,1)}, bf16[256,1024]{1,0:T(8,128)(2,1)S(1)}, u32[]{:S(2)}, u32[]{:S(2)}) collective-permute-start(bf16[256,1024]{1,0:T(8,128)(2,1)} %refs_2_.1), channel_id=1, source_target_pairs={{0,2},{1,3},{2,0},{3,1},{4,6},{5,7},{6,4},{7,5},{8,10},{9,11},{10,... | collective-permute-start | bytes 1572872 | tf_op jit(solution)/shard_map/ppermute | solution.py:33
  4.7 1.6 collective-permute-start.4
  9.7 3.9 %collective-permute-start.2 = (f32[4,256]{1,0:T(4,128)S(1)}, f32[4,256]{1,0:T(4,128)S(1)}, u32[]{:S(2)}, u32[]{:S(2)}) collective-permute-start(f32[4,256]{1,0:T(4,128)S(1)} %get-tuple-element.175), channel_id=1, source_target_pairs={{0,3},{1,2},{2,1},{3,0},{4,7},{5,6},{6,5},{7,4},{8,11},{9,10},{10,... | collective-permute-start | bytes 12296 | tf_op jit(solution)/shard_map/ppermute | solution.py:33
  13.5 14.9 %collective-permute-done.1 = f32[4,256]{1,0:T(4,128)S(1)} collective-permute-done((f32[4,256]{1,0:T(4,128)S(1)}, f32[4,256]{1,0:T(4,128)S(1)}, u32[]{:S(2)}, u32[]{:S(2)}) %collective-permute-start.1) | collective-permute-done | bytes 4128 | tf_op jit(solution)/shard_map/ppermute | solution.py:33
  32.0 1.6 collective-permute-start.6
  33.5 1.5 collective-permute-start.7
  35.5 2.4 %collective-permute-start.12 = (bf16[256,1024]{1,0:T(8,128)(2,1)S(1)}, bf16[256,1024]{1,0:T(8,128)(2,1)}, u32[]{:S(2)}, u32[]{:S(2)}) collective-permute-start(bf16[256,1024]{1,0:T(8,128)(2,1)S(1)} %copy-done.5), channel_id=1, source_target_pairs={{0,2},{1,3},{2,0},{3,1},{4,6},{5,7},{6,4},{7,5},{8,10},{9,11},{10,... | collective-permute-start | bytes 1572872 | tf_op jit(solution)/shard_map/ppermute | solution.py:33
  38.0 11.0 %collective-permute-done.5.refs_2_ = bf16[256,1024]{1,0:T(8,128)(2,1)S(1)} collective-permute-done((bf16[256,1024]{1,0:T(8,128)(2,1)S(1)}, bf16[256,1024]{1,0:T(8,128)(2,1)S(1)}, u32[]{:S(2)}, u32[]{:S(2)}) %collective-permute-start.5) | collective-permute-done | bytes 524320 | tf_op jit(solution)/shard_map/ppermute | solution.py:33
  49.1 2.4 %collective-permute-done.7.refs_4_ = bf16[192,1024]{1,0:T(8,128)(2,1)S(1)} collective-permute-done((bf16[192,1024]{1,0:T(8,128)(2,1)S(1)}, bf16[192,1024]{1,0:T(8,128)(2,1)S(1)}, u32[]{:S(2)}, u32[]{:S(2)}) %collective-permute-start.7) | collective-permute-done | bytes 393248 | tf_op jit(solution)/shard_map/ppermute | solution.py:275
  51.8 1.6 collective-permute-start.11
  53.3 1.5 collective-permute-start.9
  55.3 5.0 %collective-permute-done.12.refs_4_.refs_8_ = bf16[256,1024]{1,0:T(8,128)(2,1)} collective-permute-done((bf16[256,1024]{1,0:T(8,128)(2,1)S(1)}, bf16[256,1024]{1,0:T(8,128)(2,1)}, u32[]{:S(2)}, u32[]{:S(2)}) %collective-permute-start.12) | collective-permute-done | bytes 524320 | tf_op jit(solution)/shard_map/ppermute | solution.py:33
  60.3 4.8 %collective-permute-done.13.refs_3_.refs_7_ = bf16[256,1024]{1,0:T(8,128)(2,1)S(1)} collective-permute-done((bf16[256,1024]{1,0:T(8,128)(2,1)S(1)}, bf16[256,1024]{1,0:T(8,128)(2,1)S(1)}, u32[]{:S(2)}, u32[]{:S(2)}) %collective-permute-start.13) | collective-permute-done | bytes 524320 | tf_op jit(solution)/shard_map/ppermute | solution.py:33
  65.9 3.0 %pick_scaled.2 = (bf16[192,1024]{1,0:T(8,128)(2,1)S(1)}, bf16[192,1024]{1,0:T(8,128)(2,1)}, bf16[192,1024]{1,0:T(8,128)(2,1)}, bf16[192,1024]{1,0:T(8,128)(2,1)}) custom-call(s32[3,2,256]{2,1,0:T(2,128)S(1)} %slice.76.refs_0_, f32[3,2,256]{2,1,0:T(2,128)S(1)} %pad_maximum_fusion.4.refs_1_, bf16[256,1024]{1,0:T(8,128)(2,1)S(1)} %copy-done.5, ...), custom_call_target="tpu_custom_call" | custom-call | tf_op jit(solution)/shard_map/pick_scaled/pallas_call | solution.py:80
  68.8 1.5 collective-permute-start.17
  70.3 1.5 collective-permute-start.18
  73.8 10.7 %ahead.1 = (f32[1024,384]{1,0:T(8,128)S(1)}, f32[1024,384]{1,0:T(8,128)S(1)}, bf16[1024,384]{1,0:T(8,128)(2,1)S(1)}, bf16[1024,1024]{1,0:T(8,128)(2,1)}, bf16[1024,1024]{1,0:T(8,128)(2,1)}) custom-call(s32[1]{0:T(128)} %bitcast.6.head_ref, bf16[1024,1024]{1,0:T(8,128)(2,1)} %copy-done, bf16[1024,1024]{1,0:T(8,128)(2,1)} %collective-permute-done.14.other_ref, ...), custom_call_target="tpu_custom_call" | custom-call | flops 399999991808 | bytes 41943040 | tf_op jit(solution)/shard_map/ahead/pallas_call | solution.py:218
  87.6 2.3 %collective-permute-done.18.refs_4_ = bf16[192,1024]{1,0:T(8,128)(2,1)} collective-permute-done((bf16[192,1024]{1,0:T(8,128)(2,1)}, bf16[192,1024]{1,0:T(8,128)(2,1)}, u32[]{:S(2)}, u32[]{:S(2)}) %collective-permute-start.18) | collective-permute-done | bytes 393248 | tf_op jit(solution)/shard_map/ppermute | solution.py:275
  89.9 2.2 %pick_scaled.3 = (bf16[64,1024]{1,0:T(8,128)(2,1)S(1)}, bf16[64,1024]{1,0:T(8,128)(2,1)S(1)}, bf16[64,1024]{1,0:T(8,128)(2,1)}, bf16[64,1024]{1,0:T(8,128)(2,1)S(1)}) custom-call(s32[1,2,256]{2,1,0:T(2,128)S(1)} %copy-done.10, f32[1,2,256]{2,1,0:T(2,128)S(1)} %copy-done.7, bf16[256,1024]{1,0:T(8,128)(2,1)} %collective-permute-done.16.refs_2_.refs_6_), custom_call_target="tpu_custom_call" | custom-call | flops 399999991808 | bytes 41943040 | tf_op jit(solution)/shard_map/pick_scaled/pallas_call | solution.py:80
  94.1 1.4 collective-permute-start.22
  95.5 2.7 %deal.2 = (bf16[192,1024]{1,0:T(8,128)(2,1)S(1)}, bf16[64,1024]{1,0:T(8,128)(2,1)S(1)}, bf16[192,1024]{1,0:T(8,128)(2,1)}, bf16[64,1024]{1,0:T(8,128)(2,1)S(1)},...) custom-call(bf16[1024,1024]{1,0:T(8,128)(2,1)S(1)} %copy-done.3, ...), custom_call_target="tpu_custom_call" | custom-call | tf_op jit(solution)/shard_map/deal/pallas_call | solution.py:241
  98.3 1.5 collective-permute-start.29
  99.8 1.5 collective-permute-start.27
  102.2 2.7 %stack.32.mine_ref = bf16[1024,1024]{1,0:T(8,128)(2,1)} custom-call(bf16[192,1024]{1,0:T(8,128)(2,1)S(1)} %get-tuple-element.102.refs_0_, bf16[64,1024]{1,0:T(8,128)(2,1)S(1)} %get-tuple-element.110.refs_1_, bf16[192,1024]{1,0:T(8,128)(2,1)} %collective-permute-done.17.refs_2_, bf16[64,1024]{1,0:T(8,128)(2,1)S(1)} %collective-permute-done.20.refs_3_, ...), custom_call_target="tpu_custom_call" | custom-call | tf_op jit(solution)/shard_map/stack/pallas_call | solution.py:103
  105.8 1.5 collective-permute-start.24
  108.5 2.7 %join_weighted.2 = bf16[272,1024]{1,0:T(8,128)(2,1)} custom-call(s32[1,2,256]{2,1,0:T(2,128)S(1)} %copy-done.11, f32[1,2,256]{2,1,0:T(2,128)S(1)} %copy-done.8, bf16[64,1024]{1,0:T(8,128)(2,1)S(1)} %get-tuple-element.123.refs_2_, bf16[64,1024]{1,0:T(8,128)(2,1)S(1)} %collective-permute-done.27.refs_3_, bf16[64,1024]{1,0:T(8,128)(2,1)S(1)} %collective-permute-done.28.refs_4_, ...), custom_call_target="tpu_custom_call" | custom-call | flops 399999991808 | bytes 41943040 | tf_op jit(solution)/shard_map/join_weighted/pallas_call | solution.py:158
  111.2 1.8 collective-permute-start.35
  113.0 11.6 %back.1 = (bf16[1024,384]{1,0:T(8,128)(2,1)S(1)}, bf16[1024,384]{1,0:T(8,128)(2,1)S(1)}, bf16[1024,1024]{1,0:T(8,128)(2,1)}, bf16[1024,1024]{1,0:T(8,128)(2,1)}) custom-call(s32[1]{0:T(128)} %bitcast.6.head_ref, bf16[1024,1024]{1,0:T(8,128)(2,1)} %stack.32.mine_ref, bf16[1024,1024]{1,0:T(8,128)(2,1)} %collective-permute-done.26.other_ref, ...), custom_call_target="tpu_custom_call" | custom-call | flops 399999991808 | bytes 41943040 | tf_op jit(solution)/shard_map/back/pallas_call | solution.py:218
  124.6 1.5 collective-permute-done.25.refs_5_
  126.1 3.0 %join_weighted.3 = (bf16[272,1024]{1,0:T(8,128)(2,1)S(1)}, bf16[272,1024]{1,0:T(8,128)(2,1)S(1)}, bf16[272,1024]{1,0:T(8,128)(2,1)S(1)}) custom-call(s32[3,2,256]{2,1,0:T(2,128)S(1)} %slice.76.refs_0_, f32[3,2,256]{2,1,0:T(2,128)S(1)} %pad_maximum_fusion.4.refs_1_, bf16[192,1024]{1,0:T(8,128)(2,1)S(1)} %get-tuple-element.119.refs_2_, ...), custom_call_target="tpu_custom_call" | custom-call | flops 399999991808 | bytes 41943040 | tf_op jit(solution)/shard_map/join_weighted/pallas_call | solution.py:158
  129.1 1.8 collective-permute-start.31
  131.0 2.1 %add_convert_fusion.1 = bf16[272,1024]{1,0:T(8,128)(2,1)} fusion(bf16[272,1024]{1,0:T(8,128)(2,1)} %collective-permute-done.35, bf16[272,1024]{1,0:T(8,128)(2,1)S(1)} %get-tuple-element.146), kind=kLoop, calls=%fused_computation.14 | loop fusion | flops 1114112 | bytes 1671168 | tf_op jit(solution)/shard_map/convert_element_type | solution.py:53
  133.1 3.4 %collective-permute-start.37 = (bf16[272,1024]{1,0:T(8,128)(2,1)}, bf16[272,1024]{1,0:T(8,128)(2,1)}, u32[]{:S(2)}, u32[]{:S(2)}) collective-permute-start(bf16[272,1024]{1,0:T(8,128)(2,1)} %add_convert_fusion.1), channel_id=1, source_target_pairs={{0,2},{1,3},{2,0},{3,1},{4,6},{5,7},{6,4},{7,5},{8,10},{9,11},{10,... | collective-permute-start | bytes 1671176 | tf_op jit(solution)/shard_map/ppermute | solution.py:33
  136.5 1.6 copy-done.2
  138.1 2.6 %deal.3 = (bf16[128,1024]{1,0:T(8,128)(2,1)S(1)}, bf16[128,1024]{1,0:T(8,128)(2,1)S(1)}, bf16[128,1024]{1,0:T(8,128)(2,1)}, bf16[128,1024]{1,0:T(8,128)(2,1)S(1)...) custom-call(bf16[1024,1024]{1,0:T(8,128)(2,1)S(1)} %copy-done.2, ...), custom_call_target="tpu_custom_call" | custom-call | tf_op jit(solution)/shard_map/deal/pallas_call | solution.py:241
  144.1 10.1 %collective-permute-done.31 = bf16[272,1024]{1,0:T(8,128)(2,1)S(1)} collective-permute-done((bf16[272,1024]{1,0:T(8,128)(2,1)S(1)}, bf16[272,1024]{1,0:T(8,128)(2,1)S(1)}, u32[]{:S(2)}, u32[]{:S(2)}) %collective-permute-start.31) | collective-permute-done | bytes 557088 | tf_op jit(solution)/shard_map/ppermute | solution.py:33
  157.3 1.5 collective-permute-start.40
  160.4 1.9 broadcast_select_fusion.3
  162.3 3.5 %convolution_convert_fusion = bf16[2048,384]{1,0:T(8,128)(2,1)} fusion(bf16[1024,384]{1,0:T(8,128)(2,1)S(1)} %get-tuple-element.155, bf16[1024,1024]{1,0:T(8,128)(2,1)S(1)} %get-tuple-element.171, bf16[1024,1024]{1,0:T(8,128)(2,1)S(1)} %get-tuple-element.170), kind=kOutput, calls=%fused_computation.6 | convolution fusion | flops 1619787776 | bytes 6553600 | tf_op jit(solution)/shard_map/dot_general | solution.py:22
  165.8 3.5 %convolution_convert_fusion.1 = bf16[2048,384]{1,0:T(8,128)(2,1)} fusion(bf16[1024,384]{1,0:T(8,128)(2,1)S(1)} %get-tuple-element.154, bf16[1024,1024]{1,0:T(8,128)(2,1)S(1)} %get-tuple-element.171, bf16[1024,1024]{1,0:T(8,128)(2,1)S(1)} %get-tuple-element.170), kind=kOutput, calls=%fused_computation.7 | convolution fusion | flops 1619787776 | bytes 6553600 | tf_op jit(solution)/shard_map/dot_general | solution.py:22
  169.4 2.3 %collective-permute-done.36 = bf16[256,1024]{1,0:T(8,128)(2,1)S(1)} collective-permute-done((bf16[256,1024]{1,0:T(8,128)(2,1)S(1)}, bf16[256,1024]{1,0:T(8,128)(2,1)S(1)}, u32[]{:S(2)}, u32[]{:S(2)}) %collective-permute-start.36) | collective-permute-done | bytes 524320 | tf_op jit(solution)/shard_map/ppermute | solution.py:33
  172.6 2.5 %collective-permute-start.42 = (bf16[256,1024]{1,0:T(8,128)(2,1)}, bf16[256,1024]{1,0:T(8,128)(2,1)}, u32[]{:S(2)}, u32[]{:S(2)}) collective-permute-start(bf16[256,1024]{1,0:T(8,128)(2,1)} %add_convert_fusion.5), channel_id=1, source_target_pairs={{0,2},{1,3},{2,0},{3,1},{4,6},{5,7},{6,4},{7,5},{8,10},{9,11},{10,... | collective-permute-start | bytes 1572872 | tf_op jit(solution)/shard_map/ppermute | solution.py:33
  177.8 1.6 join.3
  179.5 2.6 %collective-permute-start.41 = (bf16[256,1024]{1,0:T(8,128)(2,1)S(1)}, bf16[256,1024]{1,0:T(8,128)(2,1)S(1)}, u32[]{:S(2)}, u32[]{:S(2)}) collective-permute-start(bf16[256,1024]{1,0:T(8,128)(2,1)S(1)} %get-tuple-element.163), channel_id=1, source_target_pairs={{0,1},{1,0},{2,3},{3,2},{4,5},{5,4},{6,7},{7,6},{8,9},{9,8},{10,11... | collective-permute-start | bytes 1572872 | tf_op jit(solution)/shard_map/ppermute | solution.py:33
  182.0 2.5 %broadcast_select_fusion.1 = (bf16[1024,1024]{1,0:T(8,128)(2,1)S(1)}, bf16[1024,1024]{1,0:T(8,128)(2,1)S(1)}) fusion(bf16[1024,1024]{1,0:T(8,128)(2,1)} %stack.32.mine_ref, bf16[1024,1024]{1,0:T(8,128)(2,1)} %collective-permute-done.26.other_ref, pred[]{:T(512)S(6)} %eq.34), kind=kLoop, calls=%fused_computation.10 | loop fusion | flops 2097152 | bytes 8388609 | tf_op jit(solution)/shard_map/jit(_where)/select_n | solution.py:310
  184.5 3.0 %fusion.7 = bf16[1,384,2048]{2,1,0:T(8,128)(2,1)} fusion(bf16[1024,384]{1,0:T(8,128)(2,1)S(1)} %copy-done.14, bf16[1024,1024]{1,0:T(8,128)(2,1)S(1)} %get-tuple-element.169, bf16[1024,1024]{1,0:T(8,128)(2,1)S(1)} %get-tuple-element.168), kind=kOutput, calls=%fused_computation.8 | convolution fusion | flops 1619787776 | bytes 6553600 | tf_op jit(solution)/shard_map/dot_general | solution.py:22
  189.6 14.2 %collective-permute-done.41 = bf16[256,1024]{1,0:T(8,128)(2,1)S(1)} collective-permute-done((bf16[256,1024]{1,0:T(8,128)(2,1)S(1)}, bf16[256,1024]{1,0:T(8,128)(2,1)S(1)}, u32[]{:S(2)}, u32[]{:S(2)}) %collective-permute-start.41) | collective-permute-done | bytes 524320 | tf_op jit(solution)/shard_map/ppermute | solution.py:33
  203.8 2.1 %add_convert_fusion.3 = bf16[256,1024]{1,0:T(8,128)(2,1)} fusion(bf16[256,1024]{1,0:T(8,128)(2,1)} %collective-permute-done.42, bf16[256,1024]{1,0:T(8,128)(2,1)S(1)} %collective-permute-done.41, bf16[256,1024]{1,0:T(8,128)(2,1)S(1)} %get-tuple-element.162), kind=kLoop, calls=%fused_computation.16 | loop fusion | flops 2097152 | bytes 2097152 | tf_op jit(solution)/shard_map/convert_element_type | solution.py:53
  (149 shorter events, 33.0 us)
Async XLA Ops:
  0.6 34.9 %copy-start.5 = (bf16[256,1024]{1,0:T(8,128)(2,1)S(1)}, bf16[256,1024]{1,0:T(8,128)(2,1)}, u32[]{:S(2)}) copy-start(bf16[256,1024]{1,0:T(8,128)(2,1)} %refs_6_) | copy-start | bytes 1572868
  0.6 28.9 %collective-permute-start.3 = (bf16[256,1024]{1,0:T(8,128)(2,1)}, bf16[256,1024]{1,0:T(8,128)(2,1)S(1)}, u32[]{:S(2)}, u32[]{:S(2)}) collective-permute-start(bf16[256,1024]{1,0:T(8,128)(2,1)} %refs_2_.1), channel_id=1, source_target_pairs={{0,2},{1,3},{2,0},{3,1},{4,6},{5,7},{6,4},{7,5},{8,10},{9,11},{10,... | collective-permute-start | bytes 1572872 | tf_op jit(solution)/shard_map/ppermute | solution.py:33
  4.7 24.8 %collective-permute-start.4 = (bf16[256,1024]{1,0:T(8,128)(2,1)}, bf16[256,1024]{1,0:T(8,128)(2,1)S(1)}, u32[]{:S(2)}, u32[]{:S(2)}) collective-permute-start(bf16[256,1024]{1,0:T(8,128)(2,1)} %refs_2_.1), channel_id=1, source_target_pairs={{0,1},{1,0},{2,3},{3,2},{4,5},{5,4},{6,7},{7,6},{8,9},{9,8},{10,11... | collective-permute-start | bytes 1572872 | tf_op jit(solution)/shard_map/ppermute | solution.py:33
  9.1 21.2 %copy-start.24 = (f32[1,4,256]{2,1,0:T(4,128)}, f32[1,4,256]{2,1,0:T(4,128)S(1)}, u32[]{:S(2)}) copy-start(f32[1,4,256]{2,1,0:T(4,128)S(1)} %get-tuple-element.174) | copy-start | bytes 12292
  9.1 19.3 %collective-permute-start.1 = (f32[4,256]{1,0:T(4,128)S(1)}, f32[4,256]{1,0:T(4,128)S(1)}, u32[]{:S(2)}, u32[]{:S(2)}) collective-permute-start(f32[4,256]{1,0:T(4,128)S(1)} %get-tuple-element.175), channel_id=1, source_target_pairs={{0,2},{1,3},{2,0},{3,1},{4,6},{5,7},{6,4},{7,5},{8,10},{9,11},{10,... | collective-permute-start | bytes 12296 | tf_op jit(solution)/shard_map/ppermute | solution.py:33
  9.5 19.2 %collective-permute-start = (f32[4,256]{1,0:T(4,128)S(1)}, f32[4,256]{1,0:T(4,128)S(1)}, u32[]{:S(2)}, u32[]{:S(2)}) collective-permute-start(f32[4,256]{1,0:T(4,128)S(1)} %get-tuple-element.175), channel_id=1, source_target_pairs={{0,1},{1,0},{2,3},{3,2},{4,5},{5,4},{6,7},{7,6},{8,9},{9,8},{10,11... | collective-permute-start | bytes 12296 | tf_op jit(solution)/shard_map/ppermute | solution.py:33
  9.7 19.8 %collective-permute-start.2 = (f32[4,256]{1,0:T(4,128)S(1)}, f32[4,256]{1,0:T(4,128)S(1)}, u32[]{:S(2)}, u32[]{:S(2)}) collective-permute-start(f32[4,256]{1,0:T(4,128)S(1)} %get-tuple-element.175), channel_id=1, source_target_pairs={{0,3},{1,2},{2,1},{3,0},{4,7},{5,6},{6,5},{7,4},{8,11},{9,10},{10,... | collective-permute-start | bytes 12296 | tf_op jit(solution)/shard_map/ppermute | solution.py:33
  29.5 35.7 %copy-start.30 = (f32[4,256]{1,0:T(4,128)}, f32[4,256]{1,0:T(4,128)S(1)}, u32[]{:S(2)}) copy-start(f32[4,256]{1,0:T(4,128)S(1)} %collective-permute-done.2) | copy-start | bytes 12292
  29.5 19.5 %collective-permute-start.5 = (bf16[256,1024]{1,0:T(8,128)(2,1)S(1)}, bf16[256,1024]{1,0:T(8,128)(2,1)S(1)}, u32[]{:S(2)}, u32[]{:S(2)}) collective-permute-start(bf16[256,1024]{1,0:T(8,128)(2,1)S(1)} %collective-permute-done.3.refs_4_), channel_id=1, source_target_pairs={{0,1},{1,0},{2,3},{3,2},{4,5},{5,4},{6,7},{7,6},{8,9},{9,8},{10,11... | collective-permute-start | bytes 1572872 | tf_op jit(solution)/shard_map/ppermute | solution.py:33
  30.3 35.0 %copy-start.22 = (s32[4,2,256]{2,1,0:T(2,128)}, s32[4,2,256]{2,1,0:T(2,128)S(1)}, u32[]{:S(2)}) copy-start(s32[4,2,256]{2,1,0:T(2,128)S(1)} %compare_select_fusion) | copy-start | bytes 24580
  32.0 17.1 %collective-permute-start.6 = (bf16[192,1024]{1,0:T(8,128)(2,1)S(1)}, bf16[192,1024]{1,0:T(8,128)(2,1)S(1)}, u32[]{:S(2)}, u32[]{:S(2)}) collective-permute-start(bf16[192,1024]{1,0:T(8,128)(2,1)S(1)} %get-tuple-element.90), channel_id=1, source_target_pairs={{0,8},{8,0},{16,24},{24,16},{1,9},{9,1},{17,25},{25,17},{2,10},{10... | collective-permute-start | bytes 1179656 | tf_op jit(solution)/shard_map/ppermute | solution.py:275
  33.5 17.9 %collective-permute-start.7 = (bf16[192,1024]{1,0:T(8,128)(2,1)S(1)}, bf16[192,1024]{1,0:T(8,128)(2,1)S(1)}, u32[]{:S(2)}, u32[]{:S(2)}) collective-permute-start(bf16[192,1024]{1,0:T(8,128)(2,1)S(1)} %get-tuple-element.91), channel_id=1, source_target_pairs={{0,16},{8,24},{16,0},{24,8},{1,17},{9,25},{17,1},{25,9},{2,18},{10... | collective-permute-start | bytes 1179656 | tf_op jit(solution)/shard_map/ppermute | solution.py:275
  35.1 16.4 %collective-permute-start.8 = (bf16[192,1024]{1,0:T(8,128)(2,1)S(1)}, bf16[192,1024]{1,0:T(8,128)(2,1)S(1)}, u32[]{:S(2)}, u32[]{:S(2)}) collective-permute-start(bf16[192,1024]{1,0:T(8,128)(2,1)S(1)} %get-tuple-element.92), channel_id=1, source_target_pairs={{0,24},{8,16},{16,8},{24,0},{1,25},{9,17},{17,9},{25,1},{2,26},{10... | collective-permute-start | bytes 1179656 | tf_op jit(solution)/shard_map/ppermute | solution.py:275
  35.5 24.8 %collective-permute-start.12 = (bf16[256,1024]{1,0:T(8,128)(2,1)S(1)}, bf16[256,1024]{1,0:T(8,128)(2,1)}, u32[]{:S(2)}, u32[]{:S(2)}) collective-permute-start(bf16[256,1024]{1,0:T(8,128)(2,1)S(1)} %copy-done.5), channel_id=1, source_target_pairs={{0,2},{1,3},{2,0},{3,1},{4,6},{5,7},{6,4},{7,5},{8,10},{9,11},{10,... | collective-permute-start | bytes 1572872 | tf_op jit(solution)/shard_map/ppermute | solution.py:33
  49.0 16.1 %collective-permute-start.13 = (bf16[256,1024]{1,0:T(8,128)(2,1)S(1)}, bf16[256,1024]{1,0:T(8,128)(2,1)S(1)}, u32[]{:S(2)}, u32[]{:S(2)}) collective-permute-start(bf16[256,1024]{1,0:T(8,128)(2,1)S(1)} %copy-done.5), channel_id=1, source_target_pairs={{0,1},{1,0},{2,3},{3,2},{4,5},{5,4},{6,7},{7,6},{8,9},{9,8},{10,11... | collective-permute-start | bytes 1572872 | tf_op jit(solution)/shard_map/ppermute | solution.py:33
  51.8 8.6 %collective-permute-start.11 = (bf16[64,1024]{1,0:T(8,128)(2,1)S(1)}, bf16[64,1024]{1,0:T(8,128)(2,1)S(1)}, u32[]{:S(2)}, u32[]{:S(2)}) collective-permute-start(bf16[64,1024]{1,0:T(8,128)(2,1)S(1)} %get-tuple-element.97), channel_id=1, source_target_pairs={{0,24},{8,16},{16,8},{24,0},{1,25},{9,17},{17,9},{25,1},{2,26},{10... | collective-permute-start | bytes 393224 | tf_op jit(solution)/shard_map/ppermute | solution.py:275
  53.3 11.9 %collective-permute-start.9 = (bf16[64,1024]{1,0:T(8,128)(2,1)S(1)}, bf16[64,1024]{1,0:T(8,128)(2,1)S(1)}, u32[]{:S(2)}, u32[]{:S(2)}) collective-permute-start(bf16[64,1024]{1,0:T(8,128)(2,1)S(1)} %get-tuple-element.95), channel_id=1, source_target_pairs={{0,8},{8,0},{16,24},{24,16},{1,9},{9,1},{17,25},{25,17},{2,10},{10... | collective-permute-start | bytes 393224 | tf_op jit(solution)/shard_map/ppermute | solution.py:275
  54.8 10.4 %collective-permute-start.10 = (bf16[64,1024]{1,0:T(8,128)(2,1)S(1)}, bf16[64,1024]{1,0:T(8,128)(2,1)S(1)}, u32[]{:S(2)}, u32[]{:S(2)}) collective-permute-start(bf16[64,1024]{1,0:T(8,128)(2,1)S(1)} %get-tuple-element.96), channel_id=1, source_target_pairs={{0,16},{8,24},{16,0},{24,8},{1,17},{9,25},{17,1},{25,9},{2,18},{10... | collective-permute-start | bytes 393224 | tf_op jit(solution)/shard_map/ppermute | solution.py:275
  65.3 7.0 %collective-permute-start.14 = (bf16[1024,1024]{1,0:T(8,128)(2,1)S(1)}, bf16[1024,1024]{1,0:T(8,128)(2,1)}, u32[]{:S(2)}, u32[]{:S(2)}) collective-permute-start(bf16[1024,1024]{1,0:T(8,128)(2,1)S(1)} %stack.31.mine_ref), channel_id=1, source_target_pairs={{0,4},{4,0},{1,5},{5,1},{2,6},{6,2},{3,7},{7,3},{8,12},{12,8},{9,1... | collective-permute-start | bytes 6291464 | tf_op jit(solution)/shard_map/ppermute | solution.py:305
  65.4 22.2 %collective-permute-start.16 = (bf16[256,1024]{1,0:T(8,128)(2,1)}, bf16[256,1024]{1,0:T(8,128)(2,1)}, u32[]{:S(2)}, u32[]{:S(2)}) collective-permute-start(bf16[256,1024]{1,0:T(8,128)(2,1)} %collective-permute-done.12.refs_4_.refs_8_), channel_id=1, source_target_pairs={{0,1},{1,0},{2,3},{3,2},{4,5},{5,4},{6,7},{7,6},{8,9},{9,8},{10,11... | collective-permute-start | bytes 1572872 | tf_op jit(solution)/shard_map/ppermute | solution.py:33
  68.8 18.7 %collective-permute-start.17 = (bf16[192,1024]{1,0:T(8,128)(2,1)}, bf16[192,1024]{1,0:T(8,128)(2,1)}, u32[]{:S(2)}, u32[]{:S(2)}) collective-permute-start(bf16[192,1024]{1,0:T(8,128)(2,1)} %get-tuple-element.106), channel_id=1, source_target_pairs={{0,8},{8,0},{16,24},{24,16},{1,9},{9,1},{17,25},{25,17},{2,10},{10... | collective-permute-start | bytes 1179656 | tf_op jit(solution)/shard_map/ppermute | solution.py:275
  70.3 19.5 %collective-permute-start.18 = (bf16[192,1024]{1,0:T(8,128)(2,1)}, bf16[192,1024]{1,0:T(8,128)(2,1)}, u32[]{:S(2)}, u32[]{:S(2)}) collective-permute-start(bf16[192,1024]{1,0:T(8,128)(2,1)} %get-tuple-element.107), channel_id=1, source_target_pairs={{0,16},{8,24},{16,0},{24,8},{1,17},{9,25},{17,1},{25,9},{2,18},{10... | collective-permute-start | bytes 1179656 | tf_op jit(solution)/shard_map/ppermute | solution.py:275
  71.8 18.0 %collective-permute-start.19 = (bf16[192,1024]{1,0:T(8,128)(2,1)}, bf16[192,1024]{1,0:T(8,128)(2,1)}, u32[]{:S(2)}, u32[]{:S(2)}) collective-permute-start(bf16[192,1024]{1,0:T(8,128)(2,1)} %get-tuple-element.108), channel_id=1, source_target_pairs={{0,24},{8,16},{16,8},{24,0},{1,25},{9,17},{17,9},{25,1},{2,26},{10... | collective-permute-start | bytes 1179656 | tf_op jit(solution)/shard_map/ppermute | solution.py:275
  87.6 8.0 %collective-permute-start.15 = (bf16[1024,1024]{1,0:T(8,128)(2,1)}, bf16[1024,1024]{1,0:T(8,128)(2,1)}, u32[]{:S(2)}, u32[]{:S(2)}) collective-permute-start(bf16[1024,1024]{1,0:T(8,128)(2,1)} %get-tuple-element.105), channel_id=1, source_target_pairs={{0,4},{4,0},{1,5},{5,1},{2,6},{6,2},{3,7},{7,3},{8,12},{12,8},{9,1... | collective-permute-start | bytes 6291464 | tf_op jit(solution)/shard_map/ppermute | solution.py:305
  92.0 9.2 %collective-permute-start.20 = (bf16[64,1024]{1,0:T(8,128)(2,1)S(1)}, bf16[64,1024]{1,0:T(8,128)(2,1)S(1)}, u32[]{:S(2)}, u32[]{:S(2)}) collective-permute-start(bf16[64,1024]{1,0:T(8,128)(2,1)S(1)} %get-tuple-element.116), channel_id=1, source_target_pairs={{0,8},{8,0},{16,24},{24,16},{1,9},{9,1},{17,25},{25,17},{2,10},{10... | collective-permute-start | bytes 393224 | tf_op jit(solution)/shard_map/ppermute | solution.py:275
  93.3 9.0 %collective-permute-start.21 = (bf16[64,1024]{1,0:T(8,128)(2,1)}, bf16[64,1024]{1,0:T(8,128)(2,1)S(1)}, u32[]{:S(2)}, u32[]{:S(2)}) collective-permute-start(bf16[64,1024]{1,0:T(8,128)(2,1)} %get-tuple-element.117), channel_id=1, source_target_pairs={{0,16},{8,24},{16,0},{24,8},{1,17},{9,25},{17,1},{25,9},{2,18},{10... | collective-permute-start | bytes 393224 | tf_op jit(solution)/shard_map/ppermute | solution.py:275
  94.1 8.1 %collective-permute-start.22 = (bf16[64,1024]{1,0:T(8,128)(2,1)S(1)}, bf16[64,1024]{1,0:T(8,128)(2,1)S(1)}, u32[]{:S(2)}, u32[]{:S(2)}) collective-permute-start(bf16[64,1024]{1,0:T(8,128)(2,1)S(1)} %get-tuple-element.118), channel_id=1, source_target_pairs={{0,24},{8,16},{16,8},{24,0},{1,25},{9,17},{17,9},{25,1},{2,26},{10... | collective-permute-start | bytes 393224 | tf_op jit(solution)/shard_map/ppermute | solution.py:275
  98.3 7.5 %collective-permute-start.29 = (bf16[64,1024]{1,0:T(8,128)(2,1)S(1)}, bf16[64,1024]{1,0:T(8,128)(2,1)S(1)}, u32[]{:S(2)}, u32[]{:S(2)}) collective-permute-start(bf16[64,1024]{1,0:T(8,128)(2,1)S(1)} %get-tuple-element.126), channel_id=1, source_target_pairs={{0,24},{8,16},{16,8},{24,0},{1,25},{9,17},{17,9},{25,1},{2,26},{10... | collective-permute-start | bytes 393224 | tf_op jit(solution)/shard_map/ppermute | solution.py:275
  99.8 7.5 %collective-permute-start.27 = (bf16[64,1024]{1,0:T(8,128)(2,1)S(1)}, bf16[64,1024]{1,0:T(8,128)(2,1)S(1)}, u32[]{:S(2)}, u32[]{:S(2)}) collective-permute-start(bf16[64,1024]{1,0:T(8,128)(2,1)S(1)} %get-tuple-element.124), channel_id=1, source_target_pairs={{0,8},{8,0},{16,24},{24,16},{1,9},{9,1},{17,25},{25,17},{2,10},{10... | collective-permute-start | bytes 393224 | tf_op jit(solution)/shard_map/ppermute | solution.py:275
  101.3 7.2 %collective-permute-start.28 = (bf16[64,1024]{1,0:T(8,128)(2,1)S(1)}, bf16[64,1024]{1,0:T(8,128)(2,1)S(1)}, u32[]{:S(2)}, u32[]{:S(2)}) collective-permute-start(bf16[64,1024]{1,0:T(8,128)(2,1)S(1)} %get-tuple-element.125), channel_id=1, source_target_pairs={{0,16},{8,24},{16,0},{24,8},{1,17},{9,25},{17,1},{25,9},{2,18},{10... | collective-permute-start | bytes 393224 | tf_op jit(solution)/shard_map/ppermute | solution.py:275
  105.0 8.0 %collective-permute-start.26 = (bf16[1024,1024]{1,0:T(8,128)(2,1)}, bf16[1024,1024]{1,0:T(8,128)(2,1)}, u32[]{:S(2)}, u32[]{:S(2)}) collective-permute-start(bf16[1024,1024]{1,0:T(8,128)(2,1)} %stack.32.mine_ref), channel_id=1, source_target_pairs={{0,4},{4,0},{1,5},{5,1},{2,6},{6,2},{3,7},{7,3},{8,12},{12,8},{9,1... | collective-permute-start | bytes 6291464 | tf_op jit(solution)/shard_map/ppermute | solution.py:305
  105.0 21.1 %collective-permute-start.23 = (bf16[192,1024]{1,0:T(8,128)(2,1)}, bf16[192,1024]{1,0:T(8,128)(2,1)}, u32[]{:S(2)}, u32[]{:S(2)}) collective-permute-start(bf16[192,1024]{1,0:T(8,128)(2,1)} %get-tuple-element.120), channel_id=1, source_target_pairs={{0,8},{8,0},{16,24},{24,16},{1,9},{9,1},{17,25},{25,17},{2,10},{10... | collective-permute-start | bytes 1179656 | tf_op jit(solution)/shard_map/ppermute | solution.py:275
  105.8 20.3 %collective-permute-start.24 = (bf16[192,1024]{1,0:T(8,128)(2,1)}, bf16[192,1024]{1,0:T(8,128)(2,1)}, u32[]{:S(2)}, u32[]{:S(2)}) collective-permute-start(bf16[192,1024]{1,0:T(8,128)(2,1)} %get-tuple-element.121), channel_id=1, source_target_pairs={{0,16},{8,24},{16,0},{24,8},{1,17},{9,25},{17,1},{25,9},{2,18},{10... | collective-permute-start | bytes 1179656 | tf_op jit(solution)/shard_map/ppermute | solution.py:275
  107.2 18.9 %collective-permute-start.25 = (bf16[192,1024]{1,0:T(8,128)(2,1)}, bf16[192,1024]{1,0:T(8,128)(2,1)}, u32[]{:S(2)}, u32[]{:S(2)}) collective-permute-start(bf16[192,1024]{1,0:T(8,128)(2,1)} %get-tuple-element.122), channel_id=1, source_target_pairs={{0,24},{8,16},{16,8},{24,0},{1,25},{9,17},{17,9},{25,1},{2,26},{10... | collective-permute-start | bytes 1179656 | tf_op jit(solution)/shard_map/ppermute | solution.py:275
  111.2 19.8 %collective-permute-start.35 = (bf16[272,1024]{1,0:T(8,128)(2,1)}, bf16[272,1024]{1,0:T(8,128)(2,1)}, u32[]{:S(2)}, u32[]{:S(2)}) collective-permute-start(bf16[272,1024]{1,0:T(8,128)(2,1)} %join_weighted.2), channel_id=1, source_target_pairs={{0,1},{1,0},{2,3},{3,2},{4,5},{5,4},{6,7},{7,6},{8,9},{9,8},{10,11... | collective-permute-start | bytes 1671176 | tf_op jit(solution)/shard_map/ppermute | solution.py:33
  124.6 11.9 %collective-permute-start.30 = (bf16[1024,1024]{1,0:T(8,128)(2,1)}, bf16[1024,1024]{1,0:T(8,128)(2,1)}, u32[]{:S(2)}, u32[]{:S(2)}) collective-permute-start(bf16[1024,1024]{1,0:T(8,128)(2,1)} %get-tuple-element.131), channel_id=1, source_target_pairs={{0,4},{4,0},{1,5},{5,1},{2,6},{6,2},{3,7},{7,3},{8,12},{12,8},{9,1... | collective-permute-start | bytes 6291464 | tf_op jit(solution)/shard_map/ppermute | solution.py:305
  129.1 25.1 %collective-permute-start.31 = (bf16[272,1024]{1,0:T(8,128)(2,1)S(1)}, bf16[272,1024]{1,0:T(8,128)(2,1)S(1)}, u32[]{:S(2)}, u32[]{:S(2)}) collective-permute-start(bf16[272,1024]{1,0:T(8,128)(2,1)S(1)} %get-tuple-element.145), channel_id=1, source_target_pairs={{0,1},{1,0},{2,3},{3,2},{4,5},{5,4},{6,7},{7,6},{8,9},{9,8},{10,11... | collective-permute-start | bytes 1671176 | tf_op jit(solution)/shard_map/ppermute | solution.py:33
  133.1 42.1 %collective-permute-start.37 = (bf16[272,1024]{1,0:T(8,128)(2,1)}, bf16[272,1024]{1,0:T(8,128)(2,1)}, u32[]{:S(2)}, u32[]{:S(2)}) collective-permute-start(bf16[272,1024]{1,0:T(8,128)(2,1)} %add_convert_fusion.1), channel_id=1, source_target_pairs={{0,2},{1,3},{2,0},{3,1},{4,6},{5,7},{6,4},{7,5},{8,10},{9,11},{10,... | collective-permute-start | bytes 1671176 | tf_op jit(solution)/shard_map/ppermute | solution.py:33
  140.7 14.6 %collective-permute-start.32 = (bf16[128,1024]{1,0:T(8,128)(2,1)S(1)}, bf16[128,1024]{1,0:T(8,128)(2,1)S(1)}, u32[]{:S(2)}, u32[]{:S(2)}) collective-permute-start(bf16[128,1024]{1,0:T(8,128)(2,1)S(1)} %get-tuple-element.139), channel_id=1, source_target_pairs={{0,8},{8,0},{16,24},{24,16},{1,9},{9,1},{17,25},{25,17},{2,10},{10... | collective-permute-start | bytes 786440 | tf_op jit(solution)/shard_map/ppermute | solution.py:275
  141.6 13.7 %collective-permute-start.33 = (bf16[128,1024]{1,0:T(8,128)(2,1)S(1)}, bf16[128,1024]{1,0:T(8,128)(2,1)S(1)}, u32[]{:S(2)}, u32[]{:S(2)}) collective-permute-start(bf16[128,1024]{1,0:T(8,128)(2,1)S(1)} %get-tuple-element.141), channel_id=1, source_target_pairs={{0,16},{8,24},{16,0},{24,8},{1,17},{9,25},{17,1},{25,9},{2,18},{10... | collective-permute-start | bytes 786440 | tf_op jit(solution)/shard_map/ppermute | solution.py:275
  143.0 12.3 %collective-permute-start.34 = (bf16[128,1024]{1,0:T(8,128)(2,1)S(1)}, bf16[128,1024]{1,0:T(8,128)(2,1)S(1)}, u32[]{:S(2)}, u32[]{:S(2)}) collective-permute-start(bf16[128,1024]{1,0:T(8,128)(2,1)S(1)} %get-tuple-element.143), channel_id=1, source_target_pairs={{0,24},{8,16},{16,8},{24,0},{1,25},{9,17},{17,9},{25,1},{2,26},{10... | collective-permute-start | bytes 786440 | tf_op jit(solution)/shard_map/ppermute | solution.py:275
  155.3 22.5 %collective-permute-start.38 = (bf16[128,1024]{1,0:T(8,128)(2,1)}, bf16[128,1024]{1,0:T(8,128)(2,1)}, u32[]{:S(2)}, u32[]{:S(2)}) collective-permute-start(bf16[128,1024]{1,0:T(8,128)(2,1)} %get-tuple-element.158), channel_id=1, source_target_pairs={{0,8},{8,0},{16,24},{24,16},{1,9},{9,1},{17,25},{25,17},{2,10},{10... | collective-permute-start | bytes 786440 | tf_op jit(solution)/shard_map/ppermute | solution.py:275
  156.3 21.6 %collective-permute-start.39 = (bf16[128,1024]{1,0:T(8,128)(2,1)}, bf16[128,1024]{1,0:T(8,128)(2,1)}, u32[]{:S(2)}, u32[]{:S(2)}) collective-permute-start(bf16[128,1024]{1,0:T(8,128)(2,1)} %get-tuple-element.159), channel_id=1, source_target_pairs={{0,16},{8,24},{16,0},{24,8},{1,17},{9,25},{17,1},{25,9},{2,18},{10... | collective-permute-start | bytes 786440 | tf_op jit(solution)/shard_map/ppermute | solution.py:275
  157.3 19.1 %collective-permute-start.40 = (bf16[128,1024]{1,0:T(8,128)(2,1)}, bf16[128,1024]{1,0:T(8,128)(2,1)}, u32[]{:S(2)}, u32[]{:S(2)}) collective-permute-start(bf16[128,1024]{1,0:T(8,128)(2,1)} %get-tuple-element.160), channel_id=1, source_target_pairs={{0,24},{8,16},{16,8},{24,0},{1,25},{9,17},{17,9},{25,1},{2,26},{10... | collective-permute-start | bytes 786440 | tf_op jit(solution)/shard_map/ppermute | solution.py:275
  159.3 12.3 %collective-permute-start.36 = (bf16[256,1024]{1,0:T(8,128)(2,1)S(1)}, bf16[256,1024]{1,0:T(8,128)(2,1)S(1)}, u32[]{:S(2)}, u32[]{:S(2)}) collective-permute-start(bf16[256,1024]{1,0:T(8,128)(2,1)S(1)} %get-tuple-element.149), channel_id=1, source_target_pairs={{0,1},{1,0},{2,3},{3,2},{4,5},{5,4},{6,7},{7,6},{8,9},{9,8},{10,11... | collective-permute-start | bytes 1572872 | tf_op jit(solution)/shard_map/ppermute | solution.py:33
  172.6 31.2 %collective-permute-start.42 = (bf16[256,1024]{1,0:T(8,128)(2,1)}, bf16[256,1024]{1,0:T(8,128)(2,1)}, u32[]{:S(2)}, u32[]{:S(2)}) collective-permute-start(bf16[256,1024]{1,0:T(8,128)(2,1)} %add_convert_fusion.5), channel_id=1, source_target_pairs={{0,2},{1,3},{2,0},{3,1},{4,6},{5,7},{6,4},{7,5},{8,10},{9,11},{10,... | collective-permute-start | bytes 1572872 | tf_op jit(solution)/shard_map/ppermute | solution.py:33
  177.8 10.5 %collective-permute-start.43 = (f32[2,256]{1,0:T(2,128)}, f32[2,256]{1,0:T(2,128)}, u32[]{:S(2)}, u32[]{:S(2)}) collective-permute-start(f32[2,256]{1,0:T(2,128)} %add.57), channel_id=1, source_target_pairs={{0,4},{4,0},{1,5},{5,1},{2,6},{6,2},{3,7},{7,3},{8,12},{12,8},{9,1... | collective-permute-start | bytes 6152 | tf_op jit(solution)/shard_map/ppermute | solution.py:305
  179.5 24.4 %collective-permute-start.41 = (bf16[256,1024]{1,0:T(8,128)(2,1)S(1)}, bf16[256,1024]{1,0:T(8,128)(2,1)S(1)}, u32[]{:S(2)}, u32[]{:S(2)}) collective-permute-start(bf16[256,1024]{1,0:T(8,128)(2,1)S(1)} %get-tuple-element.163), channel_id=1, source_target_pairs={{0,1},{1,0},{2,3},{3,2},{4,5},{5,4},{6,7},{7,6},{8,9},{9,8},{10,11... | collective-permute-start | bytes 1572872 | tf_op jit(solution)/shard_map/ppermute | solution.py:33
  (28 other events, 130.3 us)

commit v2 on v1

--- a/solution.py
+++ b/solution.py
@@ -327,7 +327,7 @@
         "ahead",
     )
     cot_near_in = exchange(cot_near_rows)
-    cot_in[line - 1] = after(cot_in[line - 1], out_sent, *cot_near_in[1:])
+    cot_in[line - 1] = after(cot_in[line - 1], out_sent)
     cot_far_rows = pick_group(cot_in, far, True, LARGE)
     out_came = after(swap(out_sent), cot_far_rows[0])
     out_pieces = deal_rows(out_kept, out_came, [cap * (line - 1), cap] * columns)
@@ -354,6 +354,7 @@
     back_pieces = deal_rows(back_kept, back_came, [cap * (line - 2), cap * 2] * columns)
     back_last = exchange(back_pieces[1::2])
     out_parts[0] = after(out_parts[0], *back_pieces)
+    out_parts[line - 2] = after(out_parts[line - 2], *back_pieces)
     out_sums = dict(enumerate(out_parts))
     reduce_bit(out_sums, 1, line)
     back_last[-1] = after(back_last[-1], *out_sums.values())
@@ -370,7 +371,9 @@
     grad_gate = dot(inbound, d_pre_gate, 0, 0).astype(BF)
     grad_up = dot(inbound, d_pre_up, 0, 0).astype(BF)
 
-    moved = after(moved, grad_gate, grad_up)
+    back_first[-1] = after(back_first[-1], grad_gate, grad_up)
+    back_parts = join_rows(slot[first], weight[first], back_first, cap)
+    moved = after(moved, back_parts[0])
     back_pair = (back_parts_last[0].astype(F32) + moved.astype(F32)).astype(BF)
     activation, cot_mine, cot_other, _ = together(activation, cot_mine, cot_other, back_pair)
     grad_down = dot(activation, full(cot_mine, cot_other), 0, 0).astype(BF)
@@ -379,8 +382,8 @@
     for bit in powers(line)[1:]:
         reduce_bit(out_sums, bit, line)
     out_total = out_sums[0]
-    back_first[-1] = after(back_first[-1], back_pair, out_total)
-    back_sums = dict(enumerate(join_rows(slot[first], weight[first], back_first, cap) + [back_pair]))
+    back_parts[0] = after(back_parts[0], out_total)
+    back_sums = dict(enumerate(back_parts + [back_pair]))
     for bit in powers(line):
         reduce_bit(back_sums, bit, line)
     d_tokens = back_sums[0]

time: 207 us -> 201 us (0.971)
  waiting for transfers between devices: 70 us -> 66.5 us
  local copies, waits for them, and re-layouts: 10.8 us -> 8.24 us
    ppermute x24, waiting for transfers between devices: 6.6 us -> 4.25 us  [exchange(): lax.ppermute(pieces[d], 'path', [(i, i ^ d) for i in range(columns)])]
    unnamed x65 -> x61, local copies, waits for them, and re-layouts: 9.05 us -> 7.02 us
  transfers between devices with their start and end apart: 44 -> 44, of which waited for: 13 -> 14; matrix products, arithmetic and copies ran while one was open for 12% -> 12% of each run, Pallas kernels for 21% -> 22%
where the time goes in v2:
time: 201 us; the launch traced here: 200 us
  waiting for transfers between devices  66.5 us (33%)
  starting transfers between devices  56 us (28%)
  Pallas kernels  44.6 us (22%)
  other arithmetic  13.4 us (7%)
  matrix products  10.1 us (5%)
  local copies, waits for them, and re-layouts  8.24 us (4%)
    ppermute x15, waiting for transfers between devices, to_place(): return lax.ppermute(value, 'expert', [(i, i ^ d) for i in range(line)])  62.2 us
    ppermute x24, starting transfers between devices, exchange(): lax.ppermute(pieces[d], 'path', [(i, i ^ d) for i in range(columns)])  29.2 us
    ppermute x15, starting transfers between devices, to_place(): return lax.ppermute(value, 'expert', [(i, i ^ d) for i in range(line)])  26.6 us
    pallas_call x2, Pallas kernels, by_rows(): pl.pallas_call(functools.partial(kernel, half), grid=(total // block,), o...  22.2 us
    dot_general x3, matrix products, dot(): lax.dot_general(a, b, (((ca,), (cb,)), ((), ())), preferred_element_type=...  10.1 us
    pallas_call x4, Pallas kernels, join_rows(): pl.pallas_call(functools.partial(join_kernel, n, cap, columns, weighted),...  8.78 us
    unnamed x61, local copies, waits for them, and re-layouts  7.02 us
    pallas_call x4, Pallas kernels, pick_rows(): pl.pallas_call(functools.partial(pick_kernel, n, cap, columns, scaled), o...  5.46 us
  transfers between devices with their start and end apart: 44, of which 14 were waited for; matrix products, arithmetic and copies ran while one was open for 12% of the time, Pallas kernels for 22%

profile of v2, /device:TPU:0, one launch (start us, length us, event | category | flops | bytes accessed | tf_op | source)
XLA Modules:
  0.0 200.0 jit_solution(165814961521856708)
XLA Ops:
  0.6 4.1 %collective-permute-start.3 = (bf16[256,1024]{1,0:T(8,128)(2,1)}, bf16[256,1024]{1,0:T(8,128)(2,1)S(1)}, u32[]{:S(2)}, u32[]{:S(2)}) collective-permute-start(bf16[256,1024]{1,0:T(8,128)(2,1)} %refs_2_.1), channel_id=1, source_target_pairs={{0,2},{1,3},{2,0},{3,1},{4,6},{5,7},{6,4},{7,5},{8,10},{9,11},{10,... | collective-permute-start | bytes 1572872 | tf_op jit(solution)/shard_map/ppermute | solution.py:33
  4.7 1.6 collective-permute-start.4
  9.7 3.9 %collective-permute-start.2 = (f32[4,256]{1,0:T(4,128)S(1)}, f32[4,256]{1,0:T(4,128)S(1)}, u32[]{:S(2)}, u32[]{:S(2)}) collective-permute-start(f32[4,256]{1,0:T(4,128)S(1)} %get-tuple-element.179), channel_id=1, source_target_pairs={{0,3},{1,2},{2,1},{3,0},{4,7},{5,6},{6,5},{7,4},{8,11},{9,10},{10,... | collective-permute-start | bytes 12296 | tf_op jit(solution)/shard_map/ppermute | solution.py:33
  13.5 14.9 %collective-permute-done.1 = f32[4,256]{1,0:T(4,128)S(1)} collective-permute-done((f32[4,256]{1,0:T(4,128)S(1)}, f32[4,256]{1,0:T(4,128)S(1)}, u32[]{:S(2)}, u32[]{:S(2)}) %collective-permute-start.1) | collective-permute-done | bytes 4128 | tf_op jit(solution)/shard_map/ppermute | solution.py:33
  32.0 1.6 collective-permute-start.6
  33.5 1.5 collective-permute-start.7
  35.5 2.4 %collective-permute-start.12 = (bf16[256,1024]{1,0:T(8,128)(2,1)S(1)}, bf16[256,1024]{1,0:T(8,128)(2,1)}, u32[]{:S(2)}, u32[]{:S(2)}) collective-permute-start(bf16[256,1024]{1,0:T(8,128)(2,1)S(1)} %copy-done.5), channel_id=1, source_target_pairs={{0,2},{1,3},{2,0},{3,1},{4,6},{5,7},{6,4},{7,5},{8,10},{9,11},{10,... | collective-permute-start | bytes 1572872 | tf_op jit(solution)/shard_map/ppermute | solution.py:33
  38.0 11.0 %collective-permute-done.5.refs_2_ = bf16[256,1024]{1,0:T(8,128)(2,1)S(1)} collective-permute-done((bf16[256,1024]{1,0:T(8,128)(2,1)S(1)}, bf16[256,1024]{1,0:T(8,128)(2,1)S(1)}, u32[]{:S(2)}, u32[]{:S(2)}) %collective-permute-start.5) | collective-permute-done | bytes 524320 | tf_op jit(solution)/shard_map/ppermute | solution.py:33
  49.1 2.4 %collective-permute-done.7.refs_4_ = bf16[192,1024]{1,0:T(8,128)(2,1)S(1)} collective-permute-done((bf16[192,1024]{1,0:T(8,128)(2,1)S(1)}, bf16[192,1024]{1,0:T(8,128)(2,1)S(1)}, u32[]{:S(2)}, u32[]{:S(2)}) %collective-permute-start.7) | collective-permute-done | bytes 393248 | tf_op jit(solution)/shard_map/ppermute | solution.py:275
  51.8 1.6 collective-permute-start.11
  53.3 1.5 collective-permute-start.9
  55.3 5.0 %collective-permute-done.12.refs_4_.refs_8_ = bf16[256,1024]{1,0:T(8,128)(2,1)} collective-permute-done((bf16[256,1024]{1,0:T(8,128)(2,1)S(1)}, bf16[256,1024]{1,0:T(8,128)(2,1)}, u32[]{:S(2)}, u32[]{:S(2)}) %collective-permute-start.12) | collective-permute-done | bytes 524320 | tf_op jit(solution)/shard_map/ppermute | solution.py:33
  60.3 4.8 %collective-permute-done.13.refs_3_.refs_7_ = bf16[256,1024]{1,0:T(8,128)(2,1)S(1)} collective-permute-done((bf16[256,1024]{1,0:T(8,128)(2,1)S(1)}, bf16[256,1024]{1,0:T(8,128)(2,1)S(1)}, u32[]{:S(2)}, u32[]{:S(2)}) %collective-permute-start.13) | collective-permute-done | bytes 524320 | tf_op jit(solution)/shard_map/ppermute | solution.py:33
  65.9 3.0 %pick_scaled.2 = (bf16[192,1024]{1,0:T(8,128)(2,1)S(1)}, bf16[192,1024]{1,0:T(8,128)(2,1)}, bf16[192,1024]{1,0:T(8,128)(2,1)}, bf16[192,1024]{1,0:T(8,128)(2,1)}) custom-call(s32[3,2,256]{2,1,0:T(2,128)S(1)} %slice.76.refs_0_, f32[3,2,256]{2,1,0:T(2,128)S(1)} %pad_maximum_fusion.4.refs_1_, bf16[256,1024]{1,0:T(8,128)(2,1)S(1)} %copy-done.5, ...), custom_call_target="tpu_custom_call" | custom-call | tf_op jit(solution)/shard_map/pick_scaled/pallas_call | solution.py:80
  68.9 1.5 collective-permute-start.17
  70.4 1.5 collective-permute-start.19
  72.4 1.4 copy-done.12
  73.8 10.6 %ahead.1 = (f32[1024,384]{1,0:T(8,128)S(1)}, f32[1024,384]{1,0:T(8,128)S(1)}, bf16[1024,384]{1,0:T(8,128)(2,1)S(1)}, bf16[1024,1024]{1,0:T(8,128)(2,1)}, bf16[1024,1024]{1,0:T(8,128)(2,1)}) custom-call(s32[1]{0:T(128)} %bitcast.6.head_ref, bf16[1024,1024]{1,0:T(8,128)(2,1)} %copy-done, bf16[1024,1024]{1,0:T(8,128)(2,1)} %collective-permute-done.14.other_ref, ...), custom_call_target="tpu_custom_call" | custom-call | flops 399999991808 | bytes 41943040 | tf_op jit(solution)/shard_map/ahead/pallas_call | solution.py:218
  87.6 1.6 pick_scaled.3
  89.2 1.5 collective-permute-start.18
  90.8 1.5 collective-permute-start.20
  92.3 2.3 %collective-permute-start.22 = (bf16[64,1024]{1,0:T(8,128)(2,1)S(1)}, bf16[64,1024]{1,0:T(8,128)(2,1)S(1)}, u32[]{:S(2)}, u32[]{:S(2)}) collective-permute-start(bf16[64,1024]{1,0:T(8,128)(2,1)S(1)} %get-tuple-element.120), channel_id=1, source_target_pairs={{0,24},{8,16},{16,8},{24,0},{1,25},{9,17},{17,9},{25,1},{2,26},{10... | collective-permute-start | bytes 393224 | tf_op jit(solution)/shard_map/ppermute | solution.py:275
  94.6 2.7 %deal.2 = (bf16[192,1024]{1,0:T(8,128)(2,1)S(1)}, bf16[64,1024]{1,0:T(8,128)(2,1)S(1)}, bf16[192,1024]{1,0:T(8,128)(2,1)}, bf16[64,1024]{1,0:T(8,128)(2,1)S(1)},...) custom-call(bf16[1024,1024]{1,0:T(8,128)(2,1)S(1)} %copy-done.3, ...), custom_call_target="tpu_custom_call" | custom-call | tf_op jit(solution)/shard_map/deal/pallas_call | solution.py:241
  99.3 1.5 collective-permute-start.28
  100.8 2.7 %stack.32.mine_ref = bf16[1024,1024]{1,0:T(8,128)(2,1)} custom-call(bf16[192,1024]{1,0:T(8,128)(2,1)S(1)} %get-tuple-element.104.refs_0_, bf16[64,1024]{1,0:T(8,128)(2,1)S(1)} %get-tuple-element.109.refs_1_, bf16[192,1024]{1,0:T(8,128)(2,1)} %collective-permute-done.17.refs_2_, bf16[64,1024]{1,0:T(8,128)(2,1)S(1)} %collective-permute-done.18.refs_3_, ...), custom_call_target="tpu_custom_call" | custom-call | tf_op jit(solution)/shard_map/stack/pallas_call | solution.py:103
  105.3 1.8 collective-permute-start.25
  107.1 2.7 %join_weighted.2 = bf16[272,1024]{1,0:T(8,128)(2,1)} custom-call(s32[1,2,256]{2,1,0:T(2,128)S(1)} %copy-done.11, f32[1,2,256]{2,1,0:T(2,128)S(1)} %copy-done.8, bf16[64,1024]{1,0:T(8,128)(2,1)S(1)} %get-tuple-element.125.refs_2_, bf16[64,1024]{1,0:T(8,128)(2,1)S(1)} %collective-permute-done.27.refs_3_, bf16[64,1024]{1,0:T(8,128)(2,1)} %collective-permute-done.28.refs_4_, ...), custom_call_target="tpu_custom_call" | custom-call | flops 399999991808 | bytes 41943040 | tf_op jit(solution)/shard_map/join_weighted/pallas_call | solution.py:158
  109.8 1.5 collective-permute-start.35
  111.3 11.6 %back.1 = (bf16[1024,384]{1,0:T(8,128)(2,1)S(1)}, bf16[1024,384]{1,0:T(8,128)(2,1)S(1)}, bf16[1024,1024]{1,0:T(8,128)(2,1)}, bf16[1024,1024]{1,0:T(8,128)(2,1)}) custom-call(s32[1]{0:T(128)} %bitcast.6.head_ref, bf16[1024,1024]{1,0:T(8,128)(2,1)} %stack.32.mine_ref, bf16[1024,1024]{1,0:T(8,128)(2,1)} %collective-permute-done.26.other_ref, ...), custom_call_target="tpu_custom_call" | custom-call | flops 399999991808 | bytes 41943040 | tf_op jit(solution)/shard_map/back/pallas_call | solution.py:218
  124.1 3.1 %join_weighted.3 = (bf16[272,1024]{1,0:T(8,128)(2,1)S(1)}, bf16[272,1024]{1,0:T(8,128)(2,1)S(1)}, bf16[272,1024]{1,0:T(8,128)(2,1)S(1)}) custom-call(s32[3,2,256]{2,1,0:T(2,128)S(1)} %slice.76.refs_0_, f32[3,2,256]{2,1,0:T(2,128)S(1)} %pad_maximum_fusion.4.refs_1_, bf16[192,1024]{1,0:T(8,128)(2,1)S(1)} %get-tuple-element.121.refs_2_, ...), custom_call_target="tpu_custom_call" | custom-call | flops 399999991808 | bytes 41943040 | tf_op jit(solution)/shard_map/join_weighted/pallas_call | solution.py:158
  127.2 1.6 collective-permute-start.31
  128.8 2.6 %deal.3 = (bf16[128,1024]{1,0:T(8,128)(2,1)S(1)}, bf16[128,1024]{1,0:T(8,128)(2,1)S(1)}, bf16[128,1024]{1,0:T(8,128)(2,1)}, bf16[128,1024]{1,0:T(8,128)(2,1)S(1)...) custom-call(bf16[1024,1024]{1,0:T(8,128)(2,1)S(1)} %copy-done.2, ...), custom_call_target="tpu_custom_call" | custom-call | tf_op jit(solution)/shard_map/deal/pallas_call | solution.py:241
  131.4 1.5 collective-permute-start.32
  133.4 1.5 collective-permute-start.34
  134.9 2.1 %add_convert_fusion.1 = bf16[272,1024]{1,0:T(8,128)(2,1)} fusion(bf16[272,1024]{1,0:T(8,128)(2,1)} %collective-permute-done.35, bf16[272,1024]{1,0:T(8,128)(2,1)S(1)} %get-tuple-element.149), kind=kLoop, calls=%fused_computation.14 | loop fusion | flops 1114112 | bytes 1671168 | tf_op jit(solution)/shard_map/convert_element_type | solution.py:53
  137.0 3.7 %collective-permute-start.40 = (bf16[272,1024]{1,0:T(8,128)(2,1)}, bf16[272,1024]{1,0:T(8,128)(2,1)}, u32[]{:S(2)}, u32[]{:S(2)}) collective-permute-start(bf16[272,1024]{1,0:T(8,128)(2,1)} %add_convert_fusion.1), channel_id=1, source_target_pairs={{0,2},{1,3},{2,0},{3,1},{4,6},{5,7},{6,4},{7,5},{8,10},{9,11},{10,... | collective-permute-start | bytes 1671176 | tf_op jit(solution)/shard_map/ppermute | solution.py:33
  140.7 5.4 %collective-permute-done.31 = bf16[272,1024]{1,0:T(8,128)(2,1)S(1)} collective-permute-done((bf16[272,1024]{1,0:T(8,128)(2,1)S(1)}, bf16[272,1024]{1,0:T(8,128)(2,1)S(1)}, u32[]{:S(2)}, u32[]{:S(2)}) %collective-permute-start.31) | collective-permute-done | bytes 557088 | tf_op jit(solution)/shard_map/ppermute | solution.py:33
  147.2 1.5 collective-permute-start.37
  152.5 1.9 broadcast_select_fusion.3
  154.4 3.6 %convolution_convert_fusion = bf16[2048,384]{1,0:T(8,128)(2,1)} fusion(bf16[1024,384]{1,0:T(8,128)(2,1)S(1)} %get-tuple-element.161, bf16[1024,1024]{1,0:T(8,128)(2,1)S(1)} %get-tuple-element.175, bf16[1024,1024]{1,0:T(8,128)(2,1)S(1)} %get-tuple-element.174), kind=kOutput, calls=%fused_computation.6 | convolution fusion | flops 1619787776 | bytes 6553600 | tf_op jit(solution)/shard_map/dot_general | solution.py:22
  158.0 3.6 %convolution_convert_fusion.1 = bf16[2048,384]{1,0:T(8,128)(2,1)} fusion(bf16[1024,384]{1,0:T(8,128)(2,1)S(1)} %get-tuple-element.160, bf16[1024,1024]{1,0:T(8,128)(2,1)S(1)} %get-tuple-element.175, bf16[1024,1024]{1,0:T(8,128)(2,1)S(1)} %get-tuple-element.174), kind=kOutput, calls=%fused_computation.7 | convolution fusion | flops 1619787776 | bytes 6553600 | tf_op jit(solution)/shard_map/dot_general | solution.py:22
  161.5 1.7 join.3
  163.2 1.6 collective-permute-start.41
  164.8 8.0 %collective-permute-done.36 = bf16[256,1024]{1,0:T(8,128)(2,1)} collective-permute-done((bf16[256,1024]{1,0:T(8,128)(2,1)}, bf16[256,1024]{1,0:T(8,128)(2,1)}, u32[]{:S(2)}, u32[]{:S(2)}) %collective-permute-start.36) | collective-permute-done | bytes 524320 | tf_op jit(solution)/shard_map/ppermute | solution.py:33
  174.1 4.5 %collective-permute-start.42 = (bf16[256,1024]{1,0:T(8,128)(2,1)S(1)}, bf16[256,1024]{1,0:T(8,128)(2,1)S(1)}, u32[]{:S(2)}, u32[]{:S(2)}) collective-permute-start(bf16[256,1024]{1,0:T(8,128)(2,1)S(1)} %add_convert_fusion.5), channel_id=1, source_target_pairs={{0,2},{1,3},{2,0},{3,1},{4,6},{5,7},{6,4},{7,5},{8,10},{9,11},{10,... | collective-permute-start | bytes 1572872 | tf_op jit(solution)/shard_map/ppermute | solution.py:33
  180.0 2.6 %broadcast_select_fusion.1 = (bf16[1024,1024]{1,0:T(8,128)(2,1)S(1)}, bf16[1024,1024]{1,0:T(8,128)(2,1)S(1)}) fusion(bf16[1024,1024]{1,0:T(8,128)(2,1)} %stack.32.mine_ref, bf16[1024,1024]{1,0:T(8,128)(2,1)} %collective-permute-done.26.other_ref, pred[]{:T(512)S(6)} %eq.34), kind=kLoop, calls=%fused_computation.10 | loop fusion | flops 2097152 | bytes 8388609 | tf_op jit(solution)/shard_map/jit(_where)/select_n | solution.py:310
  182.6 3.0 %fusion.7 = bf16[1,384,2048]{2,1,0:T(8,128)(2,1)} fusion(bf16[1024,384]{1,0:T(8,128)(2,1)S(1)} %copy-done.14, bf16[1024,1024]{1,0:T(8,128)(2,1)S(1)} %get-tuple-element.173, bf16[1024,1024]{1,0:T(8,128)(2,1)S(1)} %get-tuple-element.172), kind=kOutput, calls=%fused_computation.8 | convolution fusion | flops 1619787776 | bytes 6553600 | tf_op jit(solution)/shard_map/dot_general | solution.py:22
  187.0 11.9 %collective-permute-done.42 = bf16[256,1024]{1,0:T(8,128)(2,1)S(1)} collective-permute-done((bf16[256,1024]{1,0:T(8,128)(2,1)S(1)}, bf16[256,1024]{1,0:T(8,128)(2,1)S(1)}, u32[]{:S(2)}, u32[]{:S(2)}) %collective-permute-start.42) | collective-permute-done | bytes 524320 | tf_op jit(solution)/shard_map/ppermute | solution.py:33
  (145 shorter events, 28.0 us)
Async XLA Ops:
  0.6 34.9 %copy-start.5 = (bf16[256,1024]{1,0:T(8,128)(2,1)S(1)}, bf16[256,1024]{1,0:T(8,128)(2,1)}, u32[]{:S(2)}) copy-start(bf16[256,1024]{1,0:T(8,128)(2,1)} %refs_6_) | copy-start | bytes 1572868
  0.6 28.9 %collective-permute-start.3 = (bf16[256,1024]{1,0:T(8,128)(2,1)}, bf16[256,1024]{1,0:T(8,128)(2,1)S(1)}, u32[]{:S(2)}, u32[]{:S(2)}) collective-permute-start(bf16[256,1024]{1,0:T(8,128)(2,1)} %refs_2_.1), channel_id=1, source_target_pairs={{0,2},{1,3},{2,0},{3,1},{4,6},{5,7},{6,4},{7,5},{8,10},{9,11},{10,... | collective-permute-start | bytes 1572872 | tf_op jit(solution)/shard_map/ppermute | solution.py:33
  4.7 24.8 %collective-permute-start.4 = (bf16[256,1024]{1,0:T(8,128)(2,1)}, bf16[256,1024]{1,0:T(8,128)(2,1)S(1)}, u32[]{:S(2)}, u32[]{:S(2)}) collective-permute-start(bf16[256,1024]{1,0:T(8,128)(2,1)} %refs_2_.1), channel_id=1, source_target_pairs={{0,1},{1,0},{2,3},{3,2},{4,5},{5,4},{6,7},{7,6},{8,9},{9,8},{10,11... | collective-permute-start | bytes 1572872 | tf_op jit(solution)/shard_map/ppermute | solution.py:33
  9.1 21.2 %copy-start.22 = (f32[1,4,256]{2,1,0:T(4,128)}, f32[1,4,256]{2,1,0:T(4,128)S(1)}, u32[]{:S(2)}) copy-start(f32[1,4,256]{2,1,0:T(4,128)S(1)} %get-tuple-element.178) | copy-start | bytes 12292
  9.1 19.3 %collective-permute-start.1 = (f32[4,256]{1,0:T(4,128)S(1)}, f32[4,256]{1,0:T(4,128)S(1)}, u32[]{:S(2)}, u32[]{:S(2)}) collective-permute-start(f32[4,256]{1,0:T(4,128)S(1)} %get-tuple-element.179), channel_id=1, source_target_pairs={{0,2},{1,3},{2,0},{3,1},{4,6},{5,7},{6,4},{7,5},{8,10},{9,11},{10,... | collective-permute-start | bytes 12296 | tf_op jit(solution)/shard_map/ppermute | solution.py:33
  9.5 19.2 %collective-permute-start = (f32[4,256]{1,0:T(4,128)S(1)}, f32[4,256]{1,0:T(4,128)S(1)}, u32[]{:S(2)}, u32[]{:S(2)}) collective-permute-start(f32[4,256]{1,0:T(4,128)S(1)} %get-tuple-element.179), channel_id=1, source_target_pairs={{0,1},{1,0},{2,3},{3,2},{4,5},{5,4},{6,7},{7,6},{8,9},{9,8},{10,11... | collective-permute-start | bytes 12296 | tf_op jit(solution)/shard_map/ppermute | solution.py:33
  9.7 19.8 %collective-permute-start.2 = (f32[4,256]{1,0:T(4,128)S(1)}, f32[4,256]{1,0:T(4,128)S(1)}, u32[]{:S(2)}, u32[]{:S(2)}) collective-permute-start(f32[4,256]{1,0:T(4,128)S(1)} %get-tuple-element.179), channel_id=1, source_target_pairs={{0,3},{1,2},{2,1},{3,0},{4,7},{5,6},{6,5},{7,4},{8,11},{9,10},{10,... | collective-permute-start | bytes 12296 | tf_op jit(solution)/shard_map/ppermute | solution.py:33
  29.5 35.7 %copy-start.28 = (f32[4,256]{1,0:T(4,128)}, f32[4,256]{1,0:T(4,128)S(1)}, u32[]{:S(2)}) copy-start(f32[4,256]{1,0:T(4,128)S(1)} %collective-permute-done.2) | copy-start | bytes 12292
  29.5 19.5 %collective-permute-start.5 = (bf16[256,1024]{1,0:T(8,128)(2,1)S(1)}, bf16[256,1024]{1,0:T(8,128)(2,1)S(1)}, u32[]{:S(2)}, u32[]{:S(2)}) collective-permute-start(bf16[256,1024]{1,0:T(8,128)(2,1)S(1)} %collective-permute-done.3.refs_4_), channel_id=1, source_target_pairs={{0,1},{1,0},{2,3},{3,2},{4,5},{5,4},{6,7},{7,6},{8,9},{9,8},{10,11... | collective-permute-start | bytes 1572872 | tf_op jit(solution)/shard_map/ppermute | solution.py:33
  30.3 35.0 %copy-start.20 = (s32[4,2,256]{2,1,0:T(2,128)}, s32[4,2,256]{2,1,0:T(2,128)S(1)}, u32[]{:S(2)}) copy-start(s32[4,2,256]{2,1,0:T(2,128)S(1)} %compare_select_fusion) | copy-start | bytes 24580
  32.0 17.1 %collective-permute-start.6 = (bf16[192,1024]{1,0:T(8,128)(2,1)S(1)}, bf16[192,1024]{1,0:T(8,128)(2,1)S(1)}, u32[]{:S(2)}, u32[]{:S(2)}) collective-permute-start(bf16[192,1024]{1,0:T(8,128)(2,1)S(1)} %get-tuple-element.92), channel_id=1, source_target_pairs={{0,8},{8,0},{16,24},{24,16},{1,9},{9,1},{17,25},{25,17},{2,10},{10... | collective-permute-start | bytes 1179656 | tf_op jit(solution)/shard_map/ppermute | solution.py:275
  33.5 17.9 %collective-permute-start.7 = (bf16[192,1024]{1,0:T(8,128)(2,1)S(1)}, bf16[192,1024]{1,0:T(8,128)(2,1)S(1)}, u32[]{:S(2)}, u32[]{:S(2)}) collective-permute-start(bf16[192,1024]{1,0:T(8,128)(2,1)S(1)} %get-tuple-element.93), channel_id=1, source_target_pairs={{0,16},{8,24},{16,0},{24,8},{1,17},{9,25},{17,1},{25,9},{2,18},{10... | collective-permute-start | bytes 1179656 | tf_op jit(solution)/shard_map/ppermute | solution.py:275
  35.1 16.4 %collective-permute-start.8 = (bf16[192,1024]{1,0:T(8,128)(2,1)S(1)}, bf16[192,1024]{1,0:T(8,128)(2,1)S(1)}, u32[]{:S(2)}, u32[]{:S(2)}) collective-permute-start(bf16[192,1024]{1,0:T(8,128)(2,1)S(1)} %get-tuple-element.94), channel_id=1, source_target_pairs={{0,24},{8,16},{16,8},{24,0},{1,25},{9,17},{17,9},{25,1},{2,26},{10... | collective-permute-start | bytes 1179656 | tf_op jit(solution)/shard_map/ppermute | solution.py:275
  35.5 24.8 %collective-permute-start.12 = (bf16[256,1024]{1,0:T(8,128)(2,1)S(1)}, bf16[256,1024]{1,0:T(8,128)(2,1)}, u32[]{:S(2)}, u32[]{:S(2)}) collective-permute-start(bf16[256,1024]{1,0:T(8,128)(2,1)S(1)} %copy-done.5), channel_id=1, source_target_pairs={{0,2},{1,3},{2,0},{3,1},{4,6},{5,7},{6,4},{7,5},{8,10},{9,11},{10,... | collective-permute-start | bytes 1572872 | tf_op jit(solution)/shard_map/ppermute | solution.py:33
  49.0 16.1 %collective-permute-start.13 = (bf16[256,1024]{1,0:T(8,128)(2,1)S(1)}, bf16[256,1024]{1,0:T(8,128)(2,1)S(1)}, u32[]{:S(2)}, u32[]{:S(2)}) collective-permute-start(bf16[256,1024]{1,0:T(8,128)(2,1)S(1)} %copy-done.5), channel_id=1, source_target_pairs={{0,1},{1,0},{2,3},{3,2},{4,5},{5,4},{6,7},{7,6},{8,9},{9,8},{10,11... | collective-permute-start | bytes 1572872 | tf_op jit(solution)/shard_map/ppermute | solution.py:33
  51.8 8.6 %collective-permute-start.11 = (bf16[64,1024]{1,0:T(8,128)(2,1)S(1)}, bf16[64,1024]{1,0:T(8,128)(2,1)S(1)}, u32[]{:S(2)}, u32[]{:S(2)}) collective-permute-start(bf16[64,1024]{1,0:T(8,128)(2,1)S(1)} %get-tuple-element.99), channel_id=1, source_target_pairs={{0,24},{8,16},{16,8},{24,0},{1,25},{9,17},{17,9},{25,1},{2,26},{10... | collective-permute-start | bytes 393224 | tf_op jit(solution)/shard_map/ppermute | solution.py:275
  53.3 11.9 %collective-permute-start.9 = (bf16[64,1024]{1,0:T(8,128)(2,1)S(1)}, bf16[64,1024]{1,0:T(8,128)(2,1)S(1)}, u32[]{:S(2)}, u32[]{:S(2)}) collective-permute-start(bf16[64,1024]{1,0:T(8,128)(2,1)S(1)} %get-tuple-element.97), channel_id=1, source_target_pairs={{0,8},{8,0},{16,24},{24,16},{1,9},{9,1},{17,25},{25,17},{2,10},{10... | collective-permute-start | bytes 393224 | tf_op jit(solution)/shard_map/ppermute | solution.py:275
  54.8 10.4 %collective-permute-start.10 = (bf16[64,1024]{1,0:T(8,128)(2,1)S(1)}, bf16[64,1024]{1,0:T(8,128)(2,1)S(1)}, u32[]{:S(2)}, u32[]{:S(2)}) collective-permute-start(bf16[64,1024]{1,0:T(8,128)(2,1)S(1)} %get-tuple-element.98), channel_id=1, source_target_pairs={{0,16},{8,24},{16,0},{24,8},{1,17},{9,25},{17,1},{25,9},{2,18},{10... | collective-permute-start | bytes 393224 | tf_op jit(solution)/shard_map/ppermute | solution.py:275
  65.3 7.0 %collective-permute-start.14 = (bf16[1024,1024]{1,0:T(8,128)(2,1)S(1)}, bf16[1024,1024]{1,0:T(8,128)(2,1)}, u32[]{:S(2)}, u32[]{:S(2)}) collective-permute-start(bf16[1024,1024]{1,0:T(8,128)(2,1)S(1)} %stack.31.mine_ref), channel_id=1, source_target_pairs={{0,4},{4,0},{1,5},{5,1},{2,6},{6,2},{3,7},{7,3},{8,12},{12,8},{9,1... | collective-permute-start | bytes 6291464 | tf_op jit(solution)/shard_map/ppermute | solution.py:305
  65.4 22.2 %collective-permute-start.16 = (bf16[256,1024]{1,0:T(8,128)(2,1)}, bf16[256,1024]{1,0:T(8,128)(2,1)}, u32[]{:S(2)}, u32[]{:S(2)}) collective-permute-start(bf16[256,1024]{1,0:T(8,128)(2,1)} %collective-permute-done.12.refs_4_.refs_8_), channel_id=1, source_target_pairs={{0,1},{1,0},{2,3},{3,2},{4,5},{5,4},{6,7},{7,6},{8,9},{9,8},{10,11... | collective-permute-start | bytes 1572872 | tf_op jit(solution)/shard_map/ppermute | solution.py:33
  68.9 21.9 %collective-permute-start.17 = (bf16[192,1024]{1,0:T(8,128)(2,1)}, bf16[192,1024]{1,0:T(8,128)(2,1)}, u32[]{:S(2)}, u32[]{:S(2)}) collective-permute-start(bf16[192,1024]{1,0:T(8,128)(2,1)} %get-tuple-element.115), channel_id=1, source_target_pairs={{0,8},{8,0},{16,24},{24,16},{1,9},{9,1},{17,25},{25,17},{2,10},{10... | collective-permute-start | bytes 1179656 | tf_op jit(solution)/shard_map/ppermute | solution.py:275
  70.4 26.9 %collective-permute-start.19 = (bf16[192,1024]{1,0:T(8,128)(2,1)}, bf16[192,1024]{1,0:T(8,128)(2,1)}, u32[]{:S(2)}, u32[]{:S(2)}) collective-permute-start(bf16[192,1024]{1,0:T(8,128)(2,1)} %get-tuple-element.117), channel_id=1, source_target_pairs={{0,16},{8,24},{16,0},{24,8},{1,17},{9,25},{17,1},{25,9},{2,18},{10... | collective-permute-start | bytes 1179656 | tf_op jit(solution)/shard_map/ppermute | solution.py:275
  71.9 26.1 %collective-permute-start.21 = (bf16[192,1024]{1,0:T(8,128)(2,1)}, bf16[192,1024]{1,0:T(8,128)(2,1)}, u32[]{:S(2)}, u32[]{:S(2)}) collective-permute-start(bf16[192,1024]{1,0:T(8,128)(2,1)} %get-tuple-element.119), channel_id=1, source_target_pairs={{0,24},{8,16},{16,8},{24,0},{1,25},{9,17},{17,9},{25,1},{2,26},{10... | collective-permute-start | bytes 1179656 | tf_op jit(solution)/shard_map/ppermute | solution.py:275
  87.6 4.7 %collective-permute-start.15 = (bf16[1024,1024]{1,0:T(8,128)(2,1)}, bf16[1024,1024]{1,0:T(8,128)(2,1)}, u32[]{:S(2)}, u32[]{:S(2)}) collective-permute-start(bf16[1024,1024]{1,0:T(8,128)(2,1)} %get-tuple-element.107), channel_id=1, source_target_pairs={{0,4},{4,0},{1,5},{5,1},{2,6},{6,2},{3,7},{7,3},{8,12},{12,8},{9,1... | collective-permute-start | bytes 6291464 | tf_op jit(solution)/shard_map/ppermute | solution.py:305
  89.2 10.0 %collective-permute-start.18 = (bf16[64,1024]{1,0:T(8,128)(2,1)S(1)}, bf16[64,1024]{1,0:T(8,128)(2,1)S(1)}, u32[]{:S(2)}, u32[]{:S(2)}) collective-permute-start(bf16[64,1024]{1,0:T(8,128)(2,1)S(1)} %get-tuple-element.116), channel_id=1, source_target_pairs={{0,8},{8,0},{16,24},{24,16},{1,9},{9,1},{17,25},{25,17},{2,10},{10... | collective-permute-start | bytes 393224 | tf_op jit(solution)/shard_map/ppermute | solution.py:275
  90.8 10.0 %collective-permute-start.20 = (bf16[64,1024]{1,0:T(8,128)(2,1)S(1)}, bf16[64,1024]{1,0:T(8,128)(2,1)S(1)}, u32[]{:S(2)}, u32[]{:S(2)}) collective-permute-start(bf16[64,1024]{1,0:T(8,128)(2,1)S(1)} %get-tuple-element.118), channel_id=1, source_target_pairs={{0,16},{8,24},{16,0},{24,8},{1,17},{9,25},{17,1},{25,9},{2,18},{10... | collective-permute-start | bytes 393224 | tf_op jit(solution)/shard_map/ppermute | solution.py:275
  92.3 8.5 %collective-permute-start.22 = (bf16[64,1024]{1,0:T(8,128)(2,1)S(1)}, bf16[64,1024]{1,0:T(8,128)(2,1)S(1)}, u32[]{:S(2)}, u32[]{:S(2)}) collective-permute-start(bf16[64,1024]{1,0:T(8,128)(2,1)S(1)} %get-tuple-element.120), channel_id=1, source_target_pairs={{0,24},{8,16},{16,8},{24,0},{1,25},{9,17},{17,9},{25,1},{2,26},{10... | collective-permute-start | bytes 393224 | tf_op jit(solution)/shard_map/ppermute | solution.py:275
  97.3 7.3 %collective-permute-start.29 = (bf16[64,1024]{1,0:T(8,128)(2,1)S(1)}, bf16[64,1024]{1,0:T(8,128)(2,1)S(1)}, u32[]{:S(2)}, u32[]{:S(2)}) collective-permute-start(bf16[64,1024]{1,0:T(8,128)(2,1)S(1)} %get-tuple-element.128), channel_id=1, source_target_pairs={{0,24},{8,16},{16,8},{24,0},{1,25},{9,17},{17,9},{25,1},{2,26},{10... | collective-permute-start | bytes 393224 | tf_op jit(solution)/shard_map/ppermute | solution.py:275
  97.9 7.3 %collective-permute-start.27 = (bf16[64,1024]{1,0:T(8,128)(2,1)S(1)}, bf16[64,1024]{1,0:T(8,128)(2,1)S(1)}, u32[]{:S(2)}, u32[]{:S(2)}) collective-permute-start(bf16[64,1024]{1,0:T(8,128)(2,1)S(1)} %get-tuple-element.126), channel_id=1, source_target_pairs={{0,8},{8,0},{16,24},{24,16},{1,9},{9,1},{17,25},{25,17},{2,10},{10... | collective-permute-start | bytes 393224 | tf_op jit(solution)/shard_map/ppermute | solution.py:275
  99.3 7.8 %collective-permute-start.28 = (bf16[64,1024]{1,0:T(8,128)(2,1)S(1)}, bf16[64,1024]{1,0:T(8,128)(2,1)}, u32[]{:S(2)}, u32[]{:S(2)}) collective-permute-start(bf16[64,1024]{1,0:T(8,128)(2,1)S(1)} %get-tuple-element.127), channel_id=1, source_target_pairs={{0,16},{8,24},{16,0},{24,8},{1,17},{9,25},{17,1},{25,9},{2,18},{10... | collective-permute-start | bytes 393224 | tf_op jit(solution)/shard_map/ppermute | solution.py:275
  103.5 7.8 %collective-permute-start.26 = (bf16[1024,1024]{1,0:T(8,128)(2,1)}, bf16[1024,1024]{1,0:T(8,128)(2,1)}, u32[]{:S(2)}, u32[]{:S(2)}) collective-permute-start(bf16[1024,1024]{1,0:T(8,128)(2,1)} %stack.32.mine_ref), channel_id=1, source_target_pairs={{0,4},{4,0},{1,5},{5,1},{2,6},{6,2},{3,7},{7,3},{8,12},{12,8},{9,1... | collective-permute-start | bytes 6291464 | tf_op jit(solution)/shard_map/ppermute | solution.py:305
  103.6 20.3 %collective-permute-start.23 = (bf16[192,1024]{1,0:T(8,128)(2,1)}, bf16[192,1024]{1,0:T(8,128)(2,1)}, u32[]{:S(2)}, u32[]{:S(2)}) collective-permute-start(bf16[192,1024]{1,0:T(8,128)(2,1)} %get-tuple-element.122), channel_id=1, source_target_pairs={{0,8},{8,0},{16,24},{24,16},{1,9},{9,1},{17,25},{25,17},{2,10},{10... | collective-permute-start | bytes 1179656 | tf_op jit(solution)/shard_map/ppermute | solution.py:275
  104.6 19.5 %collective-permute-start.24 = (bf16[192,1024]{1,0:T(8,128)(2,1)}, bf16[192,1024]{1,0:T(8,128)(2,1)}, u32[]{:S(2)}, u32[]{:S(2)}) collective-permute-start(bf16[192,1024]{1,0:T(8,128)(2,1)} %get-tuple-element.123), channel_id=1, source_target_pairs={{0,16},{8,24},{16,0},{24,8},{1,17},{9,25},{17,1},{25,9},{2,18},{10... | collective-permute-start | bytes 1179656 | tf_op jit(solution)/shard_map/ppermute | solution.py:275
  105.3 18.6 %collective-permute-start.25 = (bf16[192,1024]{1,0:T(8,128)(2,1)}, bf16[192,1024]{1,0:T(8,128)(2,1)}, u32[]{:S(2)}, u32[]{:S(2)}) collective-permute-start(bf16[192,1024]{1,0:T(8,128)(2,1)} %get-tuple-element.124), channel_id=1, source_target_pairs={{0,24},{8,16},{16,8},{24,0},{1,25},{9,17},{17,9},{25,1},{2,26},{10... | collective-permute-start | bytes 1179656 | tf_op jit(solution)/shard_map/ppermute | solution.py:275
  109.8 25.1 %collective-permute-start.35 = (bf16[272,1024]{1,0:T(8,128)(2,1)}, bf16[272,1024]{1,0:T(8,128)(2,1)}, u32[]{:S(2)}, u32[]{:S(2)}) collective-permute-start(bf16[272,1024]{1,0:T(8,128)(2,1)} %join_weighted.2), channel_id=1, source_target_pairs={{0,1},{1,0},{2,3},{3,2},{4,5},{5,4},{6,7},{7,6},{8,9},{9,8},{10,11... | collective-permute-start | bytes 1671176 | tf_op jit(solution)/shard_map/ppermute | solution.py:33
  122.9 5.9 %collective-permute-start.30 = (bf16[1024,1024]{1,0:T(8,128)(2,1)}, bf16[1024,1024]{1,0:T(8,128)(2,1)}, u32[]{:S(2)}, u32[]{:S(2)}) collective-permute-start(bf16[1024,1024]{1,0:T(8,128)(2,1)} %get-tuple-element.133), channel_id=1, source_target_pairs={{0,4},{4,0},{1,5},{5,1},{2,6},{6,2},{3,7},{7,3},{8,12},{12,8},{9,1... | collective-permute-start | bytes 6291464 | tf_op jit(solution)/shard_map/ppermute | solution.py:305
  127.2 18.9 %collective-permute-start.31 = (bf16[272,1024]{1,0:T(8,128)(2,1)S(1)}, bf16[272,1024]{1,0:T(8,128)(2,1)S(1)}, u32[]{:S(2)}, u32[]{:S(2)}) collective-permute-start(bf16[272,1024]{1,0:T(8,128)(2,1)S(1)} %get-tuple-element.147), channel_id=1, source_target_pairs={{0,1},{1,0},{2,3},{3,2},{4,5},{5,4},{6,7},{7,6},{8,9},{9,8},{10,11... | collective-permute-start | bytes 1671176 | tf_op jit(solution)/shard_map/ppermute | solution.py:33
  131.4 15.8 %collective-permute-start.32 = (bf16[128,1024]{1,0:T(8,128)(2,1)S(1)}, bf16[128,1024]{1,0:T(8,128)(2,1)S(1)}, u32[]{:S(2)}, u32[]{:S(2)}) collective-permute-start(bf16[128,1024]{1,0:T(8,128)(2,1)S(1)} %get-tuple-element.141), channel_id=1, source_target_pairs={{0,8},{8,0},{16,24},{24,16},{1,9},{9,1},{17,25},{25,17},{2,10},{10... | collective-permute-start | bytes 786440 | tf_op jit(solution)/shard_map/ppermute | solution.py:275
  132.9 14.3 %collective-permute-start.33 = (bf16[128,1024]{1,0:T(8,128)(2,1)S(1)}, bf16[128,1024]{1,0:T(8,128)(2,1)S(1)}, u32[]{:S(2)}, u32[]{:S(2)}) collective-permute-start(bf16[128,1024]{1,0:T(8,128)(2,1)S(1)} %get-tuple-element.143), channel_id=1, source_target_pairs={{0,16},{8,24},{16,0},{24,8},{1,17},{9,25},{17,1},{25,9},{2,18},{10... | collective-permute-start | bytes 786440 | tf_op jit(solution)/shard_map/ppermute | solution.py:275
  133.4 13.8 %collective-permute-start.34 = (bf16[128,1024]{1,0:T(8,128)(2,1)S(1)}, bf16[128,1024]{1,0:T(8,128)(2,1)S(1)}, u32[]{:S(2)}, u32[]{:S(2)}) collective-permute-start(bf16[128,1024]{1,0:T(8,128)(2,1)S(1)} %get-tuple-element.145), channel_id=1, source_target_pairs={{0,24},{8,16},{16,8},{24,0},{1,25},{9,17},{17,9},{25,1},{2,26},{10... | collective-permute-start | bytes 786440 | tf_op jit(solution)/shard_map/ppermute | solution.py:275
  137.0 41.6 %collective-permute-start.40 = (bf16[272,1024]{1,0:T(8,128)(2,1)}, bf16[272,1024]{1,0:T(8,128)(2,1)}, u32[]{:S(2)}, u32[]{:S(2)}) collective-permute-start(bf16[272,1024]{1,0:T(8,128)(2,1)} %add_convert_fusion.1), channel_id=1, source_target_pairs={{0,2},{1,3},{2,0},{3,1},{4,6},{5,7},{6,4},{7,5},{8,10},{9,11},{10,... | collective-permute-start | bytes 1671176 | tf_op jit(solution)/shard_map/ppermute | solution.py:33
  147.2 14.3 %collective-permute-start.37 = (bf16[128,1024]{1,0:T(8,128)(2,1)}, bf16[128,1024]{1,0:T(8,128)(2,1)}, u32[]{:S(2)}, u32[]{:S(2)}) collective-permute-start(bf16[128,1024]{1,0:T(8,128)(2,1)} %get-tuple-element.153), channel_id=1, source_target_pairs={{0,8},{8,0},{16,24},{24,16},{1,9},{9,1},{17,25},{25,17},{2,10},{10... | collective-permute-start | bytes 786440 | tf_op jit(solution)/shard_map/ppermute | solution.py:275
  148.7 12.8 %collective-permute-start.38 = (bf16[128,1024]{1,0:T(8,128)(2,1)}, bf16[128,1024]{1,0:T(8,128)(2,1)}, u32[]{:S(2)}, u32[]{:S(2)}) collective-permute-start(bf16[128,1024]{1,0:T(8,128)(2,1)} %get-tuple-element.154), channel_id=1, source_target_pairs={{0,16},{8,24},{16,0},{24,8},{1,17},{9,25},{17,1},{25,9},{2,18},{10... | collective-permute-start | bytes 786440 | tf_op jit(solution)/shard_map/ppermute | solution.py:275
  149.5 12.1 %collective-permute-start.39 = (bf16[128,1024]{1,0:T(8,128)(2,1)}, bf16[128,1024]{1,0:T(8,128)(2,1)}, u32[]{:S(2)}, u32[]{:S(2)}) collective-permute-start(bf16[128,1024]{1,0:T(8,128)(2,1)} %get-tuple-element.155), channel_id=1, source_target_pairs={{0,24},{8,16},{16,8},{24,0},{1,25},{9,17},{17,9},{25,1},{2,26},{10... | collective-permute-start | bytes 786440 | tf_op jit(solution)/shard_map/ppermute | solution.py:275
  152.1 20.8 %collective-permute-start.36 = (bf16[256,1024]{1,0:T(8,128)(2,1)}, bf16[256,1024]{1,0:T(8,128)(2,1)}, u32[]{:S(2)}, u32[]{:S(2)}) collective-permute-start(bf16[256,1024]{1,0:T(8,128)(2,1)} %get-tuple-element.152), channel_id=1, source_target_pairs={{0,1},{1,0},{2,3},{3,2},{4,5},{5,4},{6,7},{7,6},{8,9},{9,8},{10,11... | collective-permute-start | bytes 1572872 | tf_op jit(solution)/shard_map/ppermute | solution.py:33
  163.2 23.8 %collective-permute-start.41 = (bf16[256,1024]{1,0:T(8,128)(2,1)S(1)}, bf16[256,1024]{1,0:T(8,128)(2,1)S(1)}, u32[]{:S(2)}, u32[]{:S(2)}) collective-permute-start(bf16[256,1024]{1,0:T(8,128)(2,1)S(1)} %get-tuple-element.167), channel_id=1, source_target_pairs={{0,1},{1,0},{2,3},{3,2},{4,5},{5,4},{6,7},{7,6},{8,9},{9,8},{10,11... | collective-permute-start | bytes 1572872 | tf_op jit(solution)/shard_map/ppermute | solution.py:33
  174.1 24.8 %collective-permute-start.42 = (bf16[256,1024]{1,0:T(8,128)(2,1)S(1)}, bf16[256,1024]{1,0:T(8,128)(2,1)S(1)}, u32[]{:S(2)}, u32[]{:S(2)}) collective-permute-start(bf16[256,1024]{1,0:T(8,128)(2,1)S(1)} %add_convert_fusion.5), channel_id=1, source_target_pairs={{0,2},{1,3},{2,0},{3,1},{4,6},{5,7},{6,4},{7,5},{8,10},{9,11},{10,... | collective-permute-start | bytes 1572872 | tf_op jit(solution)/shard_map/ppermute | solution.py:33
  179.9 6.5 %collective-permute-start.43 = (f32[2,256]{1,0:T(2,128)S(1)}, f32[2,256]{1,0:T(2,128)S(1)}, u32[]{:S(2)}, u32[]{:S(2)}) collective-permute-start(f32[2,256]{1,0:T(2,128)S(1)} %add.57), channel_id=1, source_target_pairs={{0,4},{4,0},{1,5},{5,1},{2,6},{6,2},{3,7},{7,3},{8,12},{12,8},{9,1... | collective-permute-start | bytes 6152 | tf_op jit(solution)/shard_map/ppermute | solution.py:305
  (26 other events, 130.1 us)

commit v3 on v2

--- a/solution.py
+++ b/solution.py
@@ -111,14 +111,14 @@
     )(*pieces)
 
 
-def join_kernel(n, cap, columns, weighted, *refs):
+def join_kernel(n, cap, columns, weighted, cuts, *refs):
     slot_ref, weight_ref = refs[:2]
     pieces, rest = refs[2 : 2 + columns], refs[2 + columns :]
     held = rest[-1]
     if weighted:
         cots, parts = rest[:n], rest[n : 2 * n]
     else:
-        parts = rest[:n]
+        parts = rest[: n * cuts]
     slots = columns * cap
     top = slot_ref.shape[1]
     for j in range(n):
@@ -146,17 +146,20 @@
                     parts[j][width : width + 16, at : at + width] = jnp.broadcast_to(value, (16, width))
         else:
             pick = functools.reduce(jnp.add, [h.astype(F32) for h in hits]).astype(BF)
-            parts[j][...] = dot(pick, rows, 0, 0).astype(BF)
-
-
-def join_rows(slot, weight, pieces, cap, cots=None):
+            total = dot(pick, rows, 0, 0).astype(BF)
+            width = total.shape[1] // cuts
+            for s in range(cuts):
+                parts[j * cuts + s][...] = total[:, s * width : (s + 1) * width]
+
+
+def join_rows(slot, weight, pieces, cap, cots=None, cuts=1):
     columns, half = len(pieces), pieces[0].shape[1]
     n, top, rows = slot.shape
     weighted = cots is not None
-    outs = [jax.ShapeDtypeStruct((rows + (16 if weighted else 0), half), BF)] * n
+    outs = [jax.ShapeDtypeStruct((rows + (16 if weighted else 0), half // cuts), BF)] * (n * cuts)
     ins = [slot, weight] + list(pieces) + (list(cots) if weighted else [])
     out = pl.pallas_call(
-        functools.partial(join_kernel, n, cap, columns, weighted),
+        functools.partial(join_kernel, n, cap, columns, weighted, cuts),
         out_shape=outs,
         in_specs=[VMEM] * len(ins),
         out_specs=[VMEM] * len(outs),
@@ -358,11 +361,11 @@
     out_sums = dict(enumerate(out_parts))
     reduce_bit(out_sums, 1, line)
     back_last[-1] = after(back_last[-1], *out_sums.values())
-    back_parts_last = join_rows(slot[last], weight[last], back_last, cap)
+    back_parts_last = join_rows(slot[last], weight[last], back_last, cap, cuts=2)
     back_first = exchange(
         [back_pieces[0]] + list(together(*back_pieces[2::2], *back_last[1:])[: columns - 1])
     )
-    moved = to_place(back_parts_last[1], 1, line)
+    moved = [to_place(part, 1, line) for part in back_parts_last[2:]]
 
     d_pre_gate, d_pre_up, tok_mine, tok_other, _ = together(
         d_pre_gate, d_pre_up, tok_mine, tok_other, back_parts_last[0]
@@ -371,10 +374,11 @@
     grad_gate = dot(inbound, d_pre_gate, 0, 0).astype(BF)
     grad_up = dot(inbound, d_pre_up, 0, 0).astype(BF)
 
-    back_first[-1] = after(back_first[-1], grad_gate, grad_up)
+    back_first[-1] = after(back_first[-1], grad_gate)
     back_parts = join_rows(slot[first], weight[first], back_first, cap)
-    moved = after(moved, back_parts[0])
-    back_pair = (back_parts_last[0].astype(F32) + moved.astype(F32)).astype(BF)
+    moved[0] = after(moved[0], grad_gate, grad_up)
+    back_cut = [(k.astype(F32) + m.astype(F32)).astype(BF) for k, m in zip(back_parts_last, moved)]
+    back_pair = back_cut[1]
     activation, cot_mine, cot_other, _ = together(activation, cot_mine, cot_other, back_pair)
     grad_down = dot(activation, full(cot_mine, cot_other), 0, 0).astype(BF)
 
@@ -383,10 +387,15 @@
         reduce_bit(out_sums, bit, line)
     out_total = out_sums[0]
     back_parts[0] = after(back_parts[0], out_total)
-    back_sums = dict(enumerate(back_parts + [back_pair]))
-    for bit in powers(line):
-        reduce_bit(back_sums, bit, line)
-    d_tokens = back_sums[0]
+    if line == 4:
+        beside = to_place(back_parts[1], 1, line).astype(F32)
+        across = jnp.concatenate([to_place(part, 2, line) for part in back_cut], axis=1)
+        d_tokens = (back_parts[0].astype(F32) + beside + across.astype(F32)).astype(BF)
+    else:
+        back_sums = dict(enumerate(back_parts + [jnp.concatenate(back_cut, axis=1)]))
+        for bit in powers(line):
+            reduce_bit(back_sums, bit, line)
+        d_tokens = back_sums[0]
     layer_out = out_total[:tok_rows]
     gate_terms = out_total[tok_rows, : 2 * top * tok_rows].astype(F32).reshape(2, top, tok_rows)
     local_gates = gate_terms[0] + gate_terms[1]

time: 201 us -> 197 us (0.980)
  waiting for transfers between devices: 66.5 us -> 59.7 us
  matrix products: 10.1 us -> 12.4 us
  other arithmetic: 13.4 us -> 15.6 us
    ppermute x15 -> x17, waiting for transfers between devices: 62.2 us -> 54 us  [to_place(): return lax.ppermute(value, 'expert', [(i, i ^ d) for i in range(line)])]
    convert_element_type x1 -> x3, other arithmetic: 1.24 us -> 3.84 us  [the longest x1 2 us: shards(): (back_parts[0].astype(F32) + beside + across.astype(F32)).astype(BF)]
    dot_general x3, matrix products: 10.1 us -> 12.4 us  [dot(): lax.dot_general(a, b, (((ca,), (cb,)), ((), ())), preferred_element_type=...]
    convert_element_type x4 -> x3, other arithmetic: 5.43 us -> 4.35 us  [reduce_bit(): parts[d ^ bit] = kept.astype(moved.dtype)]
    unnamed x61 -> x63, local copies, waits for them, and re-layouts: 7.02 us -> 6 us
    ppermute x15 -> x17, starting transfers between devices: 26.6 us -> 27.5 us  [to_place(): return lax.ppermute(value, 'expert', [(i, i ^ d) for i in range(line)])]
    select_n x2 -> x1, other arithmetic: 4.42 us -> 5.12 us  [full(): jnp.where(first, mine, other)]
  transfers between devices with their start and end apart: 44 -> 46, of which waited for: 14 -> 15; matrix products, arithmetic and copies ran while one was open for 12% -> 14% of each run, Pallas kernels for 22% -> 21%
where the time goes in v3:
time: 197 us; the launch traced here: 196 us
  waiting for transfers between devices  59.7 us (30%)
  starting transfers between devices  57 us (29%)
  Pallas kernels  42.6 us (22%)
  other arithmetic  15.6 us (8%)
  matrix products  12.4 us (6%)
  local copies, waits for them, and re-layouts  7.21 us (4%)
    ppermute x17, waiting for transfers between devices, to_place(): return lax.ppermute(value, 'expert', [(i, i ^ d) for i in range(line)])  54 us
    ppermute x24, starting transfers between devices, exchange(): lax.ppermute(pieces[d], 'path', [(i, i ^ d) for i in range(columns)])  29.3 us
    ppermute x17, starting transfers between devices, to_place(): return lax.ppermute(value, 'expert', [(i, i ^ d) for i in range(line)])  27.5 us
    pallas_call x2, Pallas kernels, by_rows(): pl.pallas_call(functools.partial(kernel, half), grid=(total // block,), o...  22.4 us
    dot_general x3, matrix products, dot(): lax.dot_general(a, b, (((ca,), (cb,)), ((), ())), preferred_element_type=...  12.4 us
    pallas_call x4, Pallas kernels, join_rows(): pl.pallas_call(functools.partial(join_kernel, n, cap, columns, weighted,...  7.24 us
    unnamed x63, local copies, waits for them, and re-layouts  6 us
    ppermute x24, waiting for transfers between devices, exchange(): lax.ppermute(pieces[d], 'path', [(i, i ^ d) for i in range(columns)])  5.58 us
  transfers between devices with their start and end apart: 46, of which 15 were waited for; matrix products, arithmetic and copies ran while one was open for 14% of the time, Pallas kernels for 21%

profile of v3, /device:TPU:0, one launch (start us, length us, event | category | flops | bytes accessed | tf_op | source)
XLA Modules:
  0.0 195.6 jit_solution(15551808782168937292)
XLA Ops:
  0.6 4.1 %collective-permute-start.3 = (bf16[256,1024]{1,0:T(8,128)(2,1)}, bf16[256,1024]{1,0:T(8,128)(2,1)S(1)}, u32[]{:S(2)}, u32[]{:S(2)}) collective-permute-start(bf16[256,1024]{1,0:T(8,128)(2,1)} %refs_2_.1), channel_id=1, source_target_pairs={{0,2},{1,3},{2,0},{3,1},{4,6},{5,7},{6,4},{7,5},{8,10},{9,11},{10,... | collective-permute-start | bytes 1572872 | tf_op jit(solution)/shard_map/ppermute | solution.py:33
  4.7 1.6 collective-permute-start.4
  9.1 1.9 collective-permute-start.1
  11.0 2.5 %collective-permute-start = (f32[4,256]{1,0:T(4,128)S(1)}, f32[4,256]{1,0:T(4,128)S(1)}, u32[]{:S(2)}, u32[]{:S(2)}) collective-permute-start(f32[4,256]{1,0:T(4,128)S(1)} %get-tuple-element.183), channel_id=1, source_target_pairs={{0,1},{1,0},{2,3},{3,2},{4,5},{5,4},{6,7},{7,6},{8,9},{9,8},{10,11... | collective-permute-start | bytes 12296 | tf_op jit(solution)/shard_map/ppermute | solution.py:33
  13.5 15.9 %collective-permute-done.2 = f32[4,256]{1,0:T(4,128)S(1)} collective-permute-done((f32[4,256]{1,0:T(4,128)S(1)}, f32[4,256]{1,0:T(4,128)S(1)}, u32[]{:S(2)}, u32[]{:S(2)}) %collective-permute-start.2) | collective-permute-done | bytes 4128 | tf_op jit(solution)/shard_map/ppermute | solution.py:33
  32.0 1.6 collective-permute-start.6
  33.6 1.5 collective-permute-start.7
  35.6 2.4 %collective-permute-start.12 = (bf16[256,1024]{1,0:T(8,128)(2,1)S(1)}, bf16[256,1024]{1,0:T(8,128)(2,1)}, u32[]{:S(2)}, u32[]{:S(2)}) collective-permute-start(bf16[256,1024]{1,0:T(8,128)(2,1)S(1)} %copy-done.4), channel_id=1, source_target_pairs={{0,2},{1,3},{2,0},{3,1},{4,6},{5,7},{6,4},{7,5},{8,10},{9,11},{10,... | collective-permute-start | bytes 1572872 | tf_op jit(solution)/shard_map/ppermute | solution.py:33
  38.0 10.8 %collective-permute-done.5.refs_2_ = bf16[256,1024]{1,0:T(8,128)(2,1)S(1)} collective-permute-done((bf16[256,1024]{1,0:T(8,128)(2,1)S(1)}, bf16[256,1024]{1,0:T(8,128)(2,1)S(1)}, u32[]{:S(2)}, u32[]{:S(2)}) %collective-permute-start.5) | collective-permute-done | bytes 524320 | tf_op jit(solution)/shard_map/ppermute | solution.py:33
  48.8 2.6 %collective-permute-done.7.refs_4_ = bf16[192,1024]{1,0:T(8,128)(2,1)S(1)} collective-permute-done((bf16[192,1024]{1,0:T(8,128)(2,1)S(1)}, bf16[192,1024]{1,0:T(8,128)(2,1)S(1)}, u32[]{:S(2)}, u32[]{:S(2)}) %collective-permute-start.7) | collective-permute-done | bytes 393248 | tf_op jit(solution)/shard_map/ppermute | solution.py:278
  51.8 1.6 collective-permute-start.11
  53.3 1.5 collective-permute-start.9
  55.3 5.1 %collective-permute-done.12.refs_4_.refs_8_ = bf16[256,1024]{1,0:T(8,128)(2,1)} collective-permute-done((bf16[256,1024]{1,0:T(8,128)(2,1)S(1)}, bf16[256,1024]{1,0:T(8,128)(2,1)}, u32[]{:S(2)}, u32[]{:S(2)}) %collective-permute-start.12) | collective-permute-done | bytes 524320 | tf_op jit(solution)/shard_map/ppermute | solution.py:33
  60.4 4.6 %collective-permute-done.13.refs_3_.refs_7_ = bf16[256,1024]{1,0:T(8,128)(2,1)S(1)} collective-permute-done((bf16[256,1024]{1,0:T(8,128)(2,1)S(1)}, bf16[256,1024]{1,0:T(8,128)(2,1)S(1)}, u32[]{:S(2)}, u32[]{:S(2)}) %collective-permute-start.13) | collective-permute-done | bytes 524320 | tf_op jit(solution)/shard_map/ppermute | solution.py:33
  65.9 2.8 %pick_scaled.2 = (bf16[192,1024]{1,0:T(8,128)(2,1)S(1)}, bf16[192,1024]{1,0:T(8,128)(2,1)}, bf16[192,1024]{1,0:T(8,128)(2,1)}, bf16[192,1024]{1,0:T(8,128)(2,1)}) custom-call(s32[3,2,256]{2,1,0:T(2,128)S(1)} %slice.76.refs_0_, f32[3,2,256]{2,1,0:T(2,128)S(1)} %pad_maximum_fusion.4.refs_1_, bf16[256,1024]{1,0:T(8,128)(2,1)S(1)} %copy-done.4, ...), custom_call_target="tpu_custom_call" | custom-call | tf_op jit(solution)/shard_map/pick_scaled/pallas_call | solution.py:80
  68.7 1.5 collective-permute-start.17
  70.2 1.5 collective-permute-start.19
  72.2 1.4 copy-done.9
  73.6 10.8 %ahead.1 = (f32[1024,384]{1,0:T(8,128)S(1)}, f32[1024,384]{1,0:T(8,128)S(1)}, bf16[1024,384]{1,0:T(8,128)(2,1)S(1)}, bf16[1024,1024]{1,0:T(8,128)(2,1)}, bf16[1024,1024]{1,0:T(8,128)(2,1)}) custom-call(s32[1]{0:T(128)} %bitcast.6.head_ref, bf16[1024,1024]{1,0:T(8,128)(2,1)} %copy-done, bf16[1024,1024]{1,0:T(8,128)(2,1)} %collective-permute-done.14.other_ref, ...), custom_call_target="tpu_custom_call" | custom-call | flops 399999991808 | bytes 41943040 | tf_op jit(solution)/shard_map/ahead/pallas_call | solution.py:221
  85.4 1.6 pick_scaled.3
  87.0 1.6 collective-permute-start.18
  88.5 1.5 collective-permute-start.20
  90.1 2.3 %collective-permute-start.22 = (bf16[64,1024]{1,0:T(8,128)(2,1)S(1)}, bf16[64,1024]{1,0:T(8,128)(2,1)S(1)}, u32[]{:S(2)}, u32[]{:S(2)}) collective-permute-start(bf16[64,1024]{1,0:T(8,128)(2,1)S(1)} %get-tuple-element.122), channel_id=1, source_target_pairs={{0,24},{8,16},{16,8},{24,0},{1,25},{9,17},{17,9},{25,1},{2,26},{10... | collective-permute-start | bytes 393224 | tf_op jit(solution)/shard_map/ppermute | solution.py:278
  92.3 2.7 %deal.2 = (bf16[192,1024]{1,0:T(8,128)(2,1)S(1)}, bf16[64,1024]{1,0:T(8,128)(2,1)S(1)}, bf16[192,1024]{1,0:T(8,128)(2,1)}, bf16[64,1024]{1,0:T(8,128)(2,1)S(1)},...) custom-call(bf16[1024,1024]{1,0:T(8,128)(2,1)S(1)} %copy-done.2, ...), custom_call_target="tpu_custom_call" | custom-call | tf_op jit(solution)/shard_map/deal/pallas_call | solution.py:244
  97.0 1.5 collective-permute-start.28
  98.5 2.8 %stack.32.mine_ref = bf16[1024,1024]{1,0:T(8,128)(2,1)} custom-call(bf16[192,1024]{1,0:T(8,128)(2,1)S(1)} %get-tuple-element.106.refs_0_, bf16[64,1024]{1,0:T(8,128)(2,1)S(1)} %get-tuple-element.111.refs_1_, bf16[192,1024]{1,0:T(8,128)(2,1)} %collective-permute-done.17.refs_2_, bf16[64,1024]{1,0:T(8,128)(2,1)S(1)} %collective-permute-done.18.refs_3_, ...), custom_call_target="tpu_custom_call" | custom-call | tf_op jit(solution)/shard_map/stack/pallas_call | solution.py:103
  103.0 1.8 collective-permute-start.25
  104.8 2.5 %join_weighted.2 = bf16[272,1024]{1,0:T(8,128)(2,1)} custom-call(s32[1,2,256]{2,1,0:T(2,128)S(1)} %copy-done.6, f32[1,2,256]{2,1,0:T(2,128)S(1)} %copy-done.8, bf16[64,1024]{1,0:T(8,128)(2,1)S(1)} %get-tuple-element.127.refs_2_, bf16[64,1024]{1,0:T(8,128)(2,1)S(1)} %collective-permute-done.27.refs_3_, bf16[64,1024]{1,0:T(8,128)(2,1)S(1)} %collective-permute-done.28.refs_4_, ...), custom_call_target="tpu_custom_call" | custom-call | flops 399999991808 | bytes 41943040 | tf_op jit(solution)/shard_map/join_weighted/pallas_call | solution.py:161
  107.3 1.4 collective-permute-start.35
  108.7 11.6 %back.1 = (bf16[1024,384]{1,0:T(8,128)(2,1)S(1)}, bf16[1024,384]{1,0:T(8,128)(2,1)S(1)}, bf16[1024,1024]{1,0:T(8,128)(2,1)}, bf16[1024,1024]{1,0:T(8,128)(2,1)}) custom-call(s32[1]{0:T(128)} %bitcast.6.head_ref, bf16[1024,1024]{1,0:T(8,128)(2,1)} %stack.32.mine_ref, bf16[1024,1024]{1,0:T(8,128)(2,1)} %collective-permute-done.26.other_ref, ...), custom_call_target="tpu_custom_call" | custom-call | flops 399999991808 | bytes 41943040 | tf_op jit(solution)/shard_map/back/pallas_call | solution.py:221
  122.1 3.1 %join_weighted.3 = (bf16[272,1024]{1,0:T(8,128)(2,1)S(1)}, bf16[272,1024]{1,0:T(8,128)(2,1)S(1)}, bf16[272,1024]{1,0:T(8,128)(2,1)S(1)}) custom-call(s32[3,2,256]{2,1,0:T(2,128)S(1)} %slice.76.refs_0_, f32[3,2,256]{2,1,0:T(2,128)S(1)} %pad_maximum_fusion.4.refs_1_, bf16[192,1024]{1,0:T(8,128)(2,1)S(1)} %get-tuple-element.123.refs_2_, ...), custom_call_target="tpu_custom_call" | custom-call | flops 399999991808 | bytes 41943040 | tf_op jit(solution)/shard_map/join_weighted/pallas_call | solution.py:161
  126.6 2.1 %deal.3 = (bf16[128,1024]{1,0:T(8,128)(2,1)S(1)}, bf16[128,1024]{1,0:T(8,128)(2,1)S(1)}, bf16[128,1024]{1,0:T(8,128)(2,1)S(1)}, bf16[128,1024]{1,0:T(8,128)(2,1)...) custom-call(bf16[1024,1024]{1,0:T(8,128)(2,1)S(1)} %copy-done.1, ...), custom_call_target="tpu_custom_call" | custom-call | tf_op jit(solution)/shard_map/deal/pallas_call | solution.py:244
  128.6 1.5 collective-permute-start.32
  130.6 1.6 collective-permute-start.34
  132.2 2.1 %add_convert_fusion.1 = bf16[272,1024]{1,0:T(8,128)(2,1)} fusion(bf16[272,1024]{1,0:T(8,128)(2,1)} %collective-permute-done.35, bf16[272,1024]{1,0:T(8,128)(2,1)S(1)} %get-tuple-element.151), kind=kLoop, calls=%fused_computation.14 | loop fusion | flops 1114112 | bytes 1671168 | tf_op jit(solution)/shard_map/convert_element_type | solution.py:53
  134.3 6.1 %collective-permute-done.31 = bf16[272,1024]{1,0:T(8,128)(2,1)S(1)} collective-permute-done((bf16[272,1024]{1,0:T(8,128)(2,1)S(1)}, bf16[272,1024]{1,0:T(8,128)(2,1)S(1)}, u32[]{:S(2)}, u32[]{:S(2)}) %collective-permute-start.31) | collective-permute-done | bytes 557088 | tf_op jit(solution)/shard_map/ppermute | solution.py:33
  145.7 4.9 %collective-permute-start.37 = (bf16[272,1024]{1,0:T(8,128)(2,1)}, bf16[272,1024]{1,0:T(8,128)(2,1)}, u32[]{:S(2)}, u32[]{:S(2)}) collective-permute-start(bf16[272,1024]{1,0:T(8,128)(2,1)} %add_convert_fusion.1), channel_id=1, source_target_pairs={{0,2},{1,3},{2,0},{3,1},{4,6},{5,7},{6,4},{7,5},{8,10},{9,11},{10,... | collective-permute-start | bytes 1671176 | tf_op jit(solution)/shard_map/ppermute | solution.py:33
  152.3 1.7 collective-permute-start.40
  154.1 4.7 %collective-permute-done.36 = bf16[256,512]{1,0:T(8,128)(2,1)S(1)} collective-permute-done((bf16[256,512]{1,0:T(8,128)(2,1)S(1)}, bf16[256,512]{1,0:T(8,128)(2,1)S(1)}, u32[]{:S(2)}, u32[]{:S(2)}) %collective-permute-start.36) | collective-permute-done | bytes 262176 | tf_op jit(solution)/shard_map/ppermute | solution.py:33
  159.6 5.1 %broadcast_select_fusion.1 = (bf16[1024,1024]{1,0:T(8,128)(2,1)}, bf16[1024,1024]{1,0:T(8,128)(2,1)}, bf16[1024,1024]{1,0:T(8,128)(2,1)S(1)}, bf16[1024,1024]{1,0:T(8,128)(2,1)S(1)}) fusion(bf16[1024,1024]{1,0:T(8,128)(2,1)} %stack.32.mine_ref, bf16[1024,1024]{1,0:T(8,128)(2,1)} %collective-permute-done.26.other_ref, pred[]{:T(512)S(6)} %eq.34, ...), kind=kLoop, calls=%fused_computation.10 | loop fusion | flops 4194304 | bytes 16777216 | tf_op jit(solution)/shard_map/jit(_where)/select_n | solution.py:313
  164.7 3.6 %convolution_convert_fusion.1 = bf16[2048,384]{1,0:T(8,128)(2,1)} fusion(bf16[1024,384]{1,0:T(8,128)(2,1)S(1)} %copy-done.15, bf16[1024,1024]{1,0:T(8,128)(2,1)S(1)} %get-tuple-element.184, bf16[1024,1024]{1,0:T(8,128)(2,1)S(1)} %get-tuple-element.185), kind=kOutput, calls=%fused_computation.7 | convolution fusion | flops 1619787776 | bytes 6553600 | tf_op jit(solution)/shard_map/dot_general | solution.py:22
  169.1 2.0 %collective-permute-start.41 = (bf16[256,1024]{1,0:T(8,128)(2,1)S(1)}, bf16[256,1024]{1,0:T(8,128)(2,1)S(1)}, u32[]{:S(2)}, u32[]{:S(2)}) collective-permute-start(bf16[256,1024]{1,0:T(8,128)(2,1)S(1)} %get-tuple-element.168), channel_id=1, source_target_pairs={{0,1},{1,0},{2,3},{3,2},{4,5},{5,4},{6,7},{7,6},{8,9},{9,8},{10,11... | collective-permute-start | bytes 1572872 | tf_op jit(solution)/shard_map/ppermute | solution.py:33
  171.0 3.6 %convolution_convert_fusion = bf16[2048,384]{1,0:T(8,128)(2,1)} fusion(bf16[1024,384]{1,0:T(8,128)(2,1)S(1)} %copy-done.13, bf16[1024,1024]{1,0:T(8,128)(2,1)S(1)} %copy-done.18, bf16[1024,1024]{1,0:T(8,128)(2,1)S(1)} %copy-done.20), kind=kOutput, calls=%fused_computation.6 | convolution fusion | flops 1619787776 | bytes 6553600 | tf_op jit(solution)/shard_map/dot_general | solution.py:22
  175.7 2.9 %collective-permute-start.43 = (bf16[256,512]{1,0:T(8,128)(2,1)S(1)}, bf16[256,512]{1,0:T(8,128)(2,1)S(1)}, u32[]{:S(2)}, u32[]{:S(2)}) collective-permute-start(bf16[256,512]{1,0:T(8,128)(2,1)S(1)} %add_convert_fusion.4), channel_id=1, source_target_pairs={{0,2},{1,3},{2,0},{3,1},{4,6},{5,7},{6,4},{7,5},{8,10},{9,11},{10,... | collective-permute-start | bytes 786440 | tf_op jit(solution)/shard_map/ppermute | solution.py:33
  178.7 3.4 %collective-permute-done.37 = bf16[272,1024]{1,0:T(8,128)(2,1)} collective-permute-done((bf16[272,1024]{1,0:T(8,128)(2,1)}, bf16[272,1024]{1,0:T(8,128)(2,1)}, u32[]{:S(2)}, u32[]{:S(2)}) %collective-permute-start.37) | collective-permute-done | bytes 557088 | tf_op jit(solution)/shard_map/ppermute | solution.py:33
  183.4 5.2 %fusion.7 = bf16[1,384,2048]{2,1,0:T(8,128)(2,1)} fusion(bf16[1024,384]{1,0:T(8,128)(2,1)S(1)} %copy-done.11, bf16[1024,1024]{1,0:T(8,128)(2,1)} %get-tuple-element.177, bf16[1024,1024]{1,0:T(8,128)(2,1)} %get-tuple-element.176), kind=kOutput, calls=%fused_computation.8 | convolution fusion | flops 1619787776 | bytes 6553600 | tf_op jit(solution)/shard_map/dot_general | solution.py:22
  190.1 2.5 %collective-permute-done.43 = bf16[256,512]{1,0:T(8,128)(2,1)S(1)} collective-permute-done((bf16[256,512]{1,0:T(8,128)(2,1)S(1)}, bf16[256,512]{1,0:T(8,128)(2,1)S(1)}, u32[]{:S(2)}, u32[]{:S(2)}) %collective-permute-start.43) | collective-permute-done | bytes 262176 | tf_op jit(solution)/shard_map/ppermute | solution.py:33
  193.6 2.0 %add_convert_fusion.3 = bf16[256,1024]{1,0:T(8,128)(2,1)} fusion(bf16[256,1024]{1,0:T(8,128)(2,1)S(1)} %collective-permute-done.41, bf16[256,1024]{1,0:T(8,128)(2,1)S(1)} %get-tuple-element.167, bf16[256,512]{1,0:T(8,128)(2,1)} %collective-permute-done.44, bf16[256,512]{1,0:T(8,128)(2,1)S(1)} %collective-permute-done.43), kind=kLoop, calls=%fused_computation.16 | loop fusion | flops 2359296 | bytes 2097152 | tf_op jit(solution)/shard_map/convert_element_type | solution.py:393
  (151 shorter events, 29.7 us)
Async XLA Ops:
  0.6 35.0 %copy-start.4 = (bf16[256,1024]{1,0:T(8,128)(2,1)S(1)}, bf16[256,1024]{1,0:T(8,128)(2,1)}, u32[]{:S(2)}) copy-start(bf16[256,1024]{1,0:T(8,128)(2,1)} %refs_6_) | copy-start | bytes 1572868
  0.6 28.8 %collective-permute-start.3 = (bf16[256,1024]{1,0:T(8,128)(2,1)}, bf16[256,1024]{1,0:T(8,128)(2,1)S(1)}, u32[]{:S(2)}, u32[]{:S(2)}) collective-permute-start(bf16[256,1024]{1,0:T(8,128)(2,1)} %refs_2_.1), channel_id=1, source_target_pairs={{0,2},{1,3},{2,0},{3,1},{4,6},{5,7},{6,4},{7,5},{8,10},{9,11},{10,... | collective-permute-start | bytes 1572872 | tf_op jit(solution)/shard_map/ppermute | solution.py:33
  4.7 24.7 %collective-permute-start.4 = (bf16[256,1024]{1,0:T(8,128)(2,1)}, bf16[256,1024]{1,0:T(8,128)(2,1)S(1)}, u32[]{:S(2)}, u32[]{:S(2)}) collective-permute-start(bf16[256,1024]{1,0:T(8,128)(2,1)} %refs_2_.1), channel_id=1, source_target_pairs={{0,1},{1,0},{2,3},{3,2},{4,5},{5,4},{6,7},{7,6},{8,9},{9,8},{10,11... | collective-permute-start | bytes 1572872 | tf_op jit(solution)/shard_map/ppermute | solution.py:33
  9.1 20.3 %collective-permute-start.2 = (f32[4,256]{1,0:T(4,128)S(1)}, f32[4,256]{1,0:T(4,128)S(1)}, u32[]{:S(2)}, u32[]{:S(2)}) collective-permute-start(f32[4,256]{1,0:T(4,128)S(1)} %get-tuple-element.183), channel_id=1, source_target_pairs={{0,3},{1,2},{2,1},{3,0},{4,7},{5,6},{6,5},{7,4},{8,11},{9,10},{10,... | collective-permute-start | bytes 12296 | tf_op jit(solution)/shard_map/ppermute | solution.py:33
  9.1 20.3 %collective-permute-start.1 = (f32[4,256]{1,0:T(4,128)S(1)}, f32[4,256]{1,0:T(4,128)S(1)}, u32[]{:S(2)}, u32[]{:S(2)}) collective-permute-start(f32[4,256]{1,0:T(4,128)S(1)} %get-tuple-element.183), channel_id=1, source_target_pairs={{0,2},{1,3},{2,0},{3,1},{4,6},{5,7},{6,4},{7,5},{8,10},{9,11},{10,... | collective-permute-start | bytes 12296 | tf_op jit(solution)/shard_map/ppermute | solution.py:33
  11.0 18.4 %collective-permute-start = (f32[4,256]{1,0:T(4,128)S(1)}, f32[4,256]{1,0:T(4,128)S(1)}, u32[]{:S(2)}, u32[]{:S(2)}) collective-permute-start(f32[4,256]{1,0:T(4,128)S(1)} %get-tuple-element.183), channel_id=1, source_target_pairs={{0,1},{1,0},{2,3},{3,2},{4,5},{5,4},{6,7},{7,6},{8,9},{9,8},{10,11... | collective-permute-start | bytes 12296 | tf_op jit(solution)/shard_map/ppermute | solution.py:33
  29.4 35.6 %copy-start.29 = (f32[4,256]{1,0:T(4,128)}, f32[4,256]{1,0:T(4,128)S(1)}, u32[]{:S(2)}) copy-start(f32[4,256]{1,0:T(4,128)S(1)} %collective-permute-done.2) | copy-start | bytes 12292
  29.5 19.3 %collective-permute-start.5 = (bf16[256,1024]{1,0:T(8,128)(2,1)S(1)}, bf16[256,1024]{1,0:T(8,128)(2,1)S(1)}, u32[]{:S(2)}, u32[]{:S(2)}) collective-permute-start(bf16[256,1024]{1,0:T(8,128)(2,1)S(1)} %collective-permute-done.3.refs_4_), channel_id=1, source_target_pairs={{0,1},{1,0},{2,3},{3,2},{4,5},{5,4},{6,7},{7,6},{8,9},{9,8},{10,11... | collective-permute-start | bytes 1572872 | tf_op jit(solution)/shard_map/ppermute | solution.py:33
  32.0 16.8 %collective-permute-start.6 = (bf16[192,1024]{1,0:T(8,128)(2,1)S(1)}, bf16[192,1024]{1,0:T(8,128)(2,1)S(1)}, u32[]{:S(2)}, u32[]{:S(2)}) collective-permute-start(bf16[192,1024]{1,0:T(8,128)(2,1)S(1)} %get-tuple-element.94), channel_id=1, source_target_pairs={{0,8},{8,0},{16,24},{24,16},{1,9},{9,1},{17,25},{25,17},{2,10},{10... | collective-permute-start | bytes 1179656 | tf_op jit(solution)/shard_map/ppermute | solution.py:278
  33.6 17.8 %collective-permute-start.7 = (bf16[192,1024]{1,0:T(8,128)(2,1)S(1)}, bf16[192,1024]{1,0:T(8,128)(2,1)S(1)}, u32[]{:S(2)}, u32[]{:S(2)}) collective-permute-start(bf16[192,1024]{1,0:T(8,128)(2,1)S(1)} %get-tuple-element.95), channel_id=1, source_target_pairs={{0,16},{8,24},{16,0},{24,8},{1,17},{9,25},{17,1},{25,9},{2,18},{10... | collective-permute-start | bytes 1179656 | tf_op jit(solution)/shard_map/ppermute | solution.py:278
  35.1 16.3 %collective-permute-start.8 = (bf16[192,1024]{1,0:T(8,128)(2,1)S(1)}, bf16[192,1024]{1,0:T(8,128)(2,1)S(1)}, u32[]{:S(2)}, u32[]{:S(2)}) collective-permute-start(bf16[192,1024]{1,0:T(8,128)(2,1)S(1)} %get-tuple-element.96), channel_id=1, source_target_pairs={{0,24},{8,16},{16,8},{24,0},{1,25},{9,17},{17,9},{25,1},{2,26},{10... | collective-permute-start | bytes 1179656 | tf_op jit(solution)/shard_map/ppermute | solution.py:278
  35.6 24.8 %collective-permute-start.12 = (bf16[256,1024]{1,0:T(8,128)(2,1)S(1)}, bf16[256,1024]{1,0:T(8,128)(2,1)}, u32[]{:S(2)}, u32[]{:S(2)}) collective-permute-start(bf16[256,1024]{1,0:T(8,128)(2,1)S(1)} %copy-done.4), channel_id=1, source_target_pairs={{0,2},{1,3},{2,0},{3,1},{4,6},{5,7},{6,4},{7,5},{8,10},{9,11},{10,... | collective-permute-start | bytes 1572872 | tf_op jit(solution)/shard_map/ppermute | solution.py:33
  48.8 16.2 %collective-permute-start.13 = (bf16[256,1024]{1,0:T(8,128)(2,1)S(1)}, bf16[256,1024]{1,0:T(8,128)(2,1)S(1)}, u32[]{:S(2)}, u32[]{:S(2)}) collective-permute-start(bf16[256,1024]{1,0:T(8,128)(2,1)S(1)} %copy-done.4), channel_id=1, source_target_pairs={{0,1},{1,0},{2,3},{3,2},{4,5},{5,4},{6,7},{7,6},{8,9},{9,8},{10,11... | collective-permute-start | bytes 1572872 | tf_op jit(solution)/shard_map/ppermute | solution.py:33
  51.8 8.6 %collective-permute-start.11 = (bf16[64,1024]{1,0:T(8,128)(2,1)S(1)}, bf16[64,1024]{1,0:T(8,128)(2,1)S(1)}, u32[]{:S(2)}, u32[]{:S(2)}) collective-permute-start(bf16[64,1024]{1,0:T(8,128)(2,1)S(1)} %get-tuple-element.101), channel_id=1, source_target_pairs={{0,24},{8,16},{16,8},{24,0},{1,25},{9,17},{17,9},{25,1},{2,26},{10... | collective-permute-start | bytes 393224 | tf_op jit(solution)/shard_map/ppermute | solution.py:278
  53.3 11.6 %collective-permute-start.9 = (bf16[64,1024]{1,0:T(8,128)(2,1)S(1)}, bf16[64,1024]{1,0:T(8,128)(2,1)S(1)}, u32[]{:S(2)}, u32[]{:S(2)}) collective-permute-start(bf16[64,1024]{1,0:T(8,128)(2,1)S(1)} %get-tuple-element.99), channel_id=1, source_target_pairs={{0,8},{8,0},{16,24},{24,16},{1,9},{9,1},{17,25},{25,17},{2,10},{10... | collective-permute-start | bytes 393224 | tf_op jit(solution)/shard_map/ppermute | solution.py:278
  54.8 10.2 %collective-permute-start.10 = (bf16[64,1024]{1,0:T(8,128)(2,1)S(1)}, bf16[64,1024]{1,0:T(8,128)(2,1)S(1)}, u32[]{:S(2)}, u32[]{:S(2)}) collective-permute-start(bf16[64,1024]{1,0:T(8,128)(2,1)S(1)} %get-tuple-element.100), channel_id=1, source_target_pairs={{0,16},{8,24},{16,0},{24,8},{1,17},{9,25},{17,1},{25,9},{2,18},{10... | collective-permute-start | bytes 393224 | tf_op jit(solution)/shard_map/ppermute | solution.py:278
  65.1 7.1 %collective-permute-start.14 = (bf16[1024,1024]{1,0:T(8,128)(2,1)S(1)}, bf16[1024,1024]{1,0:T(8,128)(2,1)}, u32[]{:S(2)}, u32[]{:S(2)}) collective-permute-start(bf16[1024,1024]{1,0:T(8,128)(2,1)S(1)} %stack.31.mine_ref), channel_id=1, source_target_pairs={{0,4},{4,0},{1,5},{5,1},{2,6},{6,2},{3,7},{7,3},{8,12},{12,8},{9,1... | collective-permute-start | bytes 6291464 | tf_op jit(solution)/shard_map/ppermute | solution.py:308
  65.2 20.1 %collective-permute-start.16 = (bf16[256,1024]{1,0:T(8,128)(2,1)}, bf16[256,1024]{1,0:T(8,128)(2,1)}, u32[]{:S(2)}, u32[]{:S(2)}) collective-permute-start(bf16[256,1024]{1,0:T(8,128)(2,1)} %collective-permute-done.12.refs_4_.refs_8_), channel_id=1, source_target_pairs={{0,1},{1,0},{2,3},{3,2},{4,5},{5,4},{6,7},{7,6},{8,9},{9,8},{10,11... | collective-permute-start | bytes 1572872 | tf_op jit(solution)/shard_map/ppermute | solution.py:33
  68.7 19.8 %collective-permute-start.17 = (bf16[192,1024]{1,0:T(8,128)(2,1)}, bf16[192,1024]{1,0:T(8,128)(2,1)}, u32[]{:S(2)}, u32[]{:S(2)}) collective-permute-start(bf16[192,1024]{1,0:T(8,128)(2,1)} %get-tuple-element.117), channel_id=1, source_target_pairs={{0,8},{8,0},{16,24},{24,16},{1,9},{9,1},{17,25},{25,17},{2,10},{10... | collective-permute-start | bytes 1179656 | tf_op jit(solution)/shard_map/ppermute | solution.py:278
  70.2 24.8 %collective-permute-start.19 = (bf16[192,1024]{1,0:T(8,128)(2,1)}, bf16[192,1024]{1,0:T(8,128)(2,1)}, u32[]{:S(2)}, u32[]{:S(2)}) collective-permute-start(bf16[192,1024]{1,0:T(8,128)(2,1)} %get-tuple-element.119), channel_id=1, source_target_pairs={{0,16},{8,24},{16,0},{24,8},{1,17},{9,25},{17,1},{25,9},{2,18},{10... | collective-permute-start | bytes 1179656 | tf_op jit(solution)/shard_map/ppermute | solution.py:278
  71.7 24.0 %collective-permute-start.21 = (bf16[192,1024]{1,0:T(8,128)(2,1)}, bf16[192,1024]{1,0:T(8,128)(2,1)}, u32[]{:S(2)}, u32[]{:S(2)}) collective-permute-start(bf16[192,1024]{1,0:T(8,128)(2,1)} %get-tuple-element.121), channel_id=1, source_target_pairs={{0,24},{8,16},{16,8},{24,0},{1,25},{9,17},{17,9},{25,1},{2,26},{10... | collective-permute-start | bytes 1179656 | tf_op jit(solution)/shard_map/ppermute | solution.py:278
  85.4 4.7 %collective-permute-start.15 = (bf16[1024,1024]{1,0:T(8,128)(2,1)}, bf16[1024,1024]{1,0:T(8,128)(2,1)}, u32[]{:S(2)}, u32[]{:S(2)}) collective-permute-start(bf16[1024,1024]{1,0:T(8,128)(2,1)} %get-tuple-element.109), channel_id=1, source_target_pairs={{0,4},{4,0},{1,5},{5,1},{2,6},{6,2},{3,7},{7,3},{8,12},{12,8},{9,1... | collective-permute-start | bytes 6291464 | tf_op jit(solution)/shard_map/ppermute | solution.py:308
  87.0 10.0 %collective-permute-start.18 = (bf16[64,1024]{1,0:T(8,128)(2,1)S(1)}, bf16[64,1024]{1,0:T(8,128)(2,1)S(1)}, u32[]{:S(2)}, u32[]{:S(2)}) collective-permute-start(bf16[64,1024]{1,0:T(8,128)(2,1)S(1)} %get-tuple-element.118), channel_id=1, source_target_pairs={{0,8},{8,0},{16,24},{24,16},{1,9},{9,1},{17,25},{25,17},{2,10},{10... | collective-permute-start | bytes 393224 | tf_op jit(solution)/shard_map/ppermute | solution.py:278
  88.5 10.0 %collective-permute-start.20 = (bf16[64,1024]{1,0:T(8,128)(2,1)S(1)}, bf16[64,1024]{1,0:T(8,128)(2,1)S(1)}, u32[]{:S(2)}, u32[]{:S(2)}) collective-permute-start(bf16[64,1024]{1,0:T(8,128)(2,1)S(1)} %get-tuple-element.120), channel_id=1, source_target_pairs={{0,16},{8,24},{16,0},{24,8},{1,17},{9,25},{17,1},{25,9},{2,18},{10... | collective-permute-start | bytes 393224 | tf_op jit(solution)/shard_map/ppermute | solution.py:278
  90.1 8.5 %collective-permute-start.22 = (bf16[64,1024]{1,0:T(8,128)(2,1)S(1)}, bf16[64,1024]{1,0:T(8,128)(2,1)S(1)}, u32[]{:S(2)}, u32[]{:S(2)}) collective-permute-start(bf16[64,1024]{1,0:T(8,128)(2,1)S(1)} %get-tuple-element.122), channel_id=1, source_target_pairs={{0,24},{8,16},{16,8},{24,0},{1,25},{9,17},{17,9},{25,1},{2,26},{10... | collective-permute-start | bytes 393224 | tf_op jit(solution)/shard_map/ppermute | solution.py:278
  95.0 7.3 %collective-permute-start.29 = (bf16[64,1024]{1,0:T(8,128)(2,1)S(1)}, bf16[64,1024]{1,0:T(8,128)(2,1)S(1)}, u32[]{:S(2)}, u32[]{:S(2)}) collective-permute-start(bf16[64,1024]{1,0:T(8,128)(2,1)S(1)} %get-tuple-element.130), channel_id=1, source_target_pairs={{0,24},{8,16},{16,8},{24,0},{1,25},{9,17},{17,9},{25,1},{2,26},{10... | collective-permute-start | bytes 393224 | tf_op jit(solution)/shard_map/ppermute | solution.py:278
  95.7 7.3 %collective-permute-start.27 = (bf16[64,1024]{1,0:T(8,128)(2,1)S(1)}, bf16[64,1024]{1,0:T(8,128)(2,1)S(1)}, u32[]{:S(2)}, u32[]{:S(2)}) collective-permute-start(bf16[64,1024]{1,0:T(8,128)(2,1)S(1)} %get-tuple-element.128), channel_id=1, source_target_pairs={{0,8},{8,0},{16,24},{24,16},{1,9},{9,1},{17,25},{25,17},{2,10},{10... | collective-permute-start | bytes 393224 | tf_op jit(solution)/shard_map/ppermute | solution.py:278
  97.0 7.8 %collective-permute-start.28 = (bf16[64,1024]{1,0:T(8,128)(2,1)S(1)}, bf16[64,1024]{1,0:T(8,128)(2,1)S(1)}, u32[]{:S(2)}, u32[]{:S(2)}) collective-permute-start(bf16[64,1024]{1,0:T(8,128)(2,1)S(1)} %get-tuple-element.129), channel_id=1, source_target_pairs={{0,16},{8,24},{16,0},{24,8},{1,17},{9,25},{17,1},{25,9},{2,18},{10... | collective-permute-start | bytes 393224 | tf_op jit(solution)/shard_map/ppermute | solution.py:278
  101.3 7.4 %collective-permute-start.26 = (bf16[1024,1024]{1,0:T(8,128)(2,1)}, bf16[1024,1024]{1,0:T(8,128)(2,1)}, u32[]{:S(2)}, u32[]{:S(2)}) collective-permute-start(bf16[1024,1024]{1,0:T(8,128)(2,1)} %stack.32.mine_ref), channel_id=1, source_target_pairs={{0,4},{4,0},{1,5},{5,1},{2,6},{6,2},{3,7},{7,3},{8,12},{12,8},{9,1... | collective-permute-start | bytes 6291464 | tf_op jit(solution)/shard_map/ppermute | solution.py:308
  101.3 20.8 %collective-permute-start.23 = (bf16[192,1024]{1,0:T(8,128)(2,1)}, bf16[192,1024]{1,0:T(8,128)(2,1)}, u32[]{:S(2)}, u32[]{:S(2)}) collective-permute-start(bf16[192,1024]{1,0:T(8,128)(2,1)} %get-tuple-element.124), channel_id=1, source_target_pairs={{0,8},{8,0},{16,24},{24,16},{1,9},{9,1},{17,25},{25,17},{2,10},{10... | collective-permute-start | bytes 1179656 | tf_op jit(solution)/shard_map/ppermute | solution.py:278
  102.3 19.8 %collective-permute-start.24 = (bf16[192,1024]{1,0:T(8,128)(2,1)}, bf16[192,1024]{1,0:T(8,128)(2,1)}, u32[]{:S(2)}, u32[]{:S(2)}) collective-permute-start(bf16[192,1024]{1,0:T(8,128)(2,1)} %get-tuple-element.125), channel_id=1, source_target_pairs={{0,16},{8,24},{16,0},{24,8},{1,17},{9,25},{17,1},{25,9},{2,18},{10... | collective-permute-start | bytes 1179656 | tf_op jit(solution)/shard_map/ppermute | solution.py:278
  103.0 19.0 %collective-permute-start.25 = (bf16[192,1024]{1,0:T(8,128)(2,1)}, bf16[192,1024]{1,0:T(8,128)(2,1)}, u32[]{:S(2)}, u32[]{:S(2)}) collective-permute-start(bf16[192,1024]{1,0:T(8,128)(2,1)} %get-tuple-element.126), channel_id=1, source_target_pairs={{0,24},{8,16},{16,8},{24,0},{1,25},{9,17},{17,9},{25,1},{2,26},{10... | collective-permute-start | bytes 1179656 | tf_op jit(solution)/shard_map/ppermute | solution.py:278
  107.3 24.9 %collective-permute-start.35 = (bf16[272,1024]{1,0:T(8,128)(2,1)}, bf16[272,1024]{1,0:T(8,128)(2,1)}, u32[]{:S(2)}, u32[]{:S(2)}) collective-permute-start(bf16[272,1024]{1,0:T(8,128)(2,1)} %join_weighted.2), channel_id=1, source_target_pairs={{0,1},{1,0},{2,3},{3,2},{4,5},{5,4},{6,7},{7,6},{8,9},{9,8},{10,11... | collective-permute-start | bytes 1671176 | tf_op jit(solution)/shard_map/ppermute | solution.py:33
  122.1 4.5 %collective-permute-start.30 = (bf16[1024,1024]{1,0:T(8,128)(2,1)}, bf16[1024,1024]{1,0:T(8,128)(2,1)}, u32[]{:S(2)}, u32[]{:S(2)}) collective-permute-start(bf16[1024,1024]{1,0:T(8,128)(2,1)} %get-tuple-element.135), channel_id=1, source_target_pairs={{0,4},{4,0},{1,5},{5,1},{2,6},{6,2},{3,7},{7,3},{8,12},{12,8},{9,1... | collective-permute-start | bytes 6291464 | tf_op jit(solution)/shard_map/ppermute | solution.py:308
  125.3 15.1 %collective-permute-start.31 = (bf16[272,1024]{1,0:T(8,128)(2,1)S(1)}, bf16[272,1024]{1,0:T(8,128)(2,1)S(1)}, u32[]{:S(2)}, u32[]{:S(2)}) collective-permute-start(bf16[272,1024]{1,0:T(8,128)(2,1)S(1)} %get-tuple-element.149), channel_id=1, source_target_pairs={{0,1},{1,0},{2,3},{3,2},{4,5},{5,4},{6,7},{7,6},{8,9},{9,8},{10,11... | collective-permute-start | bytes 1671176 | tf_op jit(solution)/shard_map/ppermute | solution.py:33
  128.6 14.1 %collective-permute-start.32 = (bf16[128,1024]{1,0:T(8,128)(2,1)S(1)}, bf16[128,1024]{1,0:T(8,128)(2,1)S(1)}, u32[]{:S(2)}, u32[]{:S(2)}) collective-permute-start(bf16[128,1024]{1,0:T(8,128)(2,1)S(1)} %get-tuple-element.143), channel_id=1, source_target_pairs={{0,8},{8,0},{16,24},{24,16},{1,9},{9,1},{17,25},{25,17},{2,10},{10... | collective-permute-start | bytes 786440 | tf_op jit(solution)/shard_map/ppermute | solution.py:278
  130.1 13.5 %collective-permute-start.33 = (bf16[128,1024]{1,0:T(8,128)(2,1)S(1)}, bf16[128,1024]{1,0:T(8,128)(2,1)S(1)}, u32[]{:S(2)}, u32[]{:S(2)}) collective-permute-start(bf16[128,1024]{1,0:T(8,128)(2,1)S(1)} %get-tuple-element.145), channel_id=1, source_target_pairs={{0,16},{8,24},{16,0},{24,8},{1,17},{9,25},{17,1},{25,9},{2,18},{10... | collective-permute-start | bytes 786440 | tf_op jit(solution)/shard_map/ppermute | solution.py:278
  130.6 12.1 %collective-permute-start.34 = (bf16[128,1024]{1,0:T(8,128)(2,1)S(1)}, bf16[128,1024]{1,0:T(8,128)(2,1)S(1)}, u32[]{:S(2)}, u32[]{:S(2)}) collective-permute-start(bf16[128,1024]{1,0:T(8,128)(2,1)S(1)} %get-tuple-element.147), channel_id=1, source_target_pairs={{0,24},{8,16},{16,8},{24,0},{1,25},{9,17},{17,9},{25,1},{2,26},{10... | collective-permute-start | bytes 786440 | tf_op jit(solution)/shard_map/ppermute | solution.py:278
  144.7 14.1 %collective-permute-start.36 = (bf16[256,512]{1,0:T(8,128)(2,1)S(1)}, bf16[256,512]{1,0:T(8,128)(2,1)S(1)}, u32[]{:S(2)}, u32[]{:S(2)}) collective-permute-start(bf16[256,512]{1,0:T(8,128)(2,1)S(1)} %get-tuple-element.154), channel_id=1, source_target_pairs={{0,1},{1,0},{2,3},{3,2},{4,5},{5,4},{6,7},{7,6},{8,9},{9,8},{10,11... | collective-permute-start | bytes 786440 | tf_op jit(solution)/shard_map/ppermute | solution.py:33
  145.7 36.4 %collective-permute-start.37 = (bf16[272,1024]{1,0:T(8,128)(2,1)}, bf16[272,1024]{1,0:T(8,128)(2,1)}, u32[]{:S(2)}, u32[]{:S(2)}) collective-permute-start(bf16[272,1024]{1,0:T(8,128)(2,1)} %add_convert_fusion.1), channel_id=1, source_target_pairs={{0,2},{1,3},{2,0},{3,1},{4,6},{5,7},{6,4},{7,5},{8,10},{9,11},{10,... | collective-permute-start | bytes 1671176 | tf_op jit(solution)/shard_map/ppermute | solution.py:33
  150.6 18.0 %collective-permute-start.38 = (bf16[128,1024]{1,0:T(8,128)(2,1)S(1)}, bf16[128,1024]{1,0:T(8,128)(2,1)S(1)}, u32[]{:S(2)}, u32[]{:S(2)}) collective-permute-start(bf16[128,1024]{1,0:T(8,128)(2,1)S(1)} %get-tuple-element.156), channel_id=1, source_target_pairs={{0,8},{8,0},{16,24},{24,16},{1,9},{9,1},{17,25},{25,17},{2,10},{10... | collective-permute-start | bytes 786440 | tf_op jit(solution)/shard_map/ppermute | solution.py:278
  151.4 17.2 %collective-permute-start.39 = (bf16[128,1024]{1,0:T(8,128)(2,1)S(1)}, bf16[128,1024]{1,0:T(8,128)(2,1)S(1)}, u32[]{:S(2)}, u32[]{:S(2)}) collective-permute-start(bf16[128,1024]{1,0:T(8,128)(2,1)S(1)} %get-tuple-element.157), channel_id=1, source_target_pairs={{0,16},{8,24},{16,0},{24,8},{1,17},{9,25},{17,1},{25,9},{2,18},{10... | collective-permute-start | bytes 786440 | tf_op jit(solution)/shard_map/ppermute | solution.py:278
  152.3 16.0 %collective-permute-start.40 = (bf16[128,1024]{1,0:T(8,128)(2,1)S(1)}, bf16[128,1024]{1,0:T(8,128)(2,1)S(1)}, u32[]{:S(2)}, u32[]{:S(2)}) collective-permute-start(bf16[128,1024]{1,0:T(8,128)(2,1)S(1)} %get-tuple-element.158), channel_id=1, source_target_pairs={{0,24},{8,16},{16,8},{24,0},{1,25},{9,17},{17,9},{25,1},{2,26},{10... | collective-permute-start | bytes 786440 | tf_op jit(solution)/shard_map/ppermute | solution.py:278
  158.8 15.8 %collective-permute-start.42 = (bf16[256,512]{1,0:T(8,128)(2,1)}, bf16[256,512]{1,0:T(8,128)(2,1)}, u32[]{:S(2)}, u32[]{:S(2)}) collective-permute-start(bf16[256,512]{1,0:T(8,128)(2,1)} %get-tuple-element.169), channel_id=1, source_target_pairs={{0,1},{1,0},{2,3},{3,2},{4,5},{5,4},{6,7},{7,6},{8,9},{9,8},{10,11... | collective-permute-start | bytes 786440 | tf_op jit(solution)/shard_map/ppermute | solution.py:33
  168.3 21.8 %collective-permute-start.44 = (bf16[256,512]{1,0:T(8,128)(2,1)}, bf16[256,512]{1,0:T(8,128)(2,1)}, u32[]{:S(2)}, u32[]{:S(2)}) collective-permute-start(bf16[256,512]{1,0:T(8,128)(2,1)} %add_convert_fusion.5), channel_id=1, source_target_pairs={{0,2},{1,3},{2,0},{3,1},{4,6},{5,7},{6,4},{7,5},{8,10},{9,11},{10,... | collective-permute-start | bytes 786440 | tf_op jit(solution)/shard_map/ppermute | solution.py:33
  169.1 24.5 %collective-permute-start.41 = (bf16[256,1024]{1,0:T(8,128)(2,1)S(1)}, bf16[256,1024]{1,0:T(8,128)(2,1)S(1)}, u32[]{:S(2)}, u32[]{:S(2)}) collective-permute-start(bf16[256,1024]{1,0:T(8,128)(2,1)S(1)} %get-tuple-element.168), channel_id=1, source_target_pairs={{0,1},{1,0},{2,3},{3,2},{4,5},{5,4},{6,7},{7,6},{8,9},{9,8},{10,11... | collective-permute-start | bytes 1572872 | tf_op jit(solution)/shard_map/ppermute | solution.py:33
  175.7 16.8 %collective-permute-start.43 = (bf16[256,512]{1,0:T(8,128)(2,1)S(1)}, bf16[256,512]{1,0:T(8,128)(2,1)S(1)}, u32[]{:S(2)}, u32[]{:S(2)}) collective-permute-start(bf16[256,512]{1,0:T(8,128)(2,1)S(1)} %add_convert_fusion.4), channel_id=1, source_target_pairs={{0,2},{1,3},{2,0},{3,1},{4,6},{5,7},{6,4},{7,5},{8,10},{9,11},{10,... | collective-permute-start | bytes 786440 | tf_op jit(solution)/shard_map/ppermute | solution.py:33
  183.4 6.1 %collective-permute-start.45 = (f32[2,256]{1,0:T(2,128)S(1)}, f32[2,256]{1,0:T(2,128)S(1)}, u32[]{:S(2)}, u32[]{:S(2)}) collective-permute-start(f32[2,256]{1,0:T(2,128)S(1)} %add.61), channel_id=1, source_target_pairs={{0,4},{4,0},{1,5},{5,1},{2,6},{6,2},{3,7},{7,3},{8,12},{12,8},{9,1... | collective-permute-start | bytes 6152 | tf_op jit(solution)/shard_map/ppermute | solution.py:308
  (29 other events, 183.1 us)

commit v4 on v3

--- a/solution.py
+++ b/solution.py
@@ -213,7 +213,7 @@
 
 def by_rows(kernel, head, rows_in, whole_in, outs, name):
     total, half = rows_in[0].shape
-    block = min(256, total)
+    block = min(512, total)
 
     def cut(width):
         return pl.BlockSpec((block, width), lambda i: (i, 0))
@@ -376,7 +376,7 @@
 
     back_first[-1] = after(back_first[-1], grad_gate)
     back_parts = join_rows(slot[first], weight[first], back_first, cap)
-    moved[0] = after(moved[0], grad_gate, grad_up)
+    moved[0] = after(moved[0], grad_gate)
     back_cut = [(k.astype(F32) + m.astype(F32)).astype(BF) for k, m in zip(back_parts_last, moved)]
     back_pair = back_cut[1]
     activation, cot_mine, cot_other, _ = together(activation, cot_mine, cot_other, back_pair)

time: 197 us -> 198 us (level)
  starting transfers between devices: 57 us -> 59.4 us
    ppermute x17, starting transfers between devices: 27.5 us -> 30 us  [to_place(): return lax.ppermute(value, 'expert', [(i, i ^ d) for i in range(line)])]
  transfers between devices with their start and end apart: 46 -> 46, of which waited for: 15 -> 13; matrix products, arithmetic and copies ran while one was open for 14% -> 14% of each run, Pallas kernels for 21% -> 21%
where the time goes in v4:
time: 198 us; the launch traced here: 197 us
  starting transfers between devices  59.4 us (30%)
  waiting for transfers between devices  59.1 us (30%)
  Pallas kernels  42.4 us (21%)
  other arithmetic  15.5 us (8%)
  matrix products  12.4 us (6%)
  local copies, waits for them, and re-layouts  7.21 us (4%)
    ppermute x17, waiting for transfers between devices, to_place(): return lax.ppermute(value, 'expert', [(i, i ^ d) for i in range(line)])  53.4 us
    ppermute x17, starting transfers between devices, to_place(): return lax.ppermute(value, 'expert', [(i, i ^ d) for i in range(line)])  30 us
    ppermute x24, starting transfers between devices, exchange(): lax.ppermute(pieces[d], 'path', [(i, i ^ d) for i in range(columns)])  29.3 us
    pallas_call x2, Pallas kernels, by_rows(): pl.pallas_call(functools.partial(kernel, half), grid=(total // block,), o...  22.2 us
    dot_general x3, matrix products, dot(): lax.dot_general(a, b, (((ca,), (cb,)), ((), ())), preferred_element_type=...  12.4 us
    pallas_call x4, Pallas kernels, join_rows(): pl.pallas_call(functools.partial(join_kernel, n, cap, columns, weighted,...  7.24 us
    unnamed x63, local copies, waits for them, and re-layouts  6 us
    ppermute x24, waiting for transfers between devices, exchange(): lax.ppermute(pieces[d], 'path', [(i, i ^ d) for i in range(columns)])  5.61 us
  transfers between devices with their start and end apart: 46, of which 13 were waited for; matrix products, arithmetic and copies ran while one was open for 14% of the time, Pallas kernels for 21%

profile of v4, /device:TPU:0, one launch (start us, length us, event | category | flops | bytes accessed | tf_op | source)
XLA Modules:
  0.0 197.1 jit_solution(6412734446344562736)
XLA Ops:
  0.6 4.1 %collective-permute-start.3 = (bf16[256,1024]{1,0:T(8,128)(2,1)}, bf16[256,1024]{1,0:T(8,128)(2,1)S(1)}, u32[]{:S(2)}, u32[]{:S(2)}) collective-permute-start(bf16[256,1024]{1,0:T(8,128)(2,1)} %refs_2_.1), channel_id=1, source_target_pairs={{0,2},{1,3},{2,0},{3,1},{4,6},{5,7},{6,4},{7,5},{8,10},{9,11},{10,... | collective-permute-start | bytes 1572872 | tf_op jit(solution)/shard_map/ppermute | solution.py:33
  4.7 1.6 collective-permute-start.4
  9.1 1.9 collective-permute-start.1
  11.0 2.5 %collective-permute-start = (f32[4,256]{1,0:T(4,128)S(1)}, f32[4,256]{1,0:T(4,128)S(1)}, u32[]{:S(2)}, u32[]{:S(2)}) collective-permute-start(f32[4,256]{1,0:T(4,128)S(1)} %get-tuple-element.183), channel_id=1, source_target_pairs={{0,1},{1,0},{2,3},{3,2},{4,5},{5,4},{6,7},{7,6},{8,9},{9,8},{10,11... | collective-permute-start | bytes 12296 | tf_op jit(solution)/shard_map/ppermute | solution.py:33
  13.5 15.9 %collective-permute-done.2 = f32[4,256]{1,0:T(4,128)S(1)} collective-permute-done((f32[4,256]{1,0:T(4,128)S(1)}, f32[4,256]{1,0:T(4,128)S(1)}, u32[]{:S(2)}, u32[]{:S(2)}) %collective-permute-start.2) | collective-permute-done | bytes 4128 | tf_op jit(solution)/shard_map/ppermute | solution.py:33
  32.0 1.6 collective-permute-start.6
  33.6 1.5 collective-permute-start.7
  35.6 2.4 %collective-permute-start.12 = (bf16[256,1024]{1,0:T(8,128)(2,1)S(1)}, bf16[256,1024]{1,0:T(8,128)(2,1)}, u32[]{:S(2)}, u32[]{:S(2)}) collective-permute-start(bf16[256,1024]{1,0:T(8,128)(2,1)S(1)} %copy-done.4), channel_id=1, source_target_pairs={{0,2},{1,3},{2,0},{3,1},{4,6},{5,7},{6,4},{7,5},{8,10},{9,11},{10,... | collective-permute-start | bytes 1572872 | tf_op jit(solution)/shard_map/ppermute | solution.py:33
  38.0 10.8 %collective-permute-done.5.refs_2_ = bf16[256,1024]{1,0:T(8,128)(2,1)S(1)} collective-permute-done((bf16[256,1024]{1,0:T(8,128)(2,1)S(1)}, bf16[256,1024]{1,0:T(8,128)(2,1)S(1)}, u32[]{:S(2)}, u32[]{:S(2)}) %collective-permute-start.5) | collective-permute-done | bytes 524320 | tf_op jit(solution)/shard_map/ppermute | solution.py:33
  48.8 2.6 %collective-permute-done.7.refs_4_ = bf16[192,1024]{1,0:T(8,128)(2,1)S(1)} collective-permute-done((bf16[192,1024]{1,0:T(8,128)(2,1)S(1)}, bf16[192,1024]{1,0:T(8,128)(2,1)S(1)}, u32[]{:S(2)}, u32[]{:S(2)}) %collective-permute-start.7) | collective-permute-done | bytes 393248 | tf_op jit(solution)/shard_map/ppermute | solution.py:278
  51.8 1.6 collective-permute-start.11
  53.3 1.5 collective-permute-start.9
  55.3 5.1 %collective-permute-done.12.refs_4_.refs_8_ = bf16[256,1024]{1,0:T(8,128)(2,1)} collective-permute-done((bf16[256,1024]{1,0:T(8,128)(2,1)S(1)}, bf16[256,1024]{1,0:T(8,128)(2,1)}, u32[]{:S(2)}, u32[]{:S(2)}) %collective-permute-start.12) | collective-permute-done | bytes 524320 | tf_op jit(solution)/shard_map/ppermute | solution.py:33
  60.4 4.6 %collective-permute-done.13.refs_3_.refs_7_ = bf16[256,1024]{1,0:T(8,128)(2,1)S(1)} collective-permute-done((bf16[256,1024]{1,0:T(8,128)(2,1)S(1)}, bf16[256,1024]{1,0:T(8,128)(2,1)S(1)}, u32[]{:S(2)}, u32[]{:S(2)}) %collective-permute-start.13) | collective-permute-done | bytes 524320 | tf_op jit(solution)/shard_map/ppermute | solution.py:33
  65.9 2.8 %pick_scaled.2 = (bf16[192,1024]{1,0:T(8,128)(2,1)S(1)}, bf16[192,1024]{1,0:T(8,128)(2,1)}, bf16[192,1024]{1,0:T(8,128)(2,1)}, bf16[192,1024]{1,0:T(8,128)(2,1)}) custom-call(s32[3,2,256]{2,1,0:T(2,128)S(1)} %slice.76.refs_0_, f32[3,2,256]{2,1,0:T(2,128)S(1)} %pad_maximum_fusion.6.refs_1_, bf16[256,1024]{1,0:T(8,128)(2,1)S(1)} %copy-done.4, ...), custom_call_target="tpu_custom_call" | custom-call | tf_op jit(solution)/shard_map/pick_scaled/pallas_call | solution.py:80
  68.7 1.5 collective-permute-start.17
  70.2 1.5 collective-permute-start.19
  72.2 1.4 copy-done.9
  73.6 10.7 %ahead.1 = (f32[1024,384]{1,0:T(8,128)S(1)}, f32[1024,384]{1,0:T(8,128)S(1)}, bf16[1024,384]{1,0:T(8,128)(2,1)S(1)}, bf16[1024,1024]{1,0:T(8,128)(2,1)}, bf16[1024,1024]{1,0:T(8,128)(2,1)}) custom-call(s32[1]{0:T(128)} %bitcast.6.head_ref, bf16[1024,1024]{1,0:T(8,128)(2,1)} %copy-done, bf16[1024,1024]{1,0:T(8,128)(2,1)} %collective-permute-done.14.other_ref, ...), custom_call_target="tpu_custom_call" | custom-call | flops 399999991808 | bytes 41943040 | tf_op jit(solution)/shard_map/ahead/pallas_call | solution.py:221
  85.2 1.6 pick_scaled.3
  86.8 1.6 collective-permute-start.18
  88.4 1.5 collective-permute-start.20
  89.9 2.3 %collective-permute-start.22 = (bf16[64,1024]{1,0:T(8,128)(2,1)S(1)}, bf16[64,1024]{1,0:T(8,128)(2,1)S(1)}, u32[]{:S(2)}, u32[]{:S(2)}) collective-permute-start(bf16[64,1024]{1,0:T(8,128)(2,1)S(1)} %get-tuple-element.122), channel_id=1, source_target_pairs={{0,24},{8,16},{16,8},{24,0},{1,25},{9,17},{17,9},{25,1},{2,26},{10... | collective-permute-start | bytes 393224 | tf_op jit(solution)/shard_map/ppermute | solution.py:278
  92.1 2.7 %deal.2 = (bf16[192,1024]{1,0:T(8,128)(2,1)S(1)}, bf16[64,1024]{1,0:T(8,128)(2,1)S(1)}, bf16[192,1024]{1,0:T(8,128)(2,1)}, bf16[64,1024]{1,0:T(8,128)(2,1)S(1)},...) custom-call(bf16[1024,1024]{1,0:T(8,128)(2,1)S(1)} %copy-done.2, ...), custom_call_target="tpu_custom_call" | custom-call | tf_op jit(solution)/shard_map/deal/pallas_call | solution.py:244
  96.8 1.5 collective-permute-start.28
  98.4 2.8 %stack.32.mine_ref = bf16[1024,1024]{1,0:T(8,128)(2,1)} custom-call(bf16[192,1024]{1,0:T(8,128)(2,1)S(1)} %get-tuple-element.106.refs_0_, bf16[64,1024]{1,0:T(8,128)(2,1)S(1)} %get-tuple-element.111.refs_1_, bf16[192,1024]{1,0:T(8,128)(2,1)} %collective-permute-done.17.refs_2_, bf16[64,1024]{1,0:T(8,128)(2,1)S(1)} %collective-permute-done.18.refs_3_, ...), custom_call_target="tpu_custom_call" | custom-call | tf_op jit(solution)/shard_map/stack/pallas_call | solution.py:103
  102.9 1.8 collective-permute-start.25
  104.6 2.5 %join_weighted.2 = bf16[272,1024]{1,0:T(8,128)(2,1)} custom-call(s32[1,2,256]{2,1,0:T(2,128)S(1)} %copy-done.6, f32[1,2,256]{2,1,0:T(2,128)S(1)} %copy-done.8, bf16[64,1024]{1,0:T(8,128)(2,1)S(1)} %get-tuple-element.127.refs_2_, bf16[64,1024]{1,0:T(8,128)(2,1)S(1)} %collective-permute-done.27.refs_3_, bf16[64,1024]{1,0:T(8,128)(2,1)S(1)} %collective-permute-done.28.refs_4_, ...), custom_call_target="tpu_custom_call" | custom-call | flops 399999991808 | bytes 41943040 | tf_op jit(solution)/shard_map/join_weighted/pallas_call | solution.py:161
  107.1 1.4 collective-permute-start.35
  108.6 11.5 %back.1 = (bf16[1024,384]{1,0:T(8,128)(2,1)S(1)}, bf16[1024,384]{1,0:T(8,128)(2,1)S(1)}, bf16[1024,1024]{1,0:T(8,128)(2,1)}, bf16[1024,1024]{1,0:T(8,128)(2,1)}) custom-call(s32[1]{0:T(128)} %bitcast.6.head_ref, bf16[1024,1024]{1,0:T(8,128)(2,1)} %stack.32.mine_ref, bf16[1024,1024]{1,0:T(8,128)(2,1)} %collective-permute-done.26.other_ref, ...), custom_call_target="tpu_custom_call" | custom-call | flops 399999991808 | bytes 41943040 | tf_op jit(solution)/shard_map/back/pallas_call | solution.py:221
  121.9 3.1 %join_weighted.3 = (bf16[272,1024]{1,0:T(8,128)(2,1)S(1)}, bf16[272,1024]{1,0:T(8,128)(2,1)S(1)}, bf16[272,1024]{1,0:T(8,128)(2,1)S(1)}) custom-call(s32[3,2,256]{2,1,0:T(2,128)S(1)} %slice.76.refs_0_, f32[3,2,256]{2,1,0:T(2,128)S(1)} %pad_maximum_fusion.6.refs_1_, bf16[192,1024]{1,0:T(8,128)(2,1)S(1)} %get-tuple-element.123.refs_2_, ...), custom_call_target="tpu_custom_call" | custom-call | flops 399999991808 | bytes 41943040 | tf_op jit(solution)/shard_map/join_weighted/pallas_call | solution.py:161
  126.4 2.1 %deal.3 = (bf16[128,1024]{1,0:T(8,128)(2,1)S(1)}, bf16[128,1024]{1,0:T(8,128)(2,1)S(1)}, bf16[128,1024]{1,0:T(8,128)(2,1)S(1)}, bf16[128,1024]{1,0:T(8,128)(2,1)...) custom-call(bf16[1024,1024]{1,0:T(8,128)(2,1)S(1)} %copy-done.1, ...), custom_call_target="tpu_custom_call" | custom-call | tf_op jit(solution)/shard_map/deal/pallas_call | solution.py:244
  128.4 1.5 collective-permute-start.32
  130.5 1.5 collective-permute-start.34
  132.0 2.1 %add_convert_fusion.1 = bf16[272,1024]{1,0:T(8,128)(2,1)} fusion(bf16[272,1024]{1,0:T(8,128)(2,1)} %collective-permute-done.35, bf16[272,1024]{1,0:T(8,128)(2,1)S(1)} %get-tuple-element.151), kind=kLoop, calls=%fused_computation.15 | loop fusion | flops 1114112 | bytes 1671168 | tf_op jit(solution)/shard_map/convert_element_type | solution.py:53
  134.0 6.1 %collective-permute-done.31 = bf16[272,1024]{1,0:T(8,128)(2,1)S(1)} collective-permute-done((bf16[272,1024]{1,0:T(8,128)(2,1)S(1)}, bf16[272,1024]{1,0:T(8,128)(2,1)S(1)}, u32[]{:S(2)}, u32[]{:S(2)}) %collective-permute-start.31) | collective-permute-done | bytes 557088 | tf_op jit(solution)/shard_map/ppermute | solution.py:33
  141.2 1.4 collective-permute-done.34.refs_5_
  145.5 4.9 %collective-permute-start.37 = (bf16[272,1024]{1,0:T(8,128)(2,1)}, bf16[272,1024]{1,0:T(8,128)(2,1)}, u32[]{:S(2)}, u32[]{:S(2)}) collective-permute-start(bf16[272,1024]{1,0:T(8,128)(2,1)} %add_convert_fusion.1), channel_id=1, source_target_pairs={{0,2},{1,3},{2,0},{3,1},{4,6},{5,7},{6,4},{7,5},{8,10},{9,11},{10,... | collective-permute-start | bytes 1671176 | tf_op jit(solution)/shard_map/ppermute | solution.py:33
  152.1 1.7 collective-permute-start.40
  153.8 4.7 %collective-permute-done.36 = bf16[256,512]{1,0:T(8,128)(2,1)S(1)} collective-permute-done((bf16[256,512]{1,0:T(8,128)(2,1)S(1)}, bf16[256,512]{1,0:T(8,128)(2,1)S(1)}, u32[]{:S(2)}, u32[]{:S(2)}) %collective-permute-start.36) | collective-permute-done | bytes 262176 | tf_op jit(solution)/shard_map/ppermute | solution.py:33
  159.3 5.1 %broadcast_select_fusion.1 = (bf16[1024,1024]{1,0:T(8,128)(2,1)}, bf16[1024,1024]{1,0:T(8,128)(2,1)}, bf16[1024,1024]{1,0:T(8,128)(2,1)S(1)}, bf16[1024,1024]{1,0:T(8,128)(2,1)S(1)}) fusion(bf16[1024,1024]{1,0:T(8,128)(2,1)} %stack.32.mine_ref, bf16[1024,1024]{1,0:T(8,128)(2,1)} %collective-permute-done.26.other_ref, pred[]{:T(512)S(6)} %eq.34, ...), kind=kLoop, calls=%fused_computation.11 | loop fusion | flops 4194304 | bytes 16777216 | tf_op jit(solution)/shard_map/jit(_where)/select_n | solution.py:313
  164.4 3.6 %convolution_convert_fusion.1 = bf16[2048,384]{1,0:T(8,128)(2,1)} fusion(bf16[1024,384]{1,0:T(8,128)(2,1)S(1)} %copy-done.15, bf16[1024,1024]{1,0:T(8,128)(2,1)S(1)} %get-tuple-element.184, bf16[1024,1024]{1,0:T(8,128)(2,1)S(1)} %get-tuple-element.185), kind=kOutput, calls=%fused_computation.7 | convolution fusion | flops 1619787776 | bytes 6553600 | tf_op jit(solution)/shard_map/dot_general | solution.py:22
  168.7 2.0 %collective-permute-start.41 = (bf16[256,1024]{1,0:T(8,128)(2,1)S(1)}, bf16[256,1024]{1,0:T(8,128)(2,1)S(1)}, u32[]{:S(2)}, u32[]{:S(2)}) collective-permute-start(bf16[256,1024]{1,0:T(8,128)(2,1)S(1)} %get-tuple-element.168), channel_id=1, source_target_pairs={{0,1},{1,0},{2,3},{3,2},{4,5},{5,4},{6,7},{7,6},{8,9},{9,8},{10,11... | collective-permute-start | bytes 1572872 | tf_op jit(solution)/shard_map/ppermute | solution.py:33
  171.8 5.4 %collective-permute-start.43 = (bf16[256,512]{1,0:T(8,128)(2,1)S(1)}, bf16[256,512]{1,0:T(8,128)(2,1)S(1)}, u32[]{:S(2)}, u32[]{:S(2)}) collective-permute-start(bf16[256,512]{1,0:T(8,128)(2,1)S(1)} %add_convert_fusion.4), channel_id=1, source_target_pairs={{0,2},{1,3},{2,0},{3,1},{4,6},{5,7},{6,4},{7,5},{8,10},{9,11},{10,... | collective-permute-start | bytes 786440 | tf_op jit(solution)/shard_map/ppermute | solution.py:33
  177.2 3.6 %fusion.7 = bf16[1,2048,384]{2,1,0:T(8,128)(2,1)} fusion(bf16[1024,384]{1,0:T(8,128)(2,1)S(1)} %copy-done.13, bf16[1024,1024]{1,0:T(8,128)(2,1)S(1)} %copy-done.18, bf16[1024,1024]{1,0:T(8,128)(2,1)S(1)} %copy-done.20), kind=kOutput, calls=%fused_computation.8 | convolution fusion | flops 1619787776 | bytes 6553600 | tf_op jit(solution)/shard_map/dot_general | solution.py:22
  183.2 5.2 %fusion.8 = bf16[1,384,2048]{2,1,0:T(8,128)(2,1)} fusion(bf16[1024,384]{1,0:T(8,128)(2,1)S(1)} %copy-done.11, bf16[1024,1024]{1,0:T(8,128)(2,1)} %get-tuple-element.177, bf16[1024,1024]{1,0:T(8,128)(2,1)} %get-tuple-element.176), kind=kOutput, calls=%fused_computation.9 | convolution fusion | flops 1619787776 | bytes 6553600 | tf_op jit(solution)/shard_map/dot_general | solution.py:22
  189.8 5.3 %collective-permute-done.43 = bf16[256,512]{1,0:T(8,128)(2,1)S(1)} collective-permute-done((bf16[256,512]{1,0:T(8,128)(2,1)S(1)}, bf16[256,512]{1,0:T(8,128)(2,1)S(1)}, u32[]{:S(2)}, u32[]{:S(2)}) %collective-permute-start.43) | collective-permute-done | bytes 262176 | tf_op jit(solution)/shard_map/ppermute | solution.py:33
  195.1 2.0 %add_convert_fusion.3 = bf16[256,1024]{1,0:T(8,128)(2,1)} fusion(bf16[256,1024]{1,0:T(8,128)(2,1)S(1)} %collective-permute-done.41, bf16[256,1024]{1,0:T(8,128)(2,1)S(1)} %get-tuple-element.167, bf16[256,512]{1,0:T(8,128)(2,1)} %collective-permute-done.44, bf16[256,512]{1,0:T(8,128)(2,1)S(1)} %collective-permute-done.43), kind=kLoop, calls=%fused_computation.17 | loop fusion | flops 2359296 | bytes 2097152 | tf_op jit(solution)/shard_map/convert_element_type | solution.py:393
  (151 shorter events, 28.3 us)
Async XLA Ops:
  0.6 35.0 %copy-start.4 = (bf16[256,1024]{1,0:T(8,128)(2,1)S(1)}, bf16[256,1024]{1,0:T(8,128)(2,1)}, u32[]{:S(2)}) copy-start(bf16[256,1024]{1,0:T(8,128)(2,1)} %refs_6_) | copy-start | bytes 1572868
  0.6 28.8 %collective-permute-start.3 = (bf16[256,1024]{1,0:T(8,128)(2,1)}, bf16[256,1024]{1,0:T(8,128)(2,1)S(1)}, u32[]{:S(2)}, u32[]{:S(2)}) collective-permute-start(bf16[256,1024]{1,0:T(8,128)(2,1)} %refs_2_.1), channel_id=1, source_target_pairs={{0,2},{1,3},{2,0},{3,1},{4,6},{5,7},{6,4},{7,5},{8,10},{9,11},{10,... | collective-permute-start | bytes 1572872 | tf_op jit(solution)/shard_map/ppermute | solution.py:33
  4.7 24.7 %collective-permute-start.4 = (bf16[256,1024]{1,0:T(8,128)(2,1)}, bf16[256,1024]{1,0:T(8,128)(2,1)S(1)}, u32[]{:S(2)}, u32[]{:S(2)}) collective-permute-start(bf16[256,1024]{1,0:T(8,128)(2,1)} %refs_2_.1), channel_id=1, source_target_pairs={{0,1},{1,0},{2,3},{3,2},{4,5},{5,4},{6,7},{7,6},{8,9},{9,8},{10,11... | collective-permute-start | bytes 1572872 | tf_op jit(solution)/shard_map/ppermute | solution.py:33
  9.1 20.3 %collective-permute-start.2 = (f32[4,256]{1,0:T(4,128)S(1)}, f32[4,256]{1,0:T(4,128)S(1)}, u32[]{:S(2)}, u32[]{:S(2)}) collective-permute-start(f32[4,256]{1,0:T(4,128)S(1)} %get-tuple-element.183), channel_id=1, source_target_pairs={{0,3},{1,2},{2,1},{3,0},{4,7},{5,6},{6,5},{7,4},{8,11},{9,10},{10,... | collective-permute-start | bytes 12296 | tf_op jit(solution)/shard_map/ppermute | solution.py:33
  9.1 20.3 %collective-permute-start.1 = (f32[4,256]{1,0:T(4,128)S(1)}, f32[4,256]{1,0:T(4,128)S(1)}, u32[]{:S(2)}, u32[]{:S(2)}) collective-permute-start(f32[4,256]{1,0:T(4,128)S(1)} %get-tuple-element.183), channel_id=1, source_target_pairs={{0,2},{1,3},{2,0},{3,1},{4,6},{5,7},{6,4},{7,5},{8,10},{9,11},{10,... | collective-permute-start | bytes 12296 | tf_op jit(solution)/shard_map/ppermute | solution.py:33
  11.0 18.4 %collective-permute-start = (f32[4,256]{1,0:T(4,128)S(1)}, f32[4,256]{1,0:T(4,128)S(1)}, u32[]{:S(2)}, u32[]{:S(2)}) collective-permute-start(f32[4,256]{1,0:T(4,128)S(1)} %get-tuple-element.183), channel_id=1, source_target_pairs={{0,1},{1,0},{2,3},{3,2},{4,5},{5,4},{6,7},{7,6},{8,9},{9,8},{10,11... | collective-permute-start | bytes 12296 | tf_op jit(solution)/shard_map/ppermute | solution.py:33
  29.4 35.6 %copy-start.29 = (f32[4,256]{1,0:T(4,128)}, f32[4,256]{1,0:T(4,128)S(1)}, u32[]{:S(2)}) copy-start(f32[4,256]{1,0:T(4,128)S(1)} %collective-permute-done.2) | copy-start | bytes 12292
  29.5 19.3 %collective-permute-start.5 = (bf16[256,1024]{1,0:T(8,128)(2,1)S(1)}, bf16[256,1024]{1,0:T(8,128)(2,1)S(1)}, u32[]{:S(2)}, u32[]{:S(2)}) collective-permute-start(bf16[256,1024]{1,0:T(8,128)(2,1)S(1)} %collective-permute-done.3.refs_4_), channel_id=1, source_target_pairs={{0,1},{1,0},{2,3},{3,2},{4,5},{5,4},{6,7},{7,6},{8,9},{9,8},{10,11... | collective-permute-start | bytes 1572872 | tf_op jit(solution)/shard_map/ppermute | solution.py:33
  32.0 16.8 %collective-permute-start.6 = (bf16[192,1024]{1,0:T(8,128)(2,1)S(1)}, bf16[192,1024]{1,0:T(8,128)(2,1)S(1)}, u32[]{:S(2)}, u32[]{:S(2)}) collective-permute-start(bf16[192,1024]{1,0:T(8,128)(2,1)S(1)} %get-tuple-element.94), channel_id=1, source_target_pairs={{0,8},{8,0},{16,24},{24,16},{1,9},{9,1},{17,25},{25,17},{2,10},{10... | collective-permute-start | bytes 1179656 | tf_op jit(solution)/shard_map/ppermute | solution.py:278
  33.6 17.8 %collective-permute-start.7 = (bf16[192,1024]{1,0:T(8,128)(2,1)S(1)}, bf16[192,1024]{1,0:T(8,128)(2,1)S(1)}, u32[]{:S(2)}, u32[]{:S(2)}) collective-permute-start(bf16[192,1024]{1,0:T(8,128)(2,1)S(1)} %get-tuple-element.95), channel_id=1, source_target_pairs={{0,16},{8,24},{16,0},{24,8},{1,17},{9,25},{17,1},{25,9},{2,18},{10... | collective-permute-start | bytes 1179656 | tf_op jit(solution)/shard_map/ppermute | solution.py:278
  35.1 16.3 %collective-permute-start.8 = (bf16[192,1024]{1,0:T(8,128)(2,1)S(1)}, bf16[192,1024]{1,0:T(8,128)(2,1)S(1)}, u32[]{:S(2)}, u32[]{:S(2)}) collective-permute-start(bf16[192,1024]{1,0:T(8,128)(2,1)S(1)} %get-tuple-element.96), channel_id=1, source_target_pairs={{0,24},{8,16},{16,8},{24,0},{1,25},{9,17},{17,9},{25,1},{2,26},{10... | collective-permute-start | bytes 1179656 | tf_op jit(solution)/shard_map/ppermute | solution.py:278
  35.6 24.8 %collective-permute-start.12 = (bf16[256,1024]{1,0:T(8,128)(2,1)S(1)}, bf16[256,1024]{1,0:T(8,128)(2,1)}, u32[]{:S(2)}, u32[]{:S(2)}) collective-permute-start(bf16[256,1024]{1,0:T(8,128)(2,1)S(1)} %copy-done.4), channel_id=1, source_target_pairs={{0,2},{1,3},{2,0},{3,1},{4,6},{5,7},{6,4},{7,5},{8,10},{9,11},{10,... | collective-permute-start | bytes 1572872 | tf_op jit(solution)/shard_map/ppermute | solution.py:33
  48.8 16.2 %collective-permute-start.13 = (bf16[256,1024]{1,0:T(8,128)(2,1)S(1)}, bf16[256,1024]{1,0:T(8,128)(2,1)S(1)}, u32[]{:S(2)}, u32[]{:S(2)}) collective-permute-start(bf16[256,1024]{1,0:T(8,128)(2,1)S(1)} %copy-done.4), channel_id=1, source_target_pairs={{0,1},{1,0},{2,3},{3,2},{4,5},{5,4},{6,7},{7,6},{8,9},{9,8},{10,11... | collective-permute-start | bytes 1572872 | tf_op jit(solution)/shard_map/ppermute | solution.py:33
  51.8 8.6 %collective-permute-start.11 = (bf16[64,1024]{1,0:T(8,128)(2,1)S(1)}, bf16[64,1024]{1,0:T(8,128)(2,1)S(1)}, u32[]{:S(2)}, u32[]{:S(2)}) collective-permute-start(bf16[64,1024]{1,0:T(8,128)(2,1)S(1)} %get-tuple-element.101), channel_id=1, source_target_pairs={{0,24},{8,16},{16,8},{24,0},{1,25},{9,17},{17,9},{25,1},{2,26},{10... | collective-permute-start | bytes 393224 | tf_op jit(solution)/shard_map/ppermute | solution.py:278
  53.3 11.6 %collective-permute-start.9 = (bf16[64,1024]{1,0:T(8,128)(2,1)S(1)}, bf16[64,1024]{1,0:T(8,128)(2,1)S(1)}, u32[]{:S(2)}, u32[]{:S(2)}) collective-permute-start(bf16[64,1024]{1,0:T(8,128)(2,1)S(1)} %get-tuple-element.99), channel_id=1, source_target_pairs={{0,8},{8,0},{16,24},{24,16},{1,9},{9,1},{17,25},{25,17},{2,10},{10... | collective-permute-start | bytes 393224 | tf_op jit(solution)/shard_map/ppermute | solution.py:278
  54.8 10.2 %collective-permute-start.10 = (bf16[64,1024]{1,0:T(8,128)(2,1)S(1)}, bf16[64,1024]{1,0:T(8,128)(2,1)S(1)}, u32[]{:S(2)}, u32[]{:S(2)}) collective-permute-start(bf16[64,1024]{1,0:T(8,128)(2,1)S(1)} %get-tuple-element.100), channel_id=1, source_target_pairs={{0,16},{8,24},{16,0},{24,8},{1,17},{9,25},{17,1},{25,9},{2,18},{10... | collective-permute-start | bytes 393224 | tf_op jit(solution)/shard_map/ppermute | solution.py:278
  65.1 7.1 %collective-permute-start.14 = (bf16[1024,1024]{1,0:T(8,128)(2,1)S(1)}, bf16[1024,1024]{1,0:T(8,128)(2,1)}, u32[]{:S(2)}, u32[]{:S(2)}) collective-permute-start(bf16[1024,1024]{1,0:T(8,128)(2,1)S(1)} %stack.31.mine_ref), channel_id=1, source_target_pairs={{0,4},{4,0},{1,5},{5,1},{2,6},{6,2},{3,7},{7,3},{8,12},{12,8},{9,1... | collective-permute-start | bytes 6291464 | tf_op jit(solution)/shard_map/ppermute | solution.py:308
  65.2 20.0 %collective-permute-start.16 = (bf16[256,1024]{1,0:T(8,128)(2,1)}, bf16[256,1024]{1,0:T(8,128)(2,1)}, u32[]{:S(2)}, u32[]{:S(2)}) collective-permute-start(bf16[256,1024]{1,0:T(8,128)(2,1)} %collective-permute-done.12.refs_4_.refs_8_), channel_id=1, source_target_pairs={{0,1},{1,0},{2,3},{3,2},{4,5},{5,4},{6,7},{7,6},{8,9},{9,8},{10,11... | collective-permute-start | bytes 1572872 | tf_op jit(solution)/shard_map/ppermute | solution.py:33
  68.7 19.6 %collective-permute-start.17 = (bf16[192,1024]{1,0:T(8,128)(2,1)}, bf16[192,1024]{1,0:T(8,128)(2,1)}, u32[]{:S(2)}, u32[]{:S(2)}) collective-permute-start(bf16[192,1024]{1,0:T(8,128)(2,1)} %get-tuple-element.117), channel_id=1, source_target_pairs={{0,8},{8,0},{16,24},{24,16},{1,9},{9,1},{17,25},{25,17},{2,10},{10... | collective-permute-start | bytes 1179656 | tf_op jit(solution)/shard_map/ppermute | solution.py:278
  70.2 24.6 %collective-permute-start.19 = (bf16[192,1024]{1,0:T(8,128)(2,1)}, bf16[192,1024]{1,0:T(8,128)(2,1)}, u32[]{:S(2)}, u32[]{:S(2)}) collective-permute-start(bf16[192,1024]{1,0:T(8,128)(2,1)} %get-tuple-element.119), channel_id=1, source_target_pairs={{0,16},{8,24},{16,0},{24,8},{1,17},{9,25},{17,1},{25,9},{2,18},{10... | collective-permute-start | bytes 1179656 | tf_op jit(solution)/shard_map/ppermute | solution.py:278
  71.7 23.8 %collective-permute-start.21 = (bf16[192,1024]{1,0:T(8,128)(2,1)}, bf16[192,1024]{1,0:T(8,128)(2,1)}, u32[]{:S(2)}, u32[]{:S(2)}) collective-permute-start(bf16[192,1024]{1,0:T(8,128)(2,1)} %get-tuple-element.121), channel_id=1, source_target_pairs={{0,24},{8,16},{16,8},{24,0},{1,25},{9,17},{17,9},{25,1},{2,26},{10... | collective-permute-start | bytes 1179656 | tf_op jit(solution)/shard_map/ppermute | solution.py:278
  85.2 4.7 %collective-permute-start.15 = (bf16[1024,1024]{1,0:T(8,128)(2,1)}, bf16[1024,1024]{1,0:T(8,128)(2,1)}, u32[]{:S(2)}, u32[]{:S(2)}) collective-permute-start(bf16[1024,1024]{1,0:T(8,128)(2,1)} %get-tuple-element.109), channel_id=1, source_target_pairs={{0,4},{4,0},{1,5},{5,1},{2,6},{6,2},{3,7},{7,3},{8,12},{12,8},{9,1... | collective-permute-start | bytes 6291464 | tf_op jit(solution)/shard_map/ppermute | solution.py:308
  86.8 10.0 %collective-permute-start.18 = (bf16[64,1024]{1,0:T(8,128)(2,1)S(1)}, bf16[64,1024]{1,0:T(8,128)(2,1)S(1)}, u32[]{:S(2)}, u32[]{:S(2)}) collective-permute-start(bf16[64,1024]{1,0:T(8,128)(2,1)S(1)} %get-tuple-element.118), channel_id=1, source_target_pairs={{0,8},{8,0},{16,24},{24,16},{1,9},{9,1},{17,25},{25,17},{2,10},{10... | collective-permute-start | bytes 393224 | tf_op jit(solution)/shard_map/ppermute | solution.py:278
  88.4 10.0 %collective-permute-start.20 = (bf16[64,1024]{1,0:T(8,128)(2,1)S(1)}, bf16[64,1024]{1,0:T(8,128)(2,1)S(1)}, u32[]{:S(2)}, u32[]{:S(2)}) collective-permute-start(bf16[64,1024]{1,0:T(8,128)(2,1)S(1)} %get-tuple-element.120), channel_id=1, source_target_pairs={{0,16},{8,24},{16,0},{24,8},{1,17},{9,25},{17,1},{25,9},{2,18},{10... | collective-permute-start | bytes 393224 | tf_op jit(solution)/shard_map/ppermute | solution.py:278
  89.9 8.5 %collective-permute-start.22 = (bf16[64,1024]{1,0:T(8,128)(2,1)S(1)}, bf16[64,1024]{1,0:T(8,128)(2,1)S(1)}, u32[]{:S(2)}, u32[]{:S(2)}) collective-permute-start(bf16[64,1024]{1,0:T(8,128)(2,1)S(1)} %get-tuple-element.122), channel_id=1, source_target_pairs={{0,24},{8,16},{16,8},{24,0},{1,25},{9,17},{17,9},{25,1},{2,26},{10... | collective-permute-start | bytes 393224 | tf_op jit(solution)/shard_map/ppermute | solution.py:278
  94.9 7.3 %collective-permute-start.29 = (bf16[64,1024]{1,0:T(8,128)(2,1)S(1)}, bf16[64,1024]{1,0:T(8,128)(2,1)S(1)}, u32[]{:S(2)}, u32[]{:S(2)}) collective-permute-start(bf16[64,1024]{1,0:T(8,128)(2,1)S(1)} %get-tuple-element.130), channel_id=1, source_target_pairs={{0,24},{8,16},{16,8},{24,0},{1,25},{9,17},{17,9},{25,1},{2,26},{10... | collective-permute-start | bytes 393224 | tf_op jit(solution)/shard_map/ppermute | solution.py:278
  95.5 7.3 %collective-permute-start.27 = (bf16[64,1024]{1,0:T(8,128)(2,1)S(1)}, bf16[64,1024]{1,0:T(8,128)(2,1)S(1)}, u32[]{:S(2)}, u32[]{:S(2)}) collective-permute-start(bf16[64,1024]{1,0:T(8,128)(2,1)S(1)} %get-tuple-element.128), channel_id=1, source_target_pairs={{0,8},{8,0},{16,24},{24,16},{1,9},{9,1},{17,25},{25,17},{2,10},{10... | collective-permute-start | bytes 393224 | tf_op jit(solution)/shard_map/ppermute | solution.py:278
  96.8 7.8 %collective-permute-start.28 = (bf16[64,1024]{1,0:T(8,128)(2,1)S(1)}, bf16[64,1024]{1,0:T(8,128)(2,1)S(1)}, u32[]{:S(2)}, u32[]{:S(2)}) collective-permute-start(bf16[64,1024]{1,0:T(8,128)(2,1)S(1)} %get-tuple-element.129), channel_id=1, source_target_pairs={{0,16},{8,24},{16,0},{24,8},{1,17},{9,25},{17,1},{25,9},{2,18},{10... | collective-permute-start | bytes 393224 | tf_op jit(solution)/shard_map/ppermute | solution.py:278
  101.1 7.4 %collective-permute-start.26 = (bf16[1024,1024]{1,0:T(8,128)(2,1)}, bf16[1024,1024]{1,0:T(8,128)(2,1)}, u32[]{:S(2)}, u32[]{:S(2)}) collective-permute-start(bf16[1024,1024]{1,0:T(8,128)(2,1)} %stack.32.mine_ref), channel_id=1, source_target_pairs={{0,4},{4,0},{1,5},{5,1},{2,6},{6,2},{3,7},{7,3},{8,12},{12,8},{9,1... | collective-permute-start | bytes 6291464 | tf_op jit(solution)/shard_map/ppermute | solution.py:308
  101.1 20.7 %collective-permute-start.23 = (bf16[192,1024]{1,0:T(8,128)(2,1)}, bf16[192,1024]{1,0:T(8,128)(2,1)}, u32[]{:S(2)}, u32[]{:S(2)}) collective-permute-start(bf16[192,1024]{1,0:T(8,128)(2,1)} %get-tuple-element.124), channel_id=1, source_target_pairs={{0,8},{8,0},{16,24},{24,16},{1,9},{9,1},{17,25},{25,17},{2,10},{10... | collective-permute-start | bytes 1179656 | tf_op jit(solution)/shard_map/ppermute | solution.py:278
  102.1 19.7 %collective-permute-start.24 = (bf16[192,1024]{1,0:T(8,128)(2,1)}, bf16[192,1024]{1,0:T(8,128)(2,1)}, u32[]{:S(2)}, u32[]{:S(2)}) collective-permute-start(bf16[192,1024]{1,0:T(8,128)(2,1)} %get-tuple-element.125), channel_id=1, source_target_pairs={{0,16},{8,24},{16,0},{24,8},{1,17},{9,25},{17,1},{25,9},{2,18},{10... | collective-permute-start | bytes 1179656 | tf_op jit(solution)/shard_map/ppermute | solution.py:278
  102.9 19.0 %collective-permute-start.25 = (bf16[192,1024]{1,0:T(8,128)(2,1)}, bf16[192,1024]{1,0:T(8,128)(2,1)}, u32[]{:S(2)}, u32[]{:S(2)}) collective-permute-start(bf16[192,1024]{1,0:T(8,128)(2,1)} %get-tuple-element.126), channel_id=1, source_target_pairs={{0,24},{8,16},{16,8},{24,0},{1,25},{9,17},{17,9},{25,1},{2,26},{10... | collective-permute-start | bytes 1179656 | tf_op jit(solution)/shard_map/ppermute | solution.py:278
  107.1 24.8 %collective-permute-start.35 = (bf16[272,1024]{1,0:T(8,128)(2,1)}, bf16[272,1024]{1,0:T(8,128)(2,1)}, u32[]{:S(2)}, u32[]{:S(2)}) collective-permute-start(bf16[272,1024]{1,0:T(8,128)(2,1)} %join_weighted.2), channel_id=1, source_target_pairs={{0,1},{1,0},{2,3},{3,2},{4,5},{5,4},{6,7},{7,6},{8,9},{9,8},{10,11... | collective-permute-start | bytes 1671176 | tf_op jit(solution)/shard_map/ppermute | solution.py:33
  121.9 4.5 %collective-permute-start.30 = (bf16[1024,1024]{1,0:T(8,128)(2,1)}, bf16[1024,1024]{1,0:T(8,128)(2,1)}, u32[]{:S(2)}, u32[]{:S(2)}) collective-permute-start(bf16[1024,1024]{1,0:T(8,128)(2,1)} %get-tuple-element.135), channel_id=1, source_target_pairs={{0,4},{4,0},{1,5},{5,1},{2,6},{6,2},{3,7},{7,3},{8,12},{12,8},{9,1... | collective-permute-start | bytes 6291464 | tf_op jit(solution)/shard_map/ppermute | solution.py:308
  125.0 15.1 %collective-permute-start.31 = (bf16[272,1024]{1,0:T(8,128)(2,1)S(1)}, bf16[272,1024]{1,0:T(8,128)(2,1)S(1)}, u32[]{:S(2)}, u32[]{:S(2)}) collective-permute-start(bf16[272,1024]{1,0:T(8,128)(2,1)S(1)} %get-tuple-element.149), channel_id=1, source_target_pairs={{0,1},{1,0},{2,3},{3,2},{4,5},{5,4},{6,7},{7,6},{8,9},{9,8},{10,11... | collective-permute-start | bytes 1671176 | tf_op jit(solution)/shard_map/ppermute | solution.py:33
  128.4 14.1 %collective-permute-start.32 = (bf16[128,1024]{1,0:T(8,128)(2,1)S(1)}, bf16[128,1024]{1,0:T(8,128)(2,1)S(1)}, u32[]{:S(2)}, u32[]{:S(2)}) collective-permute-start(bf16[128,1024]{1,0:T(8,128)(2,1)S(1)} %get-tuple-element.143), channel_id=1, source_target_pairs={{0,8},{8,0},{16,24},{24,16},{1,9},{9,1},{17,25},{25,17},{2,10},{10... | collective-permute-start | bytes 786440 | tf_op jit(solution)/shard_map/ppermute | solution.py:278
  130.0 13.4 %collective-permute-start.33 = (bf16[128,1024]{1,0:T(8,128)(2,1)S(1)}, bf16[128,1024]{1,0:T(8,128)(2,1)S(1)}, u32[]{:S(2)}, u32[]{:S(2)}) collective-permute-start(bf16[128,1024]{1,0:T(8,128)(2,1)S(1)} %get-tuple-element.145), channel_id=1, source_target_pairs={{0,16},{8,24},{16,0},{24,8},{1,17},{9,25},{17,1},{25,9},{2,18},{10... | collective-permute-start | bytes 786440 | tf_op jit(solution)/shard_map/ppermute | solution.py:278
  130.5 12.0 %collective-permute-start.34 = (bf16[128,1024]{1,0:T(8,128)(2,1)S(1)}, bf16[128,1024]{1,0:T(8,128)(2,1)S(1)}, u32[]{:S(2)}, u32[]{:S(2)}) collective-permute-start(bf16[128,1024]{1,0:T(8,128)(2,1)S(1)} %get-tuple-element.147), channel_id=1, source_target_pairs={{0,24},{8,16},{16,8},{24,0},{1,25},{9,17},{17,9},{25,1},{2,26},{10... | collective-permute-start | bytes 786440 | tf_op jit(solution)/shard_map/ppermute | solution.py:278
  144.5 14.0 %collective-permute-start.36 = (bf16[256,512]{1,0:T(8,128)(2,1)S(1)}, bf16[256,512]{1,0:T(8,128)(2,1)S(1)}, u32[]{:S(2)}, u32[]{:S(2)}) collective-permute-start(bf16[256,512]{1,0:T(8,128)(2,1)S(1)} %get-tuple-element.154), channel_id=1, source_target_pairs={{0,1},{1,0},{2,3},{3,2},{4,5},{5,4},{6,7},{7,6},{8,9},{9,8},{10,11... | collective-permute-start | bytes 786440 | tf_op jit(solution)/shard_map/ppermute | solution.py:33
  145.5 36.4 %collective-permute-start.37 = (bf16[272,1024]{1,0:T(8,128)(2,1)}, bf16[272,1024]{1,0:T(8,128)(2,1)}, u32[]{:S(2)}, u32[]{:S(2)}) collective-permute-start(bf16[272,1024]{1,0:T(8,128)(2,1)} %add_convert_fusion.1), channel_id=1, source_target_pairs={{0,2},{1,3},{2,0},{3,1},{4,6},{5,7},{6,4},{7,5},{8,10},{9,11},{10,... | collective-permute-start | bytes 1671176 | tf_op jit(solution)/shard_map/ppermute | solution.py:33
  150.3 17.8 %collective-permute-start.38 = (bf16[128,1024]{1,0:T(8,128)(2,1)S(1)}, bf16[128,1024]{1,0:T(8,128)(2,1)S(1)}, u32[]{:S(2)}, u32[]{:S(2)}) collective-permute-start(bf16[128,1024]{1,0:T(8,128)(2,1)S(1)} %get-tuple-element.156), channel_id=1, source_target_pairs={{0,8},{8,0},{16,24},{24,16},{1,9},{9,1},{17,25},{25,17},{2,10},{10... | collective-permute-start | bytes 786440 | tf_op jit(solution)/shard_map/ppermute | solution.py:278
  151.2 17.0 %collective-permute-start.39 = (bf16[128,1024]{1,0:T(8,128)(2,1)S(1)}, bf16[128,1024]{1,0:T(8,128)(2,1)S(1)}, u32[]{:S(2)}, u32[]{:S(2)}) collective-permute-start(bf16[128,1024]{1,0:T(8,128)(2,1)S(1)} %get-tuple-element.157), channel_id=1, source_target_pairs={{0,16},{8,24},{16,0},{24,8},{1,17},{9,25},{17,1},{25,9},{2,18},{10... | collective-permute-start | bytes 786440 | tf_op jit(solution)/shard_map/ppermute | solution.py:278
  152.1 15.9 %collective-permute-start.40 = (bf16[128,1024]{1,0:T(8,128)(2,1)S(1)}, bf16[128,1024]{1,0:T(8,128)(2,1)S(1)}, u32[]{:S(2)}, u32[]{:S(2)}) collective-permute-start(bf16[128,1024]{1,0:T(8,128)(2,1)S(1)} %get-tuple-element.158), channel_id=1, source_target_pairs={{0,24},{8,16},{16,8},{24,0},{1,25},{9,17},{17,9},{25,1},{2,26},{10... | collective-permute-start | bytes 786440 | tf_op jit(solution)/shard_map/ppermute | solution.py:278
  158.5 12.2 %collective-permute-start.42 = (bf16[256,512]{1,0:T(8,128)(2,1)}, bf16[256,512]{1,0:T(8,128)(2,1)}, u32[]{:S(2)}, u32[]{:S(2)}) collective-permute-start(bf16[256,512]{1,0:T(8,128)(2,1)} %get-tuple-element.169), channel_id=1, source_target_pairs={{0,1},{1,0},{2,3},{3,2},{4,5},{5,4},{6,7},{7,6},{8,9},{9,8},{10,11... | collective-permute-start | bytes 786440 | tf_op jit(solution)/shard_map/ppermute | solution.py:33
  168.0 21.9 %collective-permute-start.44 = (bf16[256,512]{1,0:T(8,128)(2,1)}, bf16[256,512]{1,0:T(8,128)(2,1)}, u32[]{:S(2)}, u32[]{:S(2)}) collective-permute-start(bf16[256,512]{1,0:T(8,128)(2,1)} %add_convert_fusion.5), channel_id=1, source_target_pairs={{0,2},{1,3},{2,0},{3,1},{4,6},{5,7},{6,4},{7,5},{8,10},{9,11},{10,... | collective-permute-start | bytes 786440 | tf_op jit(solution)/shard_map/ppermute | solution.py:33
  168.7 26.4 %collective-permute-start.41 = (bf16[256,1024]{1,0:T(8,128)(2,1)S(1)}, bf16[256,1024]{1,0:T(8,128)(2,1)S(1)}, u32[]{:S(2)}, u32[]{:S(2)}) collective-permute-start(bf16[256,1024]{1,0:T(8,128)(2,1)S(1)} %get-tuple-element.168), channel_id=1, source_target_pairs={{0,1},{1,0},{2,3},{3,2},{4,5},{5,4},{6,7},{7,6},{8,9},{9,8},{10,11... | collective-permute-start | bytes 1572872 | tf_op jit(solution)/shard_map/ppermute | solution.py:33
  171.8 23.4 %collective-permute-start.43 = (bf16[256,512]{1,0:T(8,128)(2,1)S(1)}, bf16[256,512]{1,0:T(8,128)(2,1)S(1)}, u32[]{:S(2)}, u32[]{:S(2)}) collective-permute-start(bf16[256,512]{1,0:T(8,128)(2,1)S(1)} %add_convert_fusion.4), channel_id=1, source_target_pairs={{0,2},{1,3},{2,0},{3,1},{4,6},{5,7},{6,4},{7,5},{8,10},{9,11},{10,... | collective-permute-start | bytes 786440 | tf_op jit(solution)/shard_map/ppermute | solution.py:33
  183.1 6.1 %collective-permute-start.45 = (f32[2,256]{1,0:T(2,128)S(1)}, f32[2,256]{1,0:T(2,128)S(1)}, u32[]{:S(2)}, u32[]{:S(2)}) collective-permute-start(f32[2,256]{1,0:T(2,128)S(1)} %add.61), channel_id=1, source_target_pairs={{0,4},{4,0},{1,5},{5,1},{2,6},{6,2},{3,7},{7,3},{8,12},{12,8},{9,1... | collective-permute-start | bytes 6152 | tf_op jit(solution)/shard_map/ppermute | solution.py:308
  (29 other events, 202.1 us)
